TPU v7x, 256 devices: a whole 4x4x8 slice. The times are simulated.
256 devices in a mesh: dp: 32 (over x_lo, z, core), seq: 8 (over x_hi, y).
Axes of the slice: x: 4 (x_hi: 2, x_lo: 2; x = x_hi * 2 + x_lo), y: 4, z: 8, core: 2. Of those that a mesh axis runs over, the one named last changes fastest.
Arguments:
- queries: bfloat16 [32, 1024, 1024], P('dp', 'seq'), may hold values from -6 to 6
- keys: bfloat16 [32, 1024, 1024], P('dp', 'seq'), may hold values from -6 to 6
- values: bfloat16 [32, 1024, 1024], P('dp', 'seq'), may hold values from -6 to 6
- stream: bfloat16 [32, 1024, 1024], P('dp', 'seq'), may hold values from -6 to 6
- cotangent: bfloat16 [32, 1024, 1024], P('dp', 'seq'), may hold values from -6 to 6
- attn_out: bfloat16 [1024, 1024], replicated, may hold values from -0.1875 to 0.1875
- point_in: bfloat16 [1024, 2048], replicated, may hold values from -0.1875 to 0.1875
- kernel: bfloat16 [31, 1024], replicated, may hold values from -1 to 1
- point_out: bfloat16 [1024, 1024], replicated, may hold values from -0.1875 to 0.1875
- norm_gain: float32 [1024], replicated, may hold values from 0.1 to 1.9
- conv_gain: float32 [1024], replicated, may hold values from 0.1 to 1.9
- segments: int32 [32, 1024], replicated, may hold values from 0 to 511, as said below
- plan: int32 [32], replicated, may hold values from 0 to 31, as said below
Outputs:
- query_grad: bfloat16 [32, 1024, 1024], P('dp', 'seq')
- key_grad: bfloat16 [32, 1024, 1024], P('dp', 'seq')
- value_grad: bfloat16 [32, 1024, 1024], P('dp', 'seq')
- stream_grad: bfloat16 [32, 1024, 1024], P('dp', 'seq')
- kernel_grad: float32 [31, 1024], replicated
- proj_grads: float32 [1024, 2048], P(('dp', 'seq'))
Inputs may be any that keep to these rules, and one draw needn't show every extreme that they name: `segments`: along each pack the numbers never fall and change only at even frames; one number marks one utterance. `plan`: A permutation of 0 to 31.
All inputs are finite; a program needn't handle non-finite values.
Results may differ from a plain program's by a relative error of at most 0.024.
Values may be sent and summed in bfloat16 or wider, within the bound.
No kernel may reach another device: no remote copies, remote signals or barrier semaphores. Data moves between devices by JAX's collectives and lax.ppermute only.
A program may use at most 128 MiB of HBM per device.

v0:
```python
import jax
import jax.numpy as jnp
from jax import lax
from jax.sharding import PartitionSpec as P

HEAD_DIM = 64


EPSILON = 1e-05
MASKED = -1e30


def in_one_piece(arrays, axis, split_dim, concat_dim, along):
    ends, at = ([], 0)
    for a in arrays[:-1]:
        at += a.shape[along]
        ends.append(at)
    both = jnp.concatenate(arrays, axis=along)
    return tuple(
        jnp.split(
            lax.all_to_all(both, axis, split_axis=split_dim, concat_axis=concat_dim, tiled=True),
            ends,
            axis=along,
        )
    )


def extended(cells, sides, width):
    for axis, dim in sides:
        count = lax.axis_size(axis)
        ends = count - 1
        head = lax.slice_in_dim(cells, 0, width, axis=dim)
        tail = lax.slice_in_dim(cells, cells.shape[dim] - width, cells.shape[dim], axis=dim)
        cells = jnp.concatenate(
            [
                lax.ppermute(tail, axis, [(i, (i + 1) % count) for i in range(ends)]),
                cells,
                lax.ppermute(head, axis, [((i + 1) % count, i) for i in range(ends)]),
            ],
            axis=dim,
        )
    return cells


def layer_norm(stream, gain):
    center = jnp.mean(stream, -1, keepdims=True)
    shifted = stream - center
    inverse = lax.rsqrt(jnp.mean(shifted * shifted, -1, keepdims=True) + EPSILON)
    normed = shifted * inverse
    return (normed * gain, normed, inverse)


def norm_backward(upstream, normed, inverse, gain):
    scaled = upstream * gain
    return inverse * (
        scaled
        - jnp.mean(scaled, -1, keepdims=True)
        - normed * jnp.mean(scaled * normed, -1, keepdims=True)
    )


def swish_slope(values):
    logistic = jax.nn.sigmoid(values)
    return logistic * (1.0 + values * (1.0 - logistic))


def tap_table(padded_ids, own_ids, taps):
    length = own_ids.shape[0]
    return (
        jnp.stack([padded_ids[tap : tap + length] for tap in range(taps)], 1) == own_ids[:, None]
    ).astype(jnp.float32)


def depthwise(padded, weights, table):
    length = table.shape[0]
    total = jnp.zeros((length, padded.shape[1]), jnp.float32)
    for tap in range(weights.shape[0]):
        total = (
            total
            + weights[tap].astype(jnp.float32)
            * padded[tap : tap + length].astype(jnp.float32)
            * table[:, tap : tap + 1]
        )
    return total


def tap_sums(upstream, padded, table):
    length = table.shape[0]
    return jnp.stack(
        [
            jnp.sum(
                upstream * padded[tap : tap + length].astype(jnp.float32) * table[:, tap : tap + 1],
                0,
            )
            for tap in range(table.shape[1])
        ]
    )


def times_transposed(left, right):
    return lax.dot_general(
        left, right, (((1,), (1,)), ((), ())), preferred_element_type=jnp.float32
    )


def transposed_times(left, right):
    return lax.dot_general(
        left, right, (((0,), (0,)), ((), ())), preferred_element_type=jnp.float32
    )


def split_heads(matrix):
    return matrix.reshape(matrix.shape[0], -1, HEAD_DIM).transpose(1, 0, 2)


def merge_heads(tensor):
    return tensor.transpose(1, 0, 2).reshape(tensor.shape[1], -1)


def tiling(length, heads):
    block_rows = min(length, 512)
    per_group = max(1, min(heads, 1024 // block_rows))
    return (block_rows, per_group)


def to_blocks(tensor, per_group, block_rows):
    heads, length, depth = tensor.shape
    groups, blocks = (heads // per_group, length // block_rows)
    return (
        tensor.reshape(groups, per_group, blocks, block_rows, depth)
        .transpose(0, 2, 1, 3, 4)
        .reshape(groups * blocks, per_group, block_rows, depth)
    )


def from_blocks(tensor, groups):
    total, per_group, block_rows, depth = tensor.shape
    blocks = total // groups
    return (
        tensor.reshape(groups, blocks, per_group, block_rows, depth)
        .transpose(0, 2, 1, 3, 4)
        .reshape(groups * per_group, blocks * block_rows, depth)
    )


def masked_scores(query_block, key_group, query_ids, key_ids):
    scores = jnp.einsum(
        "hqe,hke->hqk", query_block, key_group, preferred_element_type=jnp.float32
    ) * HEAD_DIM ** (-0.5)
    return jnp.where((query_ids[:, None] == key_ids[None, :])[None], scores, MASKED)


def attend(queries, keys, values, query_ids, key_ids):
    query_heads = split_heads(queries)
    heads, length = (query_heads.shape[0], query_heads.shape[1])
    block_rows, per_group = tiling(length, heads)
    groups, blocks = (heads // per_group, length // block_rows)
    query_blocks = to_blocks(query_heads, per_group, block_rows)
    key_groups = split_heads(keys).reshape(groups, per_group, keys.shape[0], HEAD_DIM)
    value_groups = split_heads(values).reshape(groups, per_group, values.shape[0], HEAD_DIM)
    id_blocks = query_ids.reshape(blocks, block_rows)

    def one_block(position):
        which = position // blocks
        scores = masked_scores(
            query_blocks[position], key_groups[which], id_blocks[position % blocks], key_ids
        )
        highest = jnp.max(scores, -1, keepdims=True)
        log_total = highest + jnp.log(jnp.sum(jnp.exp(scores - highest), -1, keepdims=True))
        weights = jnp.exp(scores - log_total)
        mixed = jnp.einsum(
            "hqk,hke->hqe",
            weights.astype(jnp.bfloat16),
            value_groups[which],
            preferred_element_type=jnp.float32,
        )
        return (mixed.astype(jnp.bfloat16), weights, log_total)

    mixed, weights, log_total = lax.map(one_block, jnp.arange(groups * blocks))
    return (
        merge_heads(from_blocks(mixed, groups)),
        weights,
        from_blocks(log_total, groups)[:, :, 0].T,
    )


def attend_backward(queries, upstream, keys, values, weights):
    query_heads = split_heads(queries)
    heads, length = (query_heads.shape[0], query_heads.shape[1])
    block_rows, per_group = tiling(length, heads)
    groups, blocks = (heads // per_group, length // block_rows)
    query_blocks = to_blocks(query_heads, per_group, block_rows)
    grad_blocks = to_blocks(split_heads(upstream), per_group, block_rows)
    key_count = keys.shape[0]
    key_groups = split_heads(keys).reshape(groups, per_group, key_count, HEAD_DIM)
    value_groups = split_heads(values).reshape(groups, per_group, key_count, HEAD_DIM)
    scale = HEAD_DIM ** (-0.5)

    def one_block(totals, position):
        which = position // blocks
        weight_block = weights[position]
        slope = jnp.einsum(
            "hqe,hke->hqk",
            grad_blocks[position],
            value_groups[which],
            preferred_element_type=jnp.float32,
        )
        delta = jnp.sum(weight_block * slope, -1, keepdims=True)
        score_grad = (weight_block * (slope - delta)).astype(jnp.bfloat16)
        query_part = (
            jnp.einsum(
                "hqk,hke->hqe", score_grad, key_groups[which], preferred_element_type=jnp.float32
            )
            * scale
        ).astype(jnp.bfloat16)
        key_add = (
            jnp.einsum(
                "hqk,hqe->hke",
                score_grad,
                query_blocks[position],
                preferred_element_type=jnp.float32,
            )
            * scale
        )
        value_add = jnp.einsum(
            "hqk,hqe->hke",
            weight_block.astype(jnp.bfloat16),
            grad_blocks[position],
            preferred_element_type=jnp.float32,
        )
        totals = (totals[0].at[which].add(key_add), totals[1].at[which].add(value_add))
        return (totals, (query_part, delta))

    start_totals = ()
    empty = jnp.zeros((groups, per_group, key_count, HEAD_DIM), jnp.float32)
    start_totals = (empty, empty)
    totals, outputs = lax.scan(one_block, start_totals, jnp.arange(groups * blocks))
    query_grad = merge_heads(from_blocks(outputs[0], groups))
    delta = from_blocks(outputs[1], groups)[:, :, 0].T
    key_grad = merge_heads(totals[0].reshape(heads, key_count, HEAD_DIM)).astype(jnp.bfloat16)
    value_grad = merge_heads(totals[1].reshape(heads, key_count, HEAD_DIM)).astype(jnp.bfloat16)
    return (query_grad, delta, key_grad, value_grad)


def per_device(
    queries,
    keys,
    values,
    stream,
    cotangent,
    attn_out,
    point_in,
    kernel,
    point_out,
    norm_gain,
    conv_gain,
    segments,
    plan,
):
    frames, width = (queries.shape[1], queries.shape[2])
    seq_place = lax.axis_index("seq")
    spread = in_one_piece((queries[0], keys[0], values[0], stream[0], cotangent[0]), "dp", 0, 0, 1)

    def reorder(matrix):
        return jnp.take(matrix.reshape(plan.shape[0], -1, width), plan, axis=0).reshape(
            frames, width
        )

    arranged = [reorder(matrix) for matrix in spread]
    query_rows, key_rows, value_rows, stream_rows, grad_rows = in_one_piece(
        (arranged[0], arranged[1], arranged[2], arranged[3], arranged[4]), "dp", 0, 0, 1
    )
    source = plan[lax.axis_index("dp")]
    pack_ids = lax.dynamic_index_in_dim(segments, source, 0, keepdims=False)
    own_ids = lax.dynamic_slice_in_dim(pack_ids, seq_place * frames, frames)
    query_heads, key_heads, value_heads = (
        lax.all_to_all(query_rows, "seq", split_axis=1, concat_axis=0, tiled=True),
        lax.all_to_all(key_rows, "seq", split_axis=1, concat_axis=0, tiled=True),
        lax.all_to_all(value_rows, "seq", split_axis=1, concat_axis=0, tiled=True),
    )
    mixed_heads, weights, log_totals = attend(
        query_heads, key_heads, value_heads, pack_ids, pack_ids
    )
    mixed = lax.all_to_all(mixed_heads, "seq", split_axis=0, concat_axis=1, tiled=True)
    hidden = stream_rows.astype(jnp.float32) + jnp.dot(
        mixed, attn_out, preferred_element_type=jnp.float32
    )
    normed_in, hat_in, inv_in = layer_norm(hidden, norm_gain)
    both = jnp.dot(normed_in.astype(jnp.bfloat16), point_in, preferred_element_type=jnp.float32)
    linear = both[:, :width]
    logistic = jax.nn.sigmoid(both[:, width:])
    conv_in = (linear * logistic).astype(jnp.bfloat16)
    taps = kernel.shape[0]
    reach = taps // 2
    padded = extended(conv_in, (("seq", 0),), reach)
    padded_ids = lax.dynamic_slice_in_dim(
        jnp.pad(pack_ids, reach, constant_values=-1), seq_place * frames, frames + 2 * reach
    )
    table = tap_table(padded_ids, own_ids, taps)
    conv_out = depthwise(padded, kernel, table)
    normed_out, hat_out, inv_out = layer_norm(conv_out, conv_gain)
    activated = (normed_out * jax.nn.sigmoid(normed_out)).astype(jnp.bfloat16)
    act_grad = times_transposed(grad_rows, point_out)
    conv_grad = norm_backward(act_grad * swish_slope(normed_out), hat_out, inv_out, conv_gain)
    grad_padded = extended(conv_grad.astype(jnp.bfloat16), (("seq", 0),), reach).astype(
        conv_grad.dtype
    )
    kernel_grad = lax.psum(tap_sums(conv_grad, padded, table), ("dp", "seq"))
    in_grad = depthwise(grad_padded, kernel[::-1], table)
    both_grad = jnp.concatenate(
        [in_grad * logistic, in_grad * linear * logistic * (1.0 - logistic)], 1
    ).astype(jnp.bfloat16)
    back_in = times_transposed(both_grad, point_in)
    stream_out = (
        grad_rows.astype(jnp.float32) + norm_backward(back_in, hat_in, inv_in, norm_gain)
    ).astype(jnp.bfloat16)
    mixed_grad = times_transposed(stream_out, attn_out).astype(jnp.bfloat16)
    proj_grads = lax.psum_scatter(
        jnp.concatenate(
            [transposed_times(mixed, stream_out), transposed_times(activated, grad_rows)], 1
        ),
        ("dp", "seq"),
        scatter_dimension=0,
        tiled=True,
    )
    grad_heads = lax.all_to_all(mixed_grad, "seq", split_axis=1, concat_axis=0, tiled=True)
    query_part, unused_delta, key_part, value_part = attend_backward(
        query_heads, grad_heads, key_heads, value_heads, weights
    )
    query_grad, key_grad, value_grad = (
        lax.all_to_all(query_part, "seq", split_axis=0, concat_axis=1, tiled=True),
        lax.all_to_all(key_part, "seq", split_axis=0, concat_axis=1, tiled=True),
        lax.all_to_all(value_part, "seq", split_axis=0, concat_axis=1, tiled=True),
    )
    return (
        query_grad[None],
        key_grad[None],
        value_grad[None],
        stream_out[None],
        kernel_grad,
        proj_grads,
    )


def solution(mesh):
    placed = (
        P("dp", "seq", None),
        P("dp", "seq", None),
        P("dp", "seq", None),
        P("dp", "seq", None),
        P("dp", "seq", None),
        P(),
        P(),
        P(),
        P(),
        P(),
        P(),
        P(),
        P(),
    )
    return jax.shard_map(
        per_device,
        mesh=mesh,
        in_specs=placed,
        out_specs=(
            P("dp", "seq", None),
            P("dp", "seq", None),
            P("dp", "seq", None),
            P("dp", "seq", None),
            P(),
            P(("dp", "seq"), None),
        ),
        check_vma=False,
    )
```

profile of v0, /device:TPU:24, one launch (start us, length us, event | category | flops | bytes accessed | tf_op | source)
XLA Modules:
  0.0 553.0 jit_solution(6512067993345745831)
XLA Ops:
  16.8 9.8 %all-to-all-start = ((bf16[32,4,5120]{2,1,0:T(4,128)(2,1)}), bf16[32,4,5120]{2,1,0:T(4,128)(2,1)S(1)}, u32[]{:S(2)}, u32[]{:S(2)}) async-start(bf16[32,4,5120]{2,1,0:T(4,128)(2,1)} %constant_dynamic-update-slice_fusion), calls=%async_computation | async-start | bytes 2621440 | tf_op jit(solution)/shard_map/all_to_all | solution.py:21
  26.6 33.6 %all-to-all-done = bf16[32,4,5120]{2,1,0:T(4,128)(2,1)S(1)} async-done(((bf16[32,4,5120]{2,1,0:T(4,128)(2,1)}), bf16[32,4,5120]{2,1,0:T(4,128)(2,1)S(1)}, u32[]{:S(2)}, u32[]{:S(2)}) %all-to-all-start) | async-done | bytes 1310752 | tf_op jit(solution)/shard_map/all_to_all | solution.py:21
  80.0 4.7 all-to-all-start.1
  89.1 29.1 %all-to-all-done.1 = bf16[32,4,5120]{2,1,0:T(4,128)(2,1)} async-done(((bf16[32,4,5120]{2,1,0:T(4,128)(2,1)}), bf16[32,4,5120]{2,1,0:T(4,128)(2,1)}, u32[]{:S(2)}, u32[]{:S(2)}) %all-to-all-start.1) | async-done | bytes 1310752 | tf_op jit(solution)/shard_map/all_to_all | solution.py:21
  123.5 6.9 %all-to-all-start.2 = ((bf16[128,8,128]{0,2,1:T(8,128)(2,1)}), bf16[128,8,128]{0,2,1:T(8,128)(2,1)}, u32[]{:S(2)}, u32[]{:S(2)}) async-start(bf16[128,8,128]{0,2,1:T(8,128)(2,1)} %bitcast.424), calls=%async_computation.2 | async-start | bytes 524288 | tf_op jit(solution)/shard_map/all_to_all | solution.py:277
  132.8 4.0 all-to-all-done.2
  136.7 6.3 %all-to-all-start.3 = ((bf16[128,8,128]{2,0,1:T(8,128)(2,1)}), bf16[128,8,128]{2,0,1:T(8,128)(2,1)}, u32[]{:S(2)}, u32[]{:S(2)}) async-start(bf16[128,8,128]{2,0,1:T(8,128)(2,1)} %bitcast.421), calls=%async_computation.3 | async-start | bytes 524288 | tf_op jit(solution)/shard_map/all_to_all | solution.py:278
  149.5 6.9 %all-to-all-start.4 = ((bf16[128,8,128]{2,0,1:T(8,128)(2,1)}), bf16[128,8,128]{2,0,1:T(8,128)(2,1)}, u32[]{:S(2)}, u32[]{:S(2)}) async-start(bf16[128,8,128]{2,0,1:T(8,128)(2,1)} %bitcast.423), calls=%async_computation.4 | async-start | bytes 524288 | tf_op jit(solution)/shard_map/all_to_all | solution.py:279
  167.9 26.2 %while.33 = (s32[]{:T(128)}, bf16[2,2,512,64]{2,3,1,0:T(8,128)(2,1)S(1)}, f32[2,2,512,1024]{3,2,1,0:T(8,128)}, s32[2]{0:T(128)S(1)}, s32[2,512]{1,0:T(2,128)S(1)...) while((s32[]{:T(128)}, ...), condition=%wide.region_3.5_spmd, body=%wide.region_0.4_spmd.sunk | while | flops 283704320 | bytes 83143056 | solution.py:179
  177.8 3.2 copy-done.2
  195.3 7.2 %all-to-all-start.5 = ((bf16[8,128,128]{1,2,0:T(8,128)(2,1)}), bf16[8,128,128]{1,2,0:T(8,128)(2,1)S(1)}, u32[]{:S(2)}, u32[]{:S(2)}) async-start(bf16[8,128,128]{1,2,0:T(8,128)(2,1)} %copy.79), calls=%async_computation.5 | async-start | bytes 524288 | tf_op jit(solution)/shard_map/all_to_all | solution.py:284
  203.9 5.0 all-to-all-done.5
  217.0 7.1 %collective-permute-start = (bf16[15,1024]{1,0:T(8,128)(2,1)S(1)}, bf16[15,1024]{1,0:T(8,128)(2,1)S(1)}, u32[]{:S(2)}, u32[]{:S(2)}) collective-permute-start(bf16[15,1024]{1,0:T(8,128)(2,1)S(1)} %get-tuple-element.515), channel_id=1, source_target_pairs={{0,1},{1,2},{2,3},{3,4},{4,5},{5,6},{6,7},{8,9},{9,10},{10,11},{11... | collective-permute-start | bytes 92168 | tf_op jit(solution)/shard_map/ppermute | solution.py:36
  229.2 3.8 fusion.237
  238.4 8.1 %collective-permute-start.2 = (bf16[15,1024]{1,0:T(8,128)(2,1)S(1)}, bf16[15,1024]{1,0:T(8,128)(2,1)S(1)}, u32[]{:S(2)}, u32[]{:S(2)}) collective-permute-start(bf16[15,1024]{1,0:T(8,128)(2,1)S(1)} %get-tuple-element.513), channel_id=1, source_target_pairs={{0,1},{1,2},{2,3},{3,4},{4,5},{5,6},{6,7},{8,9},{9,10},{10,11},{11... | collective-permute-start | bytes 92168 | tf_op jit(solution)/shard_map/ppermute | solution.py:36
  249.9 4.1 stack.255
  254.2 4.1 multiply_convert_fusion.2
  262.5 4.1 pad_maximum_fusion
  268.3 4.8 all-to-all-start.6
  273.1 6.3 %all-to-all-done.6 = bf16[128,8,128]{0,2,1:T(8,128)(2,1)S(1)} async-done(((bf16[128,8,128]{0,2,1:T(8,128)(2,1)}), bf16[128,8,128]{0,2,1:T(8,128)(2,1)S(1)}, u32[]{:S(2)}, u32[]{:S(2)}) %all-to-all-start.6) | async-done | bytes 262176 | tf_op jit(solution)/shard_map/all_to_all | solution.py:326
  283.9 39.4 %while.34 = (s32[]{:T(128)}, f32[1,2,1024,64]{2,3,1,0:T(8,128)S(1)}, f32[1,2,1024,64]{2,3,1,0:T(8,128)S(1)}, bf16[2,2,512,64]{2,3,1,0:T(8,128)(2,1)}, s32[2]{0:T...) while((s32[]{:T(128)}, ...), condition=%wide.region_15.17_spmd.clone, body=%wide.region_12.16_spmd.clone.sunk | while | flops 543161344 | bytes 73412632 | solution.py:237
  286.4 3.4 fusion.323
  298.7 3.3 fusion.326
  306.1 3.3 fusion.323
  318.5 3.3 fusion.326
  327.2 5.8 %all-to-all-start.7 = ((bf16[8,128,128]{1,2,0:T(8,128)(2,1)}), bf16[8,128,128]{1,2,0:T(8,128)(2,1)S(1)}, u32[]{:S(2)}, u32[]{:S(2)}) async-start(bf16[8,128,128]{1,2,0:T(8,128)(2,1)} %copy.85), calls=%async_computation.7 | async-start | bytes 524288 | tf_op jit(solution)/shard_map/all_to_all | solution.py:331
  334.0 5.4 all-to-all-done.7
  339.4 5.7 %all-to-all-start.8 = ((bf16[8,128,128]{2,1,0:T(8,128)(2,1)}), bf16[8,128,128]{2,1,0:T(8,128)(2,1)S(1)}, u32[]{:S(2)}, u32[]{:S(2)}) async-start(bf16[8,128,128]{2,1,0:T(8,128)(2,1)} %copy.86), calls=%async_computation.8 | async-start | bytes 524288 | tf_op jit(solution)/shard_map/all_to_all | solution.py:332
  346.0 6.7 %all-to-all-done.8 = bf16[8,128,128]{2,1,0:T(8,128)(2,1)S(1)} async-done(((bf16[8,128,128]{2,1,0:T(8,128)(2,1)}), bf16[8,128,128]{2,1,0:T(8,128)(2,1)S(1)}, u32[]{:S(2)}, u32[]{:S(2)}) %all-to-all-start.8) | async-done | bytes 262176 | tf_op jit(solution)/shard_map/all_to_all | solution.py:332
  352.7 5.8 %all-to-all-start.9 = ((bf16[8,128,128]{2,1,0:T(8,128)(2,1)}), bf16[8,128,128]{2,1,0:T(8,128)(2,1)S(1)}, u32[]{:S(2)}, u32[]{:S(2)}) async-start(bf16[8,128,128]{2,1,0:T(8,128)(2,1)} %copy.88), calls=%async_computation.9 | async-start | bytes 524288 | tf_op jit(solution)/shard_map/all_to_all | solution.py:333
  360.4 4.4 all-to-all-done.9
  365.9 175.9 %all-reduce.5.cloned.1.call-done = (f32[31,1024]{1,0:T(8,128)}, f32[1024,2048]{0,1:T(8,128)}) async-done(((f32[31,1024]{1,0:T(8,128)}, f32[1024,2048]{0,1:T(8,128)}), (f32[31,1024]{1,0:T(8,128)}, f32[1024,2048]{0,1:T(8,128)})) %all-reduce.5.cloned.1.call-update) | async-done | bytes 8515600 | tf_op jit(solution)/shard_map/psum | solution.py:308
  (316 shorter events, 138.8 us)
Async XLA Ops:
  7.2 201.7 %copy-start = (bf16[1024,1024]{1,0:T(8,128)(2,1)S(1)}, bf16[1024,1024]{1,0:T(8,128)(2,1)}, u32[]{:S(2)}) copy-start(bf16[1024,1024]{1,0:T(8,128)(2,1)} %param.28) | copy-start | bytes 6291460
  16.8 43.4 %all-to-all-start = ((bf16[32,4,5120]{2,1,0:T(4,128)(2,1)}), bf16[32,4,5120]{2,1,0:T(4,128)(2,1)S(1)}, u32[]{:S(2)}, u32[]{:S(2)}) async-start(bf16[32,4,5120]{2,1,0:T(4,128)(2,1)} %constant_dynamic-update-slice_fusion), calls=%async_computation | async-start | bytes 2621440 | tf_op jit(solution)/shard_map/all_to_all | solution.py:21
  80.0 38.3 %all-to-all-start.1 = ((bf16[32,4,5120]{2,1,0:T(4,128)(2,1)}), bf16[32,4,5120]{2,1,0:T(4,128)(2,1)}, u32[]{:S(2)}, u32[]{:S(2)}) async-start(bf16[32,4,5120]{2,1,0:T(4,128)(2,1)} %select_dynamic-update-slice_fusion), calls=%async_computation.1 | async-start | bytes 2621440 | tf_op jit(solution)/shard_map/all_to_all | solution.py:21
  84.7 71.9 %copy-start.15 = (bf16[31,1024]{1,0:T(8,128)(2,1)S(1)}, bf16[31,1024]{1,0:T(8,128)(2,1)}, u32[]{:S(2)}) copy-start(bf16[31,1024]{1,0:T(8,128)(2,1)} %param.30) | copy-start | bytes 190468
  120.7 42.9 %copy-start.11 = (bf16[128,5120]{1,0:T(8,128)(2,1)}, bf16[128,5120]{1,0:T(8,128)(2,1)S(1)}, u32[]{:S(2)}) copy-start(bf16[128,5120]{1,0:T(8,128)(2,1)S(1)} %all_to_all.109) | copy-start | bytes 3932164
  123.5 13.3 %all-to-all-start.2 = ((bf16[128,8,128]{0,2,1:T(8,128)(2,1)}), bf16[128,8,128]{0,2,1:T(8,128)(2,1)}, u32[]{:S(2)}, u32[]{:S(2)}) async-start(bf16[128,8,128]{0,2,1:T(8,128)(2,1)} %bitcast.424), calls=%async_computation.2 | async-start | bytes 524288 | tf_op jit(solution)/shard_map/all_to_all | solution.py:277
  136.7 12.8 %all-to-all-start.3 = ((bf16[128,8,128]{2,0,1:T(8,128)(2,1)}), bf16[128,8,128]{2,0,1:T(8,128)(2,1)}, u32[]{:S(2)}, u32[]{:S(2)}) async-start(bf16[128,8,128]{2,0,1:T(8,128)(2,1)} %bitcast.421), calls=%async_computation.3 | async-start | bytes 524288 | tf_op jit(solution)/shard_map/all_to_all | solution.py:278
  149.5 17.1 %all-to-all-start.4 = ((bf16[128,8,128]{2,0,1:T(8,128)(2,1)}), bf16[128,8,128]{2,0,1:T(8,128)(2,1)}, u32[]{:S(2)}, u32[]{:S(2)}) async-start(bf16[128,8,128]{2,0,1:T(8,128)(2,1)} %bitcast.423), calls=%async_computation.4 | async-start | bytes 524288 | tf_op jit(solution)/shard_map/all_to_all | solution.py:279
  194.1 19.9 %copy-start.9 = (bf16[1,2,1024,64]{2,3,1,0:T(8,128)(2,1)}, bf16[1,2,1024,64]{2,3,1,0:T(8,128)(2,1)S(1)}, u32[]{:S(2)}) copy-start(bf16[1,2,1024,64]{2,3,1,0:T(8,128)(2,1)S(1)} %get-tuple-element.834) | copy-start | bytes 786436
  195.3 13.5 %all-to-all-start.5 = ((bf16[8,128,128]{1,2,0:T(8,128)(2,1)}), bf16[8,128,128]{1,2,0:T(8,128)(2,1)S(1)}, u32[]{:S(2)}, u32[]{:S(2)}) async-start(bf16[8,128,128]{1,2,0:T(8,128)(2,1)} %copy.79), calls=%async_computation.5 | async-start | bytes 524288 | tf_op jit(solution)/shard_map/all_to_all | solution.py:284
  202.6 339.2 %all-reduce.5.cloned.1.call-start = ((), (), s32[]{:S(2)}) async-start(), calls=%async_computation.10 | async-start | bytes 17039360 | tf_op jit(solution)/shard_map/psum | solution.py:308
  214.0 21.0 %copy-start.6 = (f32[128,2048]{1,0:T(8,128)}, f32[128,2048]{1,0:T(8,128)S(1)}, u32[]{:S(2)}) copy-start(f32[128,2048]{1,0:T(8,128)S(1)} %fusion.238) | copy-start | bytes 3145732
  214.2 10.1 %collective-permute-start.1 = (bf16[15,1024]{1,0:T(8,128)(2,1)S(1)}, bf16[15,1024]{1,0:T(8,128)(2,1)S(1)}, u32[]{:S(2)}, u32[]{:S(2)}) collective-permute-start(bf16[15,1024]{1,0:T(8,128)(2,1)S(1)} %get-tuple-element.516), channel_id=1, source_target_pairs={{1,0},{2,1},{3,2},{4,3},{5,4},{6,5},{7,6},{9,8},{10,9},{11,10},{12... | collective-permute-start | bytes 92168 | tf_op jit(solution)/shard_map/ppermute | solution.py:38
  217.0 8.5 %collective-permute-start = (bf16[15,1024]{1,0:T(8,128)(2,1)S(1)}, bf16[15,1024]{1,0:T(8,128)(2,1)S(1)}, u32[]{:S(2)}, u32[]{:S(2)}) collective-permute-start(bf16[15,1024]{1,0:T(8,128)(2,1)S(1)} %get-tuple-element.515), channel_id=1, source_target_pairs={{0,1},{1,2},{2,3},{3,4},{4,5},{5,6},{6,7},{8,9},{9,10},{10,11},{11... | collective-permute-start | bytes 92168 | tf_op jit(solution)/shard_map/ppermute | solution.py:36
  224.1 22.4 %copy-start.54 = (f32[128]{0:T(128)}, f32[128]{0:T(128)S(1)}, u32[]{:S(2)}) copy-start(f32[128]{0:T(128)S(1)} %get-tuple-element.572) | copy-start | bytes 1540
  224.1 22.4 %copy-start.55 = (f32[128]{0:T(128)}, f32[128]{0:T(128)S(1)}, u32[]{:S(2)}) copy-start(f32[128]{0:T(128)S(1)} %get-tuple-element.573) | copy-start | bytes 1540
  224.1 22.4 %copy-start.56 = (f32[128]{0:T(128)}, f32[128]{0:T(128)S(1)}, u32[]{:S(2)}) copy-start(f32[128]{0:T(128)S(1)} %get-tuple-element.574) | copy-start | bytes 1540
  224.1 22.4 %copy-start.57 = (f32[128]{0:T(128)}, f32[128]{0:T(128)S(1)}, u32[]{:S(2)}) copy-start(f32[128]{0:T(128)S(1)} %get-tuple-element.575) | copy-start | bytes 1540
  224.2 22.4 %copy-start.58 = (f32[128]{0:T(128)}, f32[128]{0:T(128)S(1)}, u32[]{:S(2)}) copy-start(f32[128]{0:T(128)S(1)} %get-tuple-element.576) | copy-start | bytes 1540
  224.2 22.4 %copy-start.59 = (f32[128]{0:T(128)}, f32[128]{0:T(128)S(1)}, u32[]{:S(2)}) copy-start(f32[128]{0:T(128)S(1)} %get-tuple-element.577) | copy-start | bytes 1540
  224.2 23.1 %copy-start.50 = (f32[128]{0:T(128)}, f32[128]{0:T(128)S(1)}, u32[]{:S(2)}) copy-start(f32[128]{0:T(128)S(1)} %get-tuple-element.568) | copy-start | bytes 1540
  224.2 23.1 %copy-start.51 = (f32[128]{0:T(128)}, f32[128]{0:T(128)S(1)}, u32[]{:S(2)}) copy-start(f32[128]{0:T(128)S(1)} %get-tuple-element.569) | copy-start | bytes 1540
  224.2 23.1 %copy-start.52 = (f32[128]{0:T(128)}, f32[128]{0:T(128)S(1)}, u32[]{:S(2)}) copy-start(f32[128]{0:T(128)S(1)} %get-tuple-element.570) | copy-start | bytes 1540
  224.2 23.1 %copy-start.53 = (f32[128]{0:T(128)}, f32[128]{0:T(128)S(1)}, u32[]{:S(2)}) copy-start(f32[128]{0:T(128)S(1)} %get-tuple-element.571) | copy-start | bytes 1540
  224.2 25.4 %copy-start.63 = (f32[128]{0:T(128)}, f32[128]{0:T(128)S(1)}, u32[]{:S(2)}) copy-start(f32[128]{0:T(128)S(1)} %get-tuple-element.567) | copy-start | bytes 1540
  224.2 25.4 %copy-start.64 = (f32[128]{0:T(128)}, f32[128]{0:T(128)S(1)}, u32[]{:S(2)}) copy-start(f32[128]{0:T(128)S(1)} %get-tuple-element.578) | copy-start | bytes 1540
  236.5 17.5 %collective-permute-start.3 = (bf16[15,1024]{1,0:T(8,128)(2,1)S(1)}, bf16[15,1024]{1,0:T(8,128)(2,1)S(1)}, u32[]{:S(2)}, u32[]{:S(2)}) collective-permute-start(bf16[15,1024]{1,0:T(8,128)(2,1)S(1)} %get-tuple-element.514), channel_id=1, source_target_pairs={{1,0},{2,1},{3,2},{4,3},{5,4},{6,5},{7,6},{9,8},{10,9},{11,10},{12... | collective-permute-start | bytes 92168 | tf_op jit(solution)/shard_map/ppermute | solution.py:38
  238.4 15.6 %collective-permute-start.2 = (bf16[15,1024]{1,0:T(8,128)(2,1)S(1)}, bf16[15,1024]{1,0:T(8,128)(2,1)S(1)}, u32[]{:S(2)}, u32[]{:S(2)}) collective-permute-start(bf16[15,1024]{1,0:T(8,128)(2,1)S(1)} %get-tuple-element.513), channel_id=1, source_target_pairs={{0,1},{1,2},{2,3},{3,4},{4,5},{5,6},{6,7},{8,9},{9,10},{10,11},{11... | collective-permute-start | bytes 92168 | tf_op jit(solution)/shard_map/ppermute | solution.py:36
  268.3 11.1 %all-to-all-start.6 = ((bf16[128,8,128]{0,2,1:T(8,128)(2,1)}), bf16[128,8,128]{0,2,1:T(8,128)(2,1)S(1)}, u32[]{:S(2)}, u32[]{:S(2)}) async-start(bf16[128,8,128]{0,2,1:T(8,128)(2,1)} %bitcast.119), calls=%async_computation.6 | async-start | bytes 524288 | tf_op jit(solution)/shard_map/all_to_all | solution.py:326
  327.2 12.2 %all-to-all-start.7 = ((bf16[8,128,128]{1,2,0:T(8,128)(2,1)}), bf16[8,128,128]{1,2,0:T(8,128)(2,1)S(1)}, u32[]{:S(2)}, u32[]{:S(2)}) async-start(bf16[8,128,128]{1,2,0:T(8,128)(2,1)} %copy.85), calls=%async_computation.7 | async-start | bytes 524288 | tf_op jit(solution)/shard_map/all_to_all | solution.py:331
  339.4 13.3 %all-to-all-start.8 = ((bf16[8,128,128]{2,1,0:T(8,128)(2,1)}), bf16[8,128,128]{2,1,0:T(8,128)(2,1)S(1)}, u32[]{:S(2)}, u32[]{:S(2)}) async-start(bf16[8,128,128]{2,1,0:T(8,128)(2,1)} %copy.86), calls=%async_computation.8 | async-start | bytes 524288 | tf_op jit(solution)/shard_map/all_to_all | solution.py:332
  352.7 12.2 %all-to-all-start.9 = ((bf16[8,128,128]{2,1,0:T(8,128)(2,1)}), bf16[8,128,128]{2,1,0:T(8,128)(2,1)S(1)}, u32[]{:S(2)}, u32[]{:S(2)}) async-start(bf16[8,128,128]{2,1,0:T(8,128)(2,1)} %copy.88), calls=%async_computation.9 | async-start | bytes 524288 | tf_op jit(solution)/shard_map/all_to_all | solution.py:333
  (63 other events, 717.8 us)
Sparse Core Ops, SparseCore 0:
  266.7 275.0 all-reduce.4
where the time goes:
time: 561 us; the launch traced here: 553 us
  waiting for transfers between devices  273 us (49%)
  local copies, waits for them, and re-layouts  89.5 us (16%)
  starting transfers between devices  83.8 us (15%)
  matrix products  41.1 us (7%)
  other arithmetic  33.7 us (6%)
  between operations  17.7 us (3%)
  loops' own time  14.5 us (3%)
    psum x1, waiting for transfers between devices, per_device(): kernel_grad = lax.psum(tap_sums(conv_grad, padded, table), ('dp', 'seq'))  176 us
    all_to_all x2, waiting for transfers between devices, in_one_piece(): lax.all_to_all(both, axis, split_axis=split_dim, concat_axis=concat_dim,...  62.7 us
    ppermute x2, starting transfers between devices, extended(): lax.ppermute(tail, axis, [(i, (i + 1) % count) for i in range(ends)])  15.1 us
    all_to_all x2, starting transfers between devices, in_one_piece(): lax.all_to_all(both, axis, split_axis=split_dim, concat_axis=concat_dim,...  14.5 us
    unnamed x144, local copies, waits for them, and re-layouts  13.4 us
  transfers between devices with their start and end apart: 15, of which 11 were waited for; matrix products, arithmetic and copies ran while one was open for 13% of the time, Pallas kernels for 0%

commit v1 on v0

v1 whole, which is shorter than its diff:
```python
import functools

import jax
import jax.numpy as jnp
from jax import lax
from jax.experimental import pallas as pl
from jax.experimental.pallas import tpu as pltpu
from jax.sharding import PartitionSpec as P

HEAD_DIM = 64
EPSILON = 1e-05
MASKED = -1e30
F32 = jnp.float32
BF16 = jnp.bfloat16
HALO = 32
ROWS = 128
WINDOW = ROWS + 2 * HALO
REACH = 15
TAPS = 31

ORDER = (0, 2, 3, 1)


def whole(space=pltpu.VMEM):
    return pl.BlockSpec(memory_space=space)


def across(left, right, dims):
    return lax.dot_general(left, right, (dims, ((), ())), preferred_element_type=F32)


NT = ((1,), (1,))
TN = ((0,), (0,))
NN = ((1,), (0,))


def half_of(matrix, head):
    lanes = lax.broadcasted_iota(jnp.int32, matrix.shape, 1)
    inside = (lanes >= head * HEAD_DIM) & (lanes < (head + 1) * HEAD_DIM)
    return jnp.where(inside, matrix, jnp.zeros_like(matrix))


def pack_kernel(q_ref, k_ref, v_ref, out_ref):
    for head in range(8):
        cols = slice(128 * head, 128 * head + 128)
        out_ref[head, 0] = q_ref[:, cols]
        out_ref[head, 1] = k_ref[:, cols]
        out_ref[head, 2] = v_ref[:, cols]


def pack(queries, keys, values):
    return pl.pallas_call(
        pack_kernel,
        out_shape=jax.ShapeDtypeStruct((8, 3, ROWS, 128), BF16),
        in_specs=[whole()] * 3,
        out_specs=whole(),
        name="pack",
    )(queries, keys, values)


def attend_kernel(qkv_ref, ids_ref, out_ref, weights_ref, id_scratch, mixed_scratch):
    step = pl.program_id(0)

    @pl.when(step == 0)
    def _():
        id_scratch[...] = jnp.broadcast_to(ids_ref[...], (128, 1024)).T
        mixed_scratch[0:HALO, :] = jnp.zeros((HALO, 128), BF16)
        mixed_scratch[1024 + HALO :, :] = jnp.zeros((HALO, 128), BF16)

    keys = qkv_ref[:, 1].reshape(1024, 128)
    values = qkv_ref[:, 2].reshape(1024, 128)
    queries = qkv_ref[pl.ds(2 * step, 2), 0].reshape(256, 128) * jnp.asarray(HEAD_DIM**-0.5, BF16)
    row_ids = ids_ref[:, pl.ds(pl.multiple_of(256 * step, 256), 256)]
    key_ids = id_scratch[...]
    same = jnp.concatenate([key_ids, key_ids], 1) == row_ids
    parts = []
    for head in range(2):
        scores = across(keys, half_of(queries, head), NT)
        scores = jnp.where(same, scores, MASKED)
        highest = jnp.max(scores, 0, keepdims=True)
        raised = jnp.exp(scores - highest)
        total = jnp.sum(raised, 0, keepdims=True)
        weights = (raised * (1.0 / total)).astype(BF16)
        weights_ref[head] = weights
        mixed = across(values, weights, TN)
        parts.append(mixed[64 * head : 64 * head + 64])
    mixed = jnp.concatenate(parts, 0).T.astype(BF16)
    mixed_scratch[pl.ds(pl.multiple_of(HALO + 256 * step, 32), 256), :] = mixed

    @pl.when(step == 3)
    def _():
        for s in range(8):
            out_ref[s] = mixed_scratch[128 * s : 128 * s + WINDOW, :]


def attend(qkv, ids_row):
    return pl.pallas_call(
        attend_kernel,
        grid=(4,),
        out_shape=(
            jax.ShapeDtypeStruct((8, WINDOW, 128), BF16),
            jax.ShapeDtypeStruct((2, 1024, 1024), BF16),
        ),
        in_specs=[
            pl.BlockSpec((8, 3, ROWS, 128), lambda j: (0, 0, 0, 0)),
            pl.BlockSpec((1, 1024), lambda j: (0, 0)),
        ],
        out_specs=(
            pl.BlockSpec((8, WINDOW, 128), lambda j: (0, 0, 0)),
            pl.BlockSpec((2, 1024, 256), lambda j: (0, 0, j)),
        ),
        scratch_shapes=[pltpu.VMEM((1024, 128), F32), pltpu.VMEM((1024 + 2 * HALO, 128), BF16)],
        compiler_params=pltpu.CompilerParams(dimension_semantics=("arbitrary",)),
        name="attend",
    )(qkv, ids_row)


def tap_place(tap):
    return (tap + 1) % 8, (tap + 1) // 8 - 2


def middle_kernel(
    parity_ref,
    mixed_ref,
    stream_ref,
    cotangent_ref,
    before_ref,
    after_ref,
    ids_ref,
    attn_out_ref,
    point_in_ref,
    taps_ref,
    point_out_ref,
    norm_gain_ref,
    conv_gain_ref,
    out_ref,
    keep_ref,
    send_ref,
    conv_in_ref,
    moved_ref,
    grad_ref,
    grad_moved_ref,
    ids_moved_ref,
    taps_f32_ref,
    hat_ref,
    linear_ref,
    logistic_ref,
    act_grad_ref,
    activated_ref,
    in_grad_ref,
):
    own = slice(HALO, HALO + ROWS)
    ids = jnp.broadcast_to(ids_ref[...], (128, 256)).T
    grad_ref[...] = jnp.zeros_like(grad_ref)
    taps_f32_ref[...] = taps_ref[...].astype(F32)
    conv_in_ref[0:8, 0:128] = jnp.zeros((8, 128), F32)
    for m in range(8):
        ids_moved_ref[m] = ids[m : m + WINDOW]

    mixed = jnp.concatenate([mixed_ref[h] for h in range(8)], 1)
    hidden = across(mixed, attn_out_ref[...], NN)
    hidden += jnp.concatenate([before_ref[0:HALO], stream_ref[...], after_ref[0:HALO]], 0).astype(F32)
    center = jnp.mean(hidden, -1, keepdims=True)
    shifted = hidden - center
    inverse = lax.rsqrt(jnp.mean(shifted * shifted, -1, keepdims=True) + EPSILON)
    hat = shifted * inverse
    hat_ref[...] = hat[own]
    inverse_in = inverse[own]
    normed = (hat * norm_gain_ref[...]).astype(BF16)
    for c in range(4):
        cols = slice(256 * c, 256 * c + 256)
        gate_cols = slice(1024 + 256 * c, 1024 + 256 * c + 256)
        linear = across(normed, point_in_ref[:, cols], NN)
        logistic = jax.nn.sigmoid(across(normed, point_in_ref[:, gate_cols], NN))
        conv_in_ref[0:WINDOW, cols] = (linear * logistic).astype(BF16).astype(F32)
        linear_ref[:, cols] = linear[own]
        logistic_ref[:, cols] = logistic[own]

    cotangent = jnp.concatenate(
        [before_ref[HALO : 2 * HALO], cotangent_ref[...], after_ref[HALO : 2 * HALO]], 0
    )
    act_grad_ref[...] = across(cotangent, point_out_ref[...], NT)

    @pl.loop(0, 8)
    def _(block):
        cols = pl.ds(pl.multiple_of(128 * block, 128), 128)
        for m in range(8):
            moved_ref[m, 0:184, cols] = conv_in_ref[m : m + 184, cols]

    conv_gain = conv_gain_ref[...]

    @pl.loop(0, 20)
    def _(group):
        base = pl.multiple_of(16 + 8 * group, 8)
        own_ids = ids_moved_ref[0, pl.ds(base, 8), :]
        sums = [jnp.zeros((8, 128), F32) for _ in range(8)]
        for tap in range(TAPS):
            m, a = tap_place(tap)
            rows = pl.ds(pl.multiple_of(base + 8 * a, 8), 8)
            same = ids_moved_ref[m, rows, :] == own_ids
            for block in range(8):
                cols = slice(128 * block, 128 * block + 128)
                term = jnp.where(same, moved_ref[m, rows, cols], 0.0)
                sums[block] = sums[block] + term * taps_f32_ref[tap : tap + 1, cols]
        conv_out = jnp.concatenate(sums, 1)
        shifted = conv_out - jnp.mean(conv_out, -1, keepdims=True)
        inverse = lax.rsqrt(jnp.mean(shifted * shifted, -1, keepdims=True) + EPSILON)
        hat = shifted * inverse
        normed = hat * conv_gain
        logistic = jax.nn.sigmoid(normed)
        activated_ref[pl.ds(base, 8), :] = normed * logistic
        slope = logistic * (1.0 + normed * (1.0 - logistic))
        scaled = act_grad_ref[pl.ds(base, 8), :] * slope * conv_gain
        grad_ref[pl.ds(base, 8), :] = inverse * (
            scaled
            - jnp.mean(scaled, -1, keepdims=True)
            - hat * jnp.mean(scaled * hat, -1, keepdims=True)
        )

    @pl.loop(0, 8)
    def _(block):
        cols = pl.ds(pl.multiple_of(128 * block, 128), 128)
        for m in range(8):
            grad_moved_ref[m, 0:184, cols] = grad_ref[m : m + 184, cols]

        def row_group(group, tap_sums):
            base = pl.multiple_of(HALO + 8 * group, 8)
            own_ids = ids_moved_ref[0, pl.ds(base, 8), :]
            own_grad = grad_moved_ref[0, pl.ds(base, 8), cols]
            total = jnp.zeros((8, 128), F32)
            sums = []
            for tap in range(TAPS):
                m, a = tap_place(tap)
                rows = pl.ds(pl.multiple_of(base + 8 * a, 8), 8)
                same = ids_moved_ref[m, rows, :] == own_ids
                sums.append(tap_sums[tap] + own_grad * jnp.where(same, moved_ref[m, rows, cols], 0.0))
                back = jnp.where(same, grad_moved_ref[m, rows, cols], 0.0)
                total = total + back * taps_f32_ref[30 - tap : 31 - tap, cols]
            in_grad_ref[pl.ds(pl.multiple_of(8 * group, 8), 8), cols] = total
            return tuple(sums)

        tap_sums = lax.fori_loop(
            0, 16, row_group, tuple(jnp.zeros((8, 128), F32) for _ in range(TAPS))
        )
        rows = [jnp.sum(part, 0, keepdims=True) for part in tap_sums]
        rows.append(jnp.zeros((1, 128), F32))
        out_ref[block, 256:288, :] = jnp.concatenate(rows, 0).astype(BF16)

    back = jnp.zeros((ROWS, 1024), F32)
    for c in range(4):
        cols = slice(256 * c, 256 * c + 256)
        gate_cols = slice(1024 + 256 * c, 1024 + 256 * c + 256)
        logistic = logistic_ref[:, cols]
        toward = in_grad_ref[:, cols] * logistic
        gate = (toward * linear_ref[:, cols] * (1.0 - logistic)).astype(BF16)
        back += across(toward.astype(BF16), point_in_ref[:, cols], NT)
        back += across(gate, point_in_ref[:, gate_cols], NT)
    scaled = back * norm_gain_ref[...]
    hat = hat_ref[...]
    stream_grad = cotangent_ref[...].astype(F32) + inverse_in * (
        scaled
        - jnp.mean(scaled, -1, keepdims=True)
        - hat * jnp.mean(scaled * hat, -1, keepdims=True)
    )
    stream_grad = stream_grad.astype(BF16)
    mixed_grad = across(stream_grad, attn_out_ref[...], NT).astype(BF16)
    for h in range(8):
        cols = slice(128 * h, 128 * h + 128)
        out_ref[h, 0:128, :] = mixed_grad[:, cols]
        out_ref[h, 128:256, :] = stream_grad[:, cols]
    activated = activated_ref[own, :].astype(BF16)
    own_mixed = mixed[own]

    @pl.when(parity_ref[0] == 0)
    def _():
        keep_ref[0:128] = own_mixed
        keep_ref[128:256] = stream_grad
        send_ref[0:128] = activated
        send_ref[128:256] = cotangent_ref[...]

    @pl.when(parity_ref[0] != 0)
    def _():
        keep_ref[0:128] = activated
        keep_ref[128:256] = cotangent_ref[...]
        send_ref[0:128] = own_mixed
        send_ref[128:256] = stream_grad


def middle(parity, *arrays):
    return pl.pallas_call(
        middle_kernel,
        out_shape=(
            jax.ShapeDtypeStruct((8, 288, 128), BF16),
            jax.ShapeDtypeStruct((256, 1024), BF16),
            jax.ShapeDtypeStruct((256, 1024), BF16),
        ),
        in_specs=[whole(pltpu.SMEM)] + [whole()] * 12,
        out_specs=(whole(), whole(), whole()),
        scratch_shapes=[
            pltpu.VMEM((WINDOW, 1024), F32),
            pltpu.VMEM((8, WINDOW, 1024), F32),
            pltpu.VMEM((WINDOW, 1024), F32),
            pltpu.VMEM((8, WINDOW, 1024), F32),
            pltpu.VMEM((8, WINDOW, 128), F32),
            pltpu.VMEM((TAPS, 1024), F32),
            pltpu.VMEM((ROWS, 1024), F32),
            pltpu.VMEM((ROWS, 1024), F32),
            pltpu.VMEM((ROWS, 1024), F32),
            pltpu.VMEM((WINDOW, 1024), F32),
            pltpu.VMEM((WINDOW, 1024), F32),
            pltpu.VMEM((ROWS, 1024), F32),
        ],
        name="middle",
    )(parity, *arrays)


def product_kernel(keep_ref, received_ref, order_ref, out_ref):
    left = jnp.concatenate([keep_ref[0:128], received_ref[0:128]], 0)
    right = jnp.concatenate([keep_ref[128:256], received_ref[128:256]], 0)
    left = across(left, order_ref[...], NN).astype(BF16)
    for c in range(4):
        rows = slice(256 * c, 256 * c + 256)
        out_ref[rows, :] = across(left[:, rows], right, TN).astype(BF16)


def product(keep, received, order):
    return pl.pallas_call(
        product_kernel,
        out_shape=jax.ShapeDtypeStruct((1024, 1024), BF16),
        in_specs=[whole()] * 3,
        out_specs=whole(),
        name="product",
    )(keep, received, order)


def attend_back_kernel(qkv_ref, got_ref, weights_ref, out_ref, dq_ref, dk_ref, dv_ref):
    step = pl.program_id(0)
    keys = qkv_ref[:, 1].reshape(1024, 128)
    values = qkv_ref[:, 2].reshape(1024, 128)
    queries = qkv_ref[pl.ds(2 * step, 2), 0].reshape(256, 128) * jnp.asarray(HEAD_DIM**-0.5, BF16)
    upstream = got_ref[pl.ds(2 * step, 2), 0:128].reshape(256, 128)
    dq_parts = []
    dk_add = jnp.zeros((1024, 128), F32)
    dv_add = jnp.zeros((1024, 128), F32)
    for head in range(2):
        own_up = half_of(upstream, head)
        slope = across(values, own_up, NT)
        weights = weights_ref[head]
        wide = weights.astype(F32)
        delta = jnp.sum(wide * slope, 0, keepdims=True)
        score_grad = (wide * (slope - delta)).astype(BF16)
        dv_add += across(weights, own_up, NN)
        dk_add += across(score_grad, half_of(queries, head), NN)
        dq = across(keys, score_grad, TN)
        dq_parts.append(dq[64 * head : 64 * head + 64])
    dq = jnp.concatenate(dq_parts, 0).T * HEAD_DIM**-0.5
    dq_ref[pl.ds(pl.multiple_of(256 * step, 256), 256), :] = dq.astype(BF16)

    @pl.when(step == 0)
    def _():
        dk_ref[...] = dk_add
        dv_ref[...] = dv_add

    @pl.when(step != 0)
    def _():
        dk_ref[...] += dk_add
        dv_ref[...] += dv_add

    @pl.when(step == 3)
    def _():
        grads = (
            dq_ref[...].reshape(8, 128, 128),
            dk_ref[...].astype(BF16).reshape(8, 128, 128),
            dv_ref[...].astype(BF16).reshape(8, 128, 128),
            got_ref[:, 128:256, :],
        )
        for a in range(4):
            for b in range(8):
                out_ref[8 * a + b, :, 0:16, :] = grads[a][:, 16 * b : 16 * b + 16, :]
        tap_sums = jnp.sum(got_ref[:, 256:288, :].astype(F32), 0)
        for d in range(32):
            row = jnp.broadcast_to(tap_sums[d : d + 1], (8, 128)).astype(BF16)
            out_ref[d, :, 16:24, :] = jnp.broadcast_to(row[None], (8, 8, 128))


def attend_back(qkv, got, weights):
    return pl.pallas_call(
        attend_back_kernel,
        grid=(4,),
        out_shape=jax.ShapeDtypeStruct((32, 8, 24, 128), BF16),
        in_specs=[
            pl.BlockSpec((8, 3, ROWS, 128), lambda j: (0, 0, 0, 0)),
            pl.BlockSpec((8, 288, 128), lambda j: (0, 0, 0)),
            pl.BlockSpec((2, 1024, 256), lambda j: (0, 0, j)),
        ],
        out_specs=pl.BlockSpec((32, 8, 24, 128), lambda j: (0, 0, 0, 0)),
        scratch_shapes=[
            pltpu.VMEM((1024, 128), BF16),
            pltpu.VMEM((1024, 128), F32),
            pltpu.VMEM((1024, 128), F32),
        ],
        compiler_params=pltpu.CompilerParams(dimension_semantics=("arbitrary",)),
        name="attend_back",
    )(qkv, got, weights)


def swap_kernel(plan_ref, got_ref, tail_ref, out_ref):
    parts = []
    for h in range(8):
        parts.append(jnp.sum(got_ref[:, h, 16:24, :].astype(F32), 0))
    tap_row = jnp.concatenate(parts, 1)
    row = lax.broadcasted_iota(jnp.int32, (8, 1024), 0)

    @pl.loop(0, 32)
    def _(slot):
        source = plan_ref[slot]
        for h in range(8):
            out_ref[slot, 0:16, 128 * h : 128 * h + 128] = got_ref[source, h, 0:16, :]
        out_ref[slot, 16:24, :] = jnp.where(row == 4, tap_row, tail_ref[slot]).astype(BF16)


def swap(plan, got, tail):
    return pl.pallas_call(
        swap_kernel,
        out_shape=jax.ShapeDtypeStruct((32, 24, 1024), BF16),
        in_specs=[whole(pltpu.SMEM), whole(), whole()],
        out_specs=whole(),
        name="swap",
    )(plan, got, tail)


def unpack_kernel(got_ref, dq_ref, dk_ref, dv_ref, stream_ref, taps_ref, proj_ref):
    outs = (dq_ref, dk_ref, dv_ref, stream_ref)
    for a in range(4):
        for b in range(8):
            outs[a][16 * b : 16 * b + 16, :] = got_ref[8 * a + b, 0:16, :]
    first = jnp.zeros((8, 1024), F32)
    second = jnp.zeros((8, 1024), F32)
    for d in range(32):
        tail = got_ref[d, 16:24, :].astype(F32)
        if d < TAPS:
            taps_ref[d : d + 1, :] = tail[4:5]
        if d % 2 == 0:
            first += tail
        else:
            second += tail
    proj_ref[:, 0:1024] = first[0:4]
    proj_ref[:, 1024:2048] = second[0:4]


def unpack(got):
    rows = jax.ShapeDtypeStruct((ROWS, 1024), BF16)
    return pl.pallas_call(
        unpack_kernel,
        out_shape=(
            rows,
            rows,
            rows,
            rows,
            jax.ShapeDtypeStruct((TAPS, 1024), F32),
            jax.ShapeDtypeStruct((4, 2048), F32),
        ),
        in_specs=[whole()],
        out_specs=(whole(),) * 6,
        name="unpack",
    )(got)


def spread(array, axis):
    return lax.all_to_all(array, axis, split_axis=0, concat_axis=0, tiled=True)


def place_of(s):
    y = s % 4
    return jnp.where(y == 0, 0, jnp.where(y == 3, 1, jnp.where(y == 1, 2, 3)))


def halve(kept, half, partner):
    size = kept.shape[0] // 2
    sent = lax.dynamic_slice_in_dim(kept, (1 - half) * size, size).astype(BF16)
    mine = lax.dynamic_slice_in_dim(kept, half * size, size).astype(F32)
    return mine + lax.ppermute(sent, "seq", partner).astype(F32)


def per_device(
    queries,
    keys,
    values,
    stream,
    cotangent,
    attn_out,
    point_in,
    kernel,
    point_out,
    norm_gain,
    conv_gain,
    segments,
    plan,
):
    queries, keys, values, stream, cotangent = (
        array[0] for array in (queries, keys, values, stream, cotangent)
    )
    slot = lax.axis_index("dp")
    place = lax.axis_index("seq")
    ids = lax.dynamic_index_in_dim(segments, slot, 0, keepdims=False).astype(F32)
    ids_window = lax.dynamic_slice_in_dim(
        jnp.pad(ids, (HALO, 256 - ROWS - HALO), constant_values=-1.0), place * ROWS, 256
    )
    before = lax.ppermute(
        jnp.concatenate([stream[-HALO:], cotangent[-HALO:]], 0),
        "seq",
        [(i, i + 1) for i in range(7)],
    )
    after = lax.ppermute(
        jnp.concatenate([stream[:HALO], cotangent[:HALO]], 0),
        "seq",
        [(i + 1, i) for i in range(7)],
    )
    qkv = spread(pack(queries, keys, values), "seq")
    mixed_heads, weights = attend(qkv, ids[None])
    mixed = spread(mixed_heads, "seq")
    outgoing, keep, send = middle(
        lax.rem(slot, 2)[None].astype(jnp.int32),
        mixed,
        stream,
        cotangent,
        before,
        after,
        ids_window[None],
        attn_out,
        point_in,
        kernel,
        point_out,
        norm_gain[None],
        conv_gain[None],
    )
    got = spread(outgoing, "seq")
    received = lax.ppermute(send, "dp", [(i, i ^ 1) for i in range(32)])
    row = lax.broadcasted_iota(jnp.int32, (1024, 1024), 0)
    column = lax.broadcasted_iota(jnp.int32, (1024, 1024), 1)
    seq_of = (row % 32) // 4
    goal = 512 * (seq_of // 4) + 128 * place_of(seq_of) + 4 * (row // 32) + row % 4
    order = (column == goal).astype(BF16)
    summed = product(keep, received, order)
    y_place = place_of(place)
    summed = halve(summed, place // 4, [(i, i ^ 4) for i in range(8)])
    summed = halve(summed, y_place // 2, [(i, i ^ 1) for i in range(8)])
    summed = halve(summed, y_place % 2, [(i, (i & 4) | (3 - (i & 3))) for i in range(8)])
    tail = jnp.pad(summed.reshape(32, 4, 1024), ((0, 0), (0, 4), (0, 0)))

    first = attend_back(qkv, got, weights)
    first = spread(first.reshape(256, 24, 128), ("dp", "seq")).reshape(32, 8, 24, 128)
    second = spread(swap(plan, first, tail), "dp")
    dq, dk, dv, stream_grad, kernel_grad, proj_grads = unpack(second)
    return (dq[None], dk[None], dv[None], stream_grad[None], kernel_grad, proj_grads)


def solution(mesh):
    rows = P("dp", "seq", None)
    return jax.shard_map(
        per_device,
        mesh=mesh,
        in_specs=(rows,) * 5 + (P(),) * 8,
        out_specs=(rows, rows, rows, rows, P(), P(("dp", "seq"), None)),
        check_vma=False,
    )
```

time: 561 us -> 248 us (0.44); the launches traced: 553 us -> 247 us
  waiting for transfers between devices: 273 us -> 78.1 us
  local copies, waits for them, and re-layouts: 89.5 us -> 8.28 us
  Pallas kernels: 0 us -> 60.2 us
  blocking collectives: 0 us -> 49.2 us
  starting transfers between devices: 83.8 us -> 42.2 us
  matrix products: 41.1 us -> 0 us
  other arithmetic: 33.7 us -> 8.53 us
  between operations: 17.7 us -> 0.78 us
  loops' own time: 14.5 us -> 0 us
    psum x1 -> x0, waiting for transfers between devices: 176 us -> none  [per_device(): kernel_grad = lax.psum(tap_sums(conv_grad, padded, table), ('dp', 'seq'))]
    all_to_all x10 -> x4, waiting for transfers between devices: 95.6 us -> 17.2 us  [spread(): return lax.all_to_all(array, axis, split_axis=0, concat_axis=0, tiled=True)]
    pallas_call x0 -> x7, Pallas kernels: none -> 60.2 us  [the longest x1 26.9 us: middle(): pl.pallas_call(middle_kernel, out_shape=(jax.ShapeDtypeStruct((8, 288, 12...]
    ppermute x4 -> x6, waiting for transfers between devices: 1.26 us -> 60.9 us  [the longest x3 53.7 us: halve(): return mine + lax.ppermute(sent, 'seq', partner).astype(F32)]
    all_to_all x0 -> x1, blocking collectives: none -> 49.2 us  [spread(): return lax.all_to_all(array, axis, split_axis=0, concat_axis=0, tiled=True)]
    dot_general x19 -> x0, matrix products: 41.1 us -> none  [the longest x2 6.67 us: one_block(): jnp.einsum('hqk,hqe->hke', weight_block.astype(jnp.bfloat16), grad_blocks...]
    all_to_all x10 -> x4, starting transfers between devices: 63.9 us -> 30.6 us  [spread(): return lax.all_to_all(array, axis, split_axis=0, concat_axis=0, tiled=True)]
    all_to_all x14 -> x0, local copies, waits for them, and re-layouts: 17.2 us -> none  [the longest x2 3.67 us: in_one_piece(): lax.all_to_all(both, axis, split_axis=split_dim, concat_axis=concat_dim,...]
  transfers between devices with their start and end apart: 15 -> 10, of which waited for: 11 -> 7; matrix products, arithmetic and copies ran while one was open for 13% -> 5% of each run, Pallas kernels for 0% -> 6%
where the time goes in v1:
time: 248 us; the launch traced here: 247 us
  waiting for transfers between devices  78.1 us (31%)
  Pallas kernels  60.2 us (24%)
  blocking collectives  49.2 us (20%)
  starting transfers between devices  42.2 us (17%)
  other arithmetic  8.53 us (3%)
  local copies, waits for them, and re-layouts  8.28 us (3%)
    ppermute x3, waiting for transfers between devices, halve(): return mine + lax.ppermute(sent, 'seq', partner).astype(F32)  53.7 us
    all_to_all x1, blocking collectives, spread(): return lax.all_to_all(array, axis, split_axis=0, concat_axis=0, tiled=True)  49.2 us
    all_to_all x4, starting transfers between devices, spread(): return lax.all_to_all(array, axis, split_axis=0, concat_axis=0, tiled=True)  30.6 us
    pallas_call x1, Pallas kernels, middle(): pl.pallas_call(middle_kernel, out_shape=(jax.ShapeDtypeStruct((8, 288, 12...  26.9 us
    all_to_all x4, waiting for transfers between devices, spread(): return lax.all_to_all(array, axis, split_axis=0, concat_axis=0, tiled=True)  17.2 us
    pallas_call x1, Pallas kernels, attend_back(): pl.pallas_call(attend_back_kernel, grid=(4,), out_shape=jax.ShapeDtypeStr...  10.5 us
    pallas_call x1, Pallas kernels, attend(): pl.pallas_call(attend_kernel, grid=(4,), out_shape=(jax.ShapeDtypeStruct(...  10.3 us
    ppermute x1, waiting for transfers between devices, per_device(): lax.ppermute(jnp.concatenate([stream[:HALO], cotangent[:HALO]], 0), 'seq'...  6.51 us
  transfers between devices with their start and end apart: 10, of which 7 were waited for; matrix products, arithmetic and copies ran while one was open for 5% of the time, Pallas kernels for 6%

profile of v1, /device:TPU:24, one launch (start us, length us, event | category | flops | bytes accessed | tf_op | source)
XLA Modules:
  0.0 247.3 jit_solution(10149100543080140933)
XLA Ops:
  0.6 2.1 pack.1
  2.8 7.1 %all-to-all-start = ((bf16[8,3,128,128]{3,2,1,0:T(8,128)(2,1)}), bf16[8,3,128,128]{3,2,1,0:T(8,128)(2,1)S(1)}, u32[]{:S(2)}, u32[]{:S(2)}) async-start(bf16[8,3,128,128]{3,2,1,0:T(8,128)(2,1)} %pack.1), calls=%async_computation | async-start | bytes 1572864 | tf_op jit(solution)/shard_map/all_to_all | solution.py:470
  9.9 1.4 dynamic-slice_convert_fusion.2.ids_ref
  11.3 1.0 slice_bitcast_fusion
  12.2 9.5 %all-to-all-done.qkv_ref = bf16[8,3,128,128]{3,2,1,0:T(8,128)(2,1)S(1)} async-done(((bf16[8,3,128,128]{3,2,1,0:T(8,128)(2,1)}), bf16[8,3,128,128]{3,2,1,0:T(8,128)(2,1)S(1)}, u32[]{:S(2)}, u32[]{:S(2)}) %all-to-all-start) | async-done | bytes 786464 | tf_op jit(solution)/shard_map/all_to_all | solution.py:470
  21.7 0.9 copy-done
  22.6 10.3 %attend.1 = (bf16[8,192,128]{2,1,0:T(8,128)(2,1)}, bf16[2,1024,1024]{2,1,0:T(8,128)(2,1)}) custom-call(bf16[8,3,128,128]{3,2,1,0:T(8,128)(2,1)} %copy-done, f32[1,1024]{1,0:T(1,128)} %dynamic-slice_convert_fusion.2.ids_ref), custom_call_target="tpu_custom_call" | custom-call | tf_op jit(solution)/shard_map/attend/pallas_call | solution.py:97
  32.9 5.4 %all-to-all-start.1 = ((bf16[8,192,128]{2,1,0:T(8,128)(2,1)}), bf16[8,192,128]{2,1,0:T(8,128)(2,1)S(1)}, u32[]{:S(2)}, u32[]{:S(2)}) async-start(bf16[8,192,128]{2,1,0:T(8,128)(2,1)} %get-tuple-element.17), calls=%async_computation.1 | async-start | bytes 786432 | tf_op jit(solution)/shard_map/all_to_all | solution.py:470
  38.3 4.9 %collective-permute-start = (bf16[64,1024]{1,0:T(8,128)(2,1)S(1)}, bf16[64,1024]{1,0:T(8,128)(2,1)S(1)}, u32[]{:S(2)}, u32[]{:S(2)}) collective-permute-start(bf16[64,1024]{1,0:T(8,128)(2,1)S(1)} %pad_maximum_fusion), channel_id=1, source_target_pairs={{0,1},{1,2},{2,3},{3,4},{4,5},{5,6},{6,7},{8,9},{9,10},{10,11},{11... | collective-permute-start | bytes 393224 | tf_op jit(solution)/shard_map/ppermute | solution.py:509
  43.2 1.9 collective-permute-start.1
  45.1 1.3 pad_dynamic-slice_fusion
  47.1 6.5 %collective-permute-done.1.after_ref = bf16[64,1024]{1,0:T(8,128)(2,1)S(1)} collective-permute-done((bf16[64,1024]{1,0:T(8,128)(2,1)S(1)}, bf16[64,1024]{1,0:T(8,128)(2,1)S(1)}, u32[]{:S(2)}, u32[]{:S(2)}) %collective-permute-start.1) | collective-permute-done | bytes 131104 | tf_op jit(solution)/shard_map/ppermute | solution.py:514
  54.5 26.9 %middle.1 = (bf16[8,288,128]{2,1,0:T(8,128)(2,1)}, bf16[256,1024]{1,0:T(8,128)(2,1)}, bf16[256,1024]{1,0:T(8,128)(2,1)}) custom-call(s32[1]{0:T(128)} %bitcast.3.parity_ref, bf16[8,192,128]{2,1,0:T(8,128)(2,1)} %copy-done.2, bf16[128,1024]{1,0:T(8,128)(2,1)} %bitcast.25, bf16[128,1024]{1,0:T(8,128)(2,1)} %bitcast.26, bf16[64,1024]{1,0:T(8,128)(2,1)} %copy-done.4, ...), custom_call_target="tpu_custom_call" | custom-call | tf_op jit(solution)/shard_map/middle/pallas_call | solution.py:290
  81.3 4.5 %all-to-all-start.2 = ((bf16[8,288,128]{2,1,0:T(8,128)(2,1)}), bf16[8,288,128]{2,1,0:T(8,128)(2,1)S(1)}, u32[]{:S(2)}, u32[]{:S(2)}) async-start(bf16[8,288,128]{2,1,0:T(8,128)(2,1)} %get-tuple-element.18), calls=%async_computation.2 | async-start | bytes 1179648 | tf_op jit(solution)/shard_map/all_to_all | solution.py:470
  86.0 7.7 %all-to-all-done.2.got_ref = bf16[8,288,128]{2,1,0:T(8,128)(2,1)S(1)} async-done(((bf16[8,288,128]{2,1,0:T(8,128)(2,1)}), bf16[8,288,128]{2,1,0:T(8,128)(2,1)S(1)}, u32[]{:S(2)}, u32[]{:S(2)}) %all-to-all-start.2) | async-done | bytes 589856 | tf_op jit(solution)/shard_map/all_to_all | solution.py:470
  94.5 10.5 %attend_back.1 = bf16[32,8,24,128]{3,2,1,0:T(8,128)(2,1)} custom-call(bf16[8,3,128,128]{3,2,1,0:T(8,128)(2,1)} %copy-done, bf16[8,288,128]{2,1,0:T(8,128)(2,1)} %copy-done.1, bf16[2,1024,1024]{2,1,0:T(8,128)(2,1)} %get-tuple-element.19.weights_ref), custom_call_target="tpu_custom_call" | custom-call | tf_op jit(solution)/shard_map/attend_back/pallas_call | solution.py:387
  105.0 13.6 %all-to-all-start.3 = ((bf16[256,24,128]{2,1,0:T(8,128)(2,1)}), bf16[256,24,128]{2,1,0:T(8,128)(2,1)}, u32[]{:S(2)}, u32[]{:S(2)}) async-start(bf16[256,24,128]{2,1,0:T(8,128)(2,1)} %bitcast.24), calls=%async_computation.3 | async-start | bytes 3145728 | tf_op jit(solution)/shard_map/all_to_all | solution.py:470
  118.6 4.2 %fusion.12.order_ref = bf16[1024,1024]{1,0:T(8,128)(2,1)} fusion(s32[1024]{0:T(1024)S(1)} %get-tuple-element.34, s32[1024]{0:T(1024)S(1)} %get-tuple-element.38, s32[1024]{0:T(1024)S(1)} %get-tuple-element.35, s32[1024]{0:T(1024)S(1)} %get-tuple-element.39, s32[1024]{0:T(1024)S(1)} %get-tuple-element.36, s32[1024]{0:T(1024)S(1)} %get-tuple-element.37, ...), kind=kLoop, calls=%fused_computation.25 | loop fusion | flops 53477376 | bytes 2124800 | tf_op jit(solution)/shard_map/convert_element_type | solution.py:543
  122.9 0.8 copy-done.3
  123.7 4.5 %product.1 = bf16[1024,1024]{1,0:T(8,128)(2,1)} custom-call(bf16[256,1024]{1,0:T(8,128)(2,1)} %get-tuple-element.20.keep_ref, bf16[256,1024]{1,0:T(8,128)(2,1)} %copy-done.3, bf16[1024,1024]{1,0:T(8,128)(2,1)} %fusion.12.order_ref), custom_call_target="tpu_custom_call" | custom-call | tf_op jit(solution)/shard_map/product/pallas_call | solution.py:327
  128.2 1.3 constant_dynamic-slice_fusion
  129.5 3.3 %collective-permute-start.3 = (bf16[512,1024]{1,0:T(8,128)(2,1)S(1)}, bf16[512,1024]{1,0:T(8,128)(2,1)S(1)}, u32[]{:S(2)}, u32[]{:S(2)}) collective-permute-start(bf16[512,1024]{1,0:T(8,128)(2,1)S(1)} %constant_dynamic-slice_fusion), channel_id=1, source_target_pairs={{0,4},{1,5},{2,6},{3,7},{4,0},{5,1},{6,2},{7,3},{8,12},{9,13},{10,... | collective-permute-start | bytes 3145736 | tf_op jit(solution)/shard_map/ppermute | solution.py:482
  132.7 33.6 %collective-permute-done.3 = bf16[512,1024]{1,0:T(8,128)(2,1)S(1)} collective-permute-done((bf16[512,1024]{1,0:T(8,128)(2,1)S(1)}, bf16[512,1024]{1,0:T(8,128)(2,1)S(1)}, u32[]{:S(2)}, u32[]{:S(2)}) %collective-permute-start.3) | collective-permute-done | bytes 1048608 | tf_op jit(solution)/shard_map/ppermute | solution.py:482
  166.4 1.6 convert_add_fusion
  168.1 1.1 collective-permute-start.4
  169.2 12.3 %collective-permute-done.4 = bf16[256,1024]{1,0:T(8,128)(2,1)} collective-permute-done((bf16[256,1024]{1,0:T(8,128)(2,1)S(1)}, bf16[256,1024]{1,0:T(8,128)(2,1)}, u32[]{:S(2)}, u32[]{:S(2)}) %collective-permute-start.4) | collective-permute-done | bytes 524320 | tf_op jit(solution)/shard_map/ppermute | solution.py:482
  181.5 1.2 convert_add_fusion.1
  183.1 7.7 %collective-permute-done.5 = bf16[128,1024]{1,0:T(8,128)(2,1)S(1)} collective-permute-done((bf16[128,1024]{1,0:T(8,128)(2,1)S(1)}, bf16[128,1024]{1,0:T(8,128)(2,1)S(1)}, u32[]{:S(2)}, u32[]{:S(2)}) %collective-permute-start.5) | collective-permute-done | bytes 262176 | tf_op jit(solution)/shard_map/ppermute | solution.py:482
  191.1 1.1 pad.9.tail_ref
  192.2 3.4 %swap.1 = bf16[32,24,1024]{2,1,0:T(8,128)(2,1)} custom-call(s32[32]{0:T(128)} %plan_ref.1, bf16[32,8,24,128]{3,2,1,0:T(8,128)(2,1)} %bitcast.15.got_ref, f32[32,8,1024]{2,1,0:T(8,128)} %pad.9.tail_ref), custom_call_target="tpu_custom_call" | custom-call | tf_op jit(solution)/shard_map/swap/pallas_call | solution.py:423
  195.6 49.2 %all_to_all.25.got_ref = bf16[32,24,1024]{2,1,0:T(8,128)(2,1)} all-to-all(bf16[32,24,1024]{2,1,0:T(8,128)(2,1)} %swap.1), channel_id=1, replica_groups=mesh['dp'=32,'seq'=8] {'dp'}, dimensions={0} | all-to-all | bytes 3145728 | tf_op jit(solution)/shard_map/all_to_all | solution.py:470
  244.8 2.4 unpack.1
  (27 shorter events, 3.1 us)
Async XLA Ops:
  2.8 18.9 %all-to-all-start = ((bf16[8,3,128,128]{3,2,1,0:T(8,128)(2,1)}), bf16[8,3,128,128]{3,2,1,0:T(8,128)(2,1)S(1)}, u32[]{:S(2)}, u32[]{:S(2)}) async-start(bf16[8,3,128,128]{3,2,1,0:T(8,128)(2,1)} %pack.1), calls=%async_computation | async-start | bytes 1572864 | tf_op jit(solution)/shard_map/all_to_all | solution.py:470
  21.7 0.9 copy-start
  32.9 20.8 %all-to-all-start.1 = ((bf16[8,192,128]{2,1,0:T(8,128)(2,1)}), bf16[8,192,128]{2,1,0:T(8,128)(2,1)S(1)}, u32[]{:S(2)}, u32[]{:S(2)}) async-start(bf16[8,192,128]{2,1,0:T(8,128)(2,1)} %get-tuple-element.17), calls=%async_computation.1 | async-start | bytes 786432 | tf_op jit(solution)/shard_map/all_to_all | solution.py:470
  38.3 8.9 %collective-permute-start = (bf16[64,1024]{1,0:T(8,128)(2,1)S(1)}, bf16[64,1024]{1,0:T(8,128)(2,1)S(1)}, u32[]{:S(2)}, u32[]{:S(2)}) collective-permute-start(bf16[64,1024]{1,0:T(8,128)(2,1)S(1)} %pad_maximum_fusion), channel_id=1, source_target_pairs={{0,1},{1,2},{2,3},{3,4},{4,5},{5,6},{6,7},{8,9},{9,10},{10,11},{11... | collective-permute-start | bytes 393224 | tf_op jit(solution)/shard_map/ppermute | solution.py:509
  43.2 10.5 %collective-permute-start.1 = (bf16[64,1024]{1,0:T(8,128)(2,1)S(1)}, bf16[64,1024]{1,0:T(8,128)(2,1)S(1)}, u32[]{:S(2)}, u32[]{:S(2)}) collective-permute-start(bf16[64,1024]{1,0:T(8,128)(2,1)S(1)} %pad_maximum_fusion.1), channel_id=1, source_target_pairs={{1,0},{2,1},{3,2},{4,3},{5,4},{6,5},{7,6},{9,8},{10,9},{11,10},{12... | collective-permute-start | bytes 393224 | tf_op jit(solution)/shard_map/ppermute | solution.py:514
  47.1 6.5 %copy-start.4 = (bf16[64,1024]{1,0:T(8,128)(2,1)}, bf16[64,1024]{1,0:T(8,128)(2,1)S(1)}, u32[]{:S(2)}) copy-start(bf16[64,1024]{1,0:T(8,128)(2,1)S(1)} %collective-permute-done.before_ref) | copy-start | bytes 393220
  53.6 0.7 copy-start.5
  53.6 0.8 copy-start.2
  81.3 12.4 %all-to-all-start.2 = ((bf16[8,288,128]{2,1,0:T(8,128)(2,1)}), bf16[8,288,128]{2,1,0:T(8,128)(2,1)S(1)}, u32[]{:S(2)}, u32[]{:S(2)}) async-start(bf16[8,288,128]{2,1,0:T(8,128)(2,1)} %get-tuple-element.18), calls=%async_computation.2 | async-start | bytes 1179648 | tf_op jit(solution)/shard_map/all_to_all | solution.py:470
  85.9 37.0 %collective-permute-start.2 = (bf16[256,1024]{1,0:T(8,128)(2,1)}, bf16[256,1024]{1,0:T(8,128)(2,1)S(1)}, u32[]{:S(2)}, u32[]{:S(2)}) collective-permute-start(bf16[256,1024]{1,0:T(8,128)(2,1)} %get-tuple-element.21), channel_id=1, source_target_pairs={{0,8},{8,0},{16,24},{24,16},{32,40},{40,32},{48,56},{56,48},{64,72... | collective-permute-start | bytes 1572872 | tf_op jit(solution)/shard_map/ppermute | solution.py:538
  93.7 0.8 copy-start.1
  105.0 87.1 %all-to-all-start.3 = ((bf16[256,24,128]{2,1,0:T(8,128)(2,1)}), bf16[256,24,128]{2,1,0:T(8,128)(2,1)}, u32[]{:S(2)}, u32[]{:S(2)}) async-start(bf16[256,24,128]{2,1,0:T(8,128)(2,1)} %bitcast.24), calls=%async_computation.3 | async-start | bytes 3145728 | tf_op jit(solution)/shard_map/all_to_all | solution.py:470
  122.9 0.9 copy-start.3
  129.5 36.9 %collective-permute-start.3 = (bf16[512,1024]{1,0:T(8,128)(2,1)S(1)}, bf16[512,1024]{1,0:T(8,128)(2,1)S(1)}, u32[]{:S(2)}, u32[]{:S(2)}) collective-permute-start(bf16[512,1024]{1,0:T(8,128)(2,1)S(1)} %constant_dynamic-slice_fusion), channel_id=1, source_target_pairs={{0,4},{1,5},{2,6},{3,7},{4,0},{5,1},{6,2},{7,3},{8,12},{9,13},{10,... | collective-permute-start | bytes 3145736 | tf_op jit(solution)/shard_map/ppermute | solution.py:482
  168.1 13.4 %collective-permute-start.4 = (bf16[256,1024]{1,0:T(8,128)(2,1)S(1)}, bf16[256,1024]{1,0:T(8,128)(2,1)}, u32[]{:S(2)}, u32[]{:S(2)}) collective-permute-start(bf16[256,1024]{1,0:T(8,128)(2,1)S(1)} %dynamic-slice_convert_fusion), channel_id=1, source_target_pairs={{0,1},{1,0},{2,3},{3,2},{4,5},{5,4},{6,7},{7,6},{8,9},{9,8},{10,11... | collective-permute-start | bytes 1572872 | tf_op jit(solution)/shard_map/ppermute | solution.py:482
  182.8 8.1 %collective-permute-start.5 = (bf16[128,1024]{1,0:T(8,128)(2,1)S(1)}, bf16[128,1024]{1,0:T(8,128)(2,1)S(1)}, u32[]{:S(2)}, u32[]{:S(2)}) collective-permute-start(bf16[128,1024]{1,0:T(8,128)(2,1)S(1)} %dynamic-slice_convert_fusion.1), channel_id=1, source_target_pairs={{0,3},{1,2},{2,1},{3,0},{4,7},{5,6},{6,5},{7,4},{8,11},{9,10},{10,... | collective-permute-start | bytes 786440 | tf_op jit(solution)/shard_map/ppermute | solution.py:482

commit v2 on v1

--- a/solution.py
+++ b/solution.py
@@ -1,11 +1,10 @@
-import functools
-
 import jax
 import jax.numpy as jnp
 from jax import lax
 from jax.experimental import pallas as pl
 from jax.experimental.pallas import tpu as pltpu
 from jax.sharding import PartitionSpec as P
+
 
 HEAD_DIM = 64
 EPSILON = 1e-05
@@ -15,14 +14,19 @@
 HALO = 32
 ROWS = 128
 WINDOW = ROWS + 2 * HALO
-REACH = 15
 TAPS = 31
-
-ORDER = (0, 2, 3, 1)
 
 
 def whole(space=pltpu.VMEM):
     return pl.BlockSpec(memory_space=space)
+
+
+def in_hbm(shape, dtype):
+    return pltpu.HBM(shape, dtype)
+
+
+def from_hbm(array):
+    return pltpu.with_memory_space_constraint(array, pltpu.HBM)
 
 
 def across(left, right, dims):
@@ -51,11 +55,12 @@
 def pack(queries, keys, values):
     return pl.pallas_call(
         pack_kernel,
-        out_shape=jax.ShapeDtypeStruct((8, 3, ROWS, 128), BF16),
+        out_shape=in_hbm((8, 3, ROWS, 128), BF16),
         in_specs=[whole()] * 3,
         out_specs=whole(),
+        compiler_params=pltpu.CompilerParams(vmem_limit_bytes=6 << 20),
         name="pack",
-    )(queries, keys, values)
+    )(from_hbm(queries), from_hbm(keys), from_hbm(values))
 
 
 def attend_kernel(qkv_ref, ids_ref, out_ref, weights_ref, id_scratch, mixed_scratch):
@@ -98,8 +103,8 @@
         attend_kernel,
         grid=(4,),
         out_shape=(
-            jax.ShapeDtypeStruct((8, WINDOW, 128), BF16),
-            jax.ShapeDtypeStruct((2, 1024, 1024), BF16),
+            in_hbm((8, WINDOW, 128), BF16),
+            in_hbm((2, 1024, 1024), BF16),
         ),
         in_specs=[
             pl.BlockSpec((8, 3, ROWS, 128), lambda j: (0, 0, 0, 0)),
@@ -110,7 +115,9 @@
             pl.BlockSpec((2, 1024, 256), lambda j: (0, 0, j)),
         ),
         scratch_shapes=[pltpu.VMEM((1024, 128), F32), pltpu.VMEM((1024 + 2 * HALO, 128), BF16)],
-        compiler_params=pltpu.CompilerParams(dimension_semantics=("arbitrary",)),
+        compiler_params=pltpu.CompilerParams(
+            dimension_semantics=("arbitrary",), vmem_limit_bytes=20 << 20
+        ),
         name="attend",
     )(qkv, ids_row)
 
@@ -127,15 +134,19 @@
     before_ref,
     after_ref,
     ids_ref,
-    attn_out_ref,
-    point_in_ref,
+    attn_out_hbm,
+    point_in_hbm,
     taps_ref,
-    point_out_ref,
+    point_out_hbm,
     norm_gain_ref,
     conv_gain_ref,
     out_ref,
     keep_ref,
     send_ref,
+    attn_out_ref,
+    point_in_ref,
+    point_out_ref,
+    arrivals,
     conv_in_ref,
     moved_ref,
     grad_ref,
@@ -150,6 +161,12 @@
     in_grad_ref,
 ):
     own = slice(HALO, HALO + ROWS)
+    attn_out_copy = pltpu.make_async_copy(attn_out_hbm, attn_out_ref, arrivals.at[0])
+    point_in_copy = pltpu.make_async_copy(point_in_hbm, point_in_ref, arrivals.at[1])
+    point_out_copy = pltpu.make_async_copy(point_out_hbm, point_out_ref, arrivals.at[2])
+    attn_out_copy.start()
+    point_in_copy.start()
+    point_out_copy.start()
     ids = jnp.broadcast_to(ids_ref[...], (128, 256)).T
     grad_ref[...] = jnp.zeros_like(grad_ref)
     taps_f32_ref[...] = taps_ref[...].astype(F32)
@@ -158,6 +175,7 @@
         ids_moved_ref[m] = ids[m : m + WINDOW]
 
     mixed = jnp.concatenate([mixed_ref[h] for h in range(8)], 1)
+    attn_out_copy.wait()
     hidden = across(mixed, attn_out_ref[...], NN)
     hidden += jnp.concatenate([before_ref[0:HALO], stream_ref[...], after_ref[0:HALO]], 0).astype(F32)
     center = jnp.mean(hidden, -1, keepdims=True)
@@ -167,6 +185,7 @@
     hat_ref[...] = hat[own]
     inverse_in = inverse[own]
     normed = (hat * norm_gain_ref[...]).astype(BF16)
+    point_in_copy.wait()
     for c in range(4):
         cols = slice(256 * c, 256 * c + 256)
         gate_cols = slice(1024 + 256 * c, 1024 + 256 * c + 256)
@@ -179,6 +198,7 @@
     cotangent = jnp.concatenate(
         [before_ref[HALO : 2 * HALO], cotangent_ref[...], after_ref[HALO : 2 * HALO]], 0
     )
+    point_out_copy.wait()
     act_grad_ref[...] = across(cotangent, point_out_ref[...], NT)
 
     @pl.loop(0, 8)
@@ -244,7 +264,9 @@
         )
         rows = [jnp.sum(part, 0, keepdims=True) for part in tap_sums]
         rows.append(jnp.zeros((1, 128), F32))
-        out_ref[block, 256:288, :] = jnp.concatenate(rows, 0).astype(BF16)
+        tap_part = jnp.concatenate(rows, 0).astype(BF16)
+        keep_ref[256:288, cols] = tap_part
+        send_ref[256:288, cols] = tap_part
 
     back = jnp.zeros((ROWS, 1024), F32)
     for c in range(4):
@@ -290,13 +312,19 @@
     return pl.pallas_call(
         middle_kernel,
         out_shape=(
-            jax.ShapeDtypeStruct((8, 288, 128), BF16),
-            jax.ShapeDtypeStruct((256, 1024), BF16),
-            jax.ShapeDtypeStruct((256, 1024), BF16),
+            in_hbm((8, 256, 128), BF16),
+            in_hbm((288, 1024), BF16),
+            in_hbm((288, 1024), BF16),
         ),
-        in_specs=[whole(pltpu.SMEM)] + [whole()] * 12,
+        in_specs=[whole(pltpu.SMEM)]
+        + [whole()] * 6
+        + [whole(pl.ANY), whole(pl.ANY), whole(), whole(pl.ANY), whole(), whole()],
         out_specs=(whole(), whole(), whole()),
         scratch_shapes=[
+            pltpu.VMEM((1024, 1024), BF16),
+            pltpu.VMEM((1024, 2048), BF16),
+            pltpu.VMEM((1024, 1024), BF16),
+            pltpu.SemaphoreType.DMA((3,)),
             pltpu.VMEM((WINDOW, 1024), F32),
             pltpu.VMEM((8, WINDOW, 1024), F32),
             pltpu.VMEM((WINDOW, 1024), F32),
@@ -310,27 +338,50 @@
             pltpu.VMEM((WINDOW, 1024), F32),
             pltpu.VMEM((ROWS, 1024), F32),
         ],
+        compiler_params=pltpu.CompilerParams(vmem_limit_bytes=40 << 20),
         name="middle",
     )(parity, *arrays)
 
 
-def product_kernel(keep_ref, received_ref, order_ref, out_ref):
+def product_kernel(place_ref, keep_ref, received_ref, own_ref, *out_refs):
+    taps_ref = out_refs[7]
     left = jnp.concatenate([keep_ref[0:128], received_ref[0:128]], 0)
     right = jnp.concatenate([keep_ref[128:256], received_ref[128:256]], 0)
-    left = across(left, order_ref[...], NN).astype(BF16)
+    row = lax.broadcasted_iota(jnp.int32, (1024, 128), 0)
+    block = ((row & 31) >> 2) ^ place_ref[0]
+    goal = 128 * block + 4 * (row >> 5) + (row & 3)
+    lane = lax.broadcasted_iota(jnp.int32, (1024, 128), 1)
     for c in range(4):
-        rows = slice(256 * c, 256 * c + 256)
-        out_ref[rows, :] = across(left[:, rows], right, TN).astype(BF16)
-
-
-def product(keep, received, order):
+        order = jnp.concatenate(
+            [
+                jnp.where(goal == lane + (256 * c + 128 * e), 1.0, 0.0).astype(BF16)
+                for e in range(2)
+            ],
+            1,
+        )
+        ordered = across(left, order, NN).astype(BF16)
+        result = across(ordered, right, TN)
+        if c == 0:
+            own_ref[...] = result[0:128]
+        else:
+            out_refs[2 * c - 1][...] = result[0:128].astype(BF16)
+        out_refs[2 * c][...] = result[128:256].astype(BF16)
+    taps_ref[...] = keep_ref[256:288].astype(F32) + received_ref[256:288].astype(F32)
+
+
+def product(place, keep, received):
     return pl.pallas_call(
         product_kernel,
-        out_shape=jax.ShapeDtypeStruct((1024, 1024), BF16),
-        in_specs=[whole()] * 3,
-        out_specs=whole(),
+        out_shape=(
+            jax.ShapeDtypeStruct((ROWS, 1024), F32),
+            *(in_hbm((ROWS, 1024), BF16) for _ in range(7)),
+            in_hbm((32, 1024), F32),
+        ),
+        in_specs=[whole(pltpu.SMEM), whole(), whole()],
+        out_specs=(whole(),) * 9,
+        compiler_params=pltpu.CompilerParams(vmem_limit_bytes=14 << 20),
         name="product",
-    )(keep, received, order)
+    )(place, keep, received)
 
 
 def attend_back_kernel(qkv_ref, got_ref, weights_ref, out_ref, dq_ref, dk_ref, dv_ref):
@@ -376,92 +427,79 @@
         )
         for a in range(4):
             for b in range(8):
-                out_ref[8 * a + b, :, 0:16, :] = grads[a][:, 16 * b : 16 * b + 16, :]
-        tap_sums = jnp.sum(got_ref[:, 256:288, :].astype(F32), 0)
-        for d in range(32):
-            row = jnp.broadcast_to(tap_sums[d : d + 1], (8, 128)).astype(BF16)
-            out_ref[d, :, 16:24, :] = jnp.broadcast_to(row[None], (8, 8, 128))
+                out_ref[8 * a + b] = grads[a][:, 16 * b : 16 * b + 16, :]
 
 
 def attend_back(qkv, got, weights):
     return pl.pallas_call(
         attend_back_kernel,
         grid=(4,),
-        out_shape=jax.ShapeDtypeStruct((32, 8, 24, 128), BF16),
+        out_shape=in_hbm((32, 8, 16, 128), BF16),
         in_specs=[
             pl.BlockSpec((8, 3, ROWS, 128), lambda j: (0, 0, 0, 0)),
-            pl.BlockSpec((8, 288, 128), lambda j: (0, 0, 0)),
+            pl.BlockSpec((8, 256, 128), lambda j: (0, 0, 0)),
             pl.BlockSpec((2, 1024, 256), lambda j: (0, 0, j)),
         ],
-        out_specs=pl.BlockSpec((32, 8, 24, 128), lambda j: (0, 0, 0, 0)),
+        out_specs=pl.BlockSpec((32, 8, 16, 128), lambda j: (0, 0, 0, 0)),
         scratch_shapes=[
             pltpu.VMEM((1024, 128), BF16),
             pltpu.VMEM((1024, 128), F32),
             pltpu.VMEM((1024, 128), F32),
         ],
-        compiler_params=pltpu.CompilerParams(dimension_semantics=("arbitrary",)),
+        compiler_params=pltpu.CompilerParams(
+            dimension_semantics=("arbitrary",), vmem_limit_bytes=20 << 20
+        ),
         name="attend_back",
-    )(qkv, got, weights)
+    )(qkv, got, from_hbm(weights))
 
 
 def swap_kernel(plan_ref, got_ref, tail_ref, out_ref):
-    parts = []
-    for h in range(8):
-        parts.append(jnp.sum(got_ref[:, h, 16:24, :].astype(F32), 0))
-    tap_row = jnp.concatenate(parts, 1)
-    row = lax.broadcasted_iota(jnp.int32, (8, 1024), 0)
-
     @pl.loop(0, 32)
     def _(slot):
         source = plan_ref[slot]
         for h in range(8):
-            out_ref[slot, 0:16, 128 * h : 128 * h + 128] = got_ref[source, h, 0:16, :]
-        out_ref[slot, 16:24, :] = jnp.where(row == 4, tap_row, tail_ref[slot]).astype(BF16)
+            out_ref[slot, 16 * h : 16 * h + 16, :] = got_ref[source, h]
+        rows = tail_ref[slot]
+        pieces = [rows[0:4, 128 * c : 128 * c + 128] for c in range(8)]
+        out_ref[slot, 128:160, :] = jnp.concatenate(pieces, 0).astype(BF16)
 
 
 def swap(plan, got, tail):
     return pl.pallas_call(
         swap_kernel,
-        out_shape=jax.ShapeDtypeStruct((32, 24, 1024), BF16),
+        out_shape=in_hbm((32, 160, 128), BF16),
         in_specs=[whole(pltpu.SMEM), whole(), whole()],
         out_specs=whole(),
+        compiler_params=pltpu.CompilerParams(vmem_limit_bytes=6 << 20),
         name="swap",
     )(plan, got, tail)
 
 
-def unpack_kernel(got_ref, dq_ref, dk_ref, dv_ref, stream_ref, taps_ref, proj_ref):
+def unpack_kernel(got_ref, dq_ref, dk_ref, dv_ref, stream_ref, proj_ref):
     outs = (dq_ref, dk_ref, dv_ref, stream_ref)
     for a in range(4):
         for b in range(8):
-            outs[a][16 * b : 16 * b + 16, :] = got_ref[8 * a + b, 0:16, :]
-    first = jnp.zeros((8, 1024), F32)
-    second = jnp.zeros((8, 1024), F32)
-    for d in range(32):
-        tail = got_ref[d, 16:24, :].astype(F32)
-        if d < TAPS:
-            taps_ref[d : d + 1, :] = tail[4:5]
-        if d % 2 == 0:
-            first += tail
-        else:
-            second += tail
-    proj_ref[:, 0:1024] = first[0:4]
-    proj_ref[:, 1024:2048] = second[0:4]
+            for h in range(8):
+                outs[a][16 * b : 16 * b + 16, 128 * h : 128 * h + 128] = got_ref[
+                    8 * a + b, 16 * h : 16 * h + 16, :
+                ]
+    for core in range(2):
+        total = jnp.zeros((32, 128), F32)
+        for chip in range(16):
+            total += got_ref[2 * chip + core, 128:160, :].astype(F32)
+        for c in range(8):
+            at = 1024 * core + 128 * c
+            proj_ref[:, at : at + 128] = total[4 * c : 4 * c + 4]
 
 
 def unpack(got):
     rows = jax.ShapeDtypeStruct((ROWS, 1024), BF16)
     return pl.pallas_call(
         unpack_kernel,
-        out_shape=(
-            rows,
-            rows,
-            rows,
-            rows,
-            jax.ShapeDtypeStruct((TAPS, 1024), F32),
-            jax.ShapeDtypeStruct((4, 2048), F32),
-        ),
+        out_shape=(rows, rows, rows, rows, jax.ShapeDtypeStruct((4, 2048), F32)),
         in_specs=[whole()],
-        out_specs=(whole(),) * 6,
+        out_specs=(whole(),) * 5,
+        compiler_params=pltpu.CompilerParams(vmem_limit_bytes=6 << 20),
         name="unpack",
     )(got)
 
@@ -470,16 +508,9 @@
     return lax.all_to_all(array, axis, split_axis=0, concat_axis=0, tiled=True)
 
 
-def place_of(s):
-    y = s % 4
-    return jnp.where(y == 0, 0, jnp.where(y == 3, 1, jnp.where(y == 1, 2, 3)))
-
-
-def halve(kept, half, partner):
-    size = kept.shape[0] // 2
-    sent = lax.dynamic_slice_in_dim(kept, (1 - half) * size, size).astype(BF16)
-    mine = lax.dynamic_slice_in_dim(kept, half * size, size).astype(F32)
-    return mine + lax.ppermute(sent, "seq", partner).astype(F32)
+def add_from(taps, axis, partner):
+    arrived = lax.ppermute(taps, axis, partner)
+    return taps + arrived
 
 
 def per_device(
@@ -527,36 +558,42 @@
         before,
         after,
         ids_window[None],
-        attn_out,
-        point_in,
+        from_hbm(attn_out),
+        from_hbm(point_in),
         kernel,
-        point_out,
+        from_hbm(point_out),
         norm_gain[None],
         conv_gain[None],
     )
     got = spread(outgoing, "seq")
     received = lax.ppermute(send, "dp", [(i, i ^ 1) for i in range(32)])
-    row = lax.broadcasted_iota(jnp.int32, (1024, 1024), 0)
-    column = lax.broadcasted_iota(jnp.int32, (1024, 1024), 1)
-    seq_of = (row % 32) // 4
-    goal = 512 * (seq_of // 4) + 128 * place_of(seq_of) + 4 * (row // 32) + row % 4
-    order = (column == goal).astype(BF16)
-    summed = product(keep, received, order)
-    y_place = place_of(place)
-    summed = halve(summed, place // 4, [(i, i ^ 4) for i in range(8)])
-    summed = halve(summed, y_place // 2, [(i, i ^ 1) for i in range(8)])
-    summed = halve(summed, y_place % 2, [(i, (i & 4) | (3 - (i & 3))) for i in range(8)])
-    tail = jnp.pad(summed.reshape(32, 4, 1024), ((0, 0), (0, 4), (0, 0)))
-
+    own, *parts, taps = product(place[None].astype(jnp.int32), keep, received)
+    taps = add_from(taps, "dp", [(i, i ^ 2) for i in range(32)])
+    taps = add_from(taps, "dp", [(i, i ^ 4) for i in range(32)])
+    arrived = [
+        lax.ppermute(part, "seq", [(i, i ^ (k + 1)) for i in range(8)])
+        for k, part in enumerate(parts)
+    ]
+    taps = add_from(taps, "dp", [(i, i ^ 8) for i in range(32)])
     first = attend_back(qkv, got, weights)
-    first = spread(first.reshape(256, 24, 128), ("dp", "seq")).reshape(32, 8, 24, 128)
-    second = spread(swap(plan, first, tail), "dp")
-    dq, dk, dv, stream_grad, kernel_grad, proj_grads = unpack(second)
-    return (dq[None], dk[None], dv[None], stream_grad[None], kernel_grad, proj_grads)
+    first = spread(first.reshape(256, 16, 128), ("dp", "seq"))
+    first = first.reshape(32, 8, 16, 128)
+    for part in arrived:
+        own = own + part.astype(F32)
+    tail = jnp.pad(own.reshape(32, 4, 1024), ((0, 0), (0, 4), (0, 0)))
+    taps = add_from(taps, "dp", [(i, i ^ 16) for i in range(32)])
+
+    second, taps = lax.optimization_barrier((swap(plan, first, tail), taps))
+    for bit in (4, 1, 2):
+        taps = add_from(taps, "seq", [(i, i ^ bit) for i in range(8)])
+    second = spread(second, "dp")
+    dq, dk, dv, stream_grad, proj_grads = unpack(second)
+    return (dq[None], dk[None], dv[None], stream_grad[None], taps[:TAPS], proj_grads)
 
 
 def solution(mesh):
     rows = P("dp", "seq", None)
+
     return jax.shard_map(
         per_device,
         mesh=mesh,

time: 248 us -> 227 us (0.915)
  blocking collectives: 49.2 us -> 12.2 us
  starting transfers between devices: 42.2 us -> 64.3 us
  waiting for transfers between devices: 78.1 us -> 91.9 us
  Pallas kernels: 60.2 us -> 52.3 us
  local copies, waits for them, and re-layouts: 8.28 us -> 0.72 us
  other arithmetic: 8.53 us -> 2.78 us
    all_to_all x1, blocking collectives: 49.2 us -> 12.2 us  [spread(): return lax.all_to_all(array, axis, split_axis=0, concat_axis=0, tiled=True)]
    ppermute x3 -> x14, starting transfers between devices: 4.71 us -> 27.5 us  [the longest x7 15.2 us: add_from(): arrived = lax.ppermute(taps, axis, partner)]
    pallas_call x6, Pallas kernels: 57.7 us -> 51.1 us  [the longest x1 25.2 us: middle(): pl.pallas_call(middle_kernel, out_shape=(in_hbm((8, 256, 128), BF16), in_...]
    ppermute x3 -> x14, waiting for transfers between devices: 53.7 us -> 60 us  [the longest x7 42.4 us: add_from(): arrived = lax.ppermute(taps, axis, partner)]
    all_to_all x4, waiting for transfers between devices: 17.2 us -> 21.5 us  [spread(): return lax.all_to_all(array, axis, split_axis=0, concat_axis=0, tiled=True)]
    convert_element_type x1 -> x0, other arithmetic: 4.24 us -> none  [per_device(): order = (column == goal).astype(BF16)]
    unnamed x12 -> x16, local copies, waits for them, and re-layouts: 3.36 us -> 0.39 us
  transfers between devices with their start and end apart: 10 -> 21, of which waited for: 7 -> 13; matrix products, arithmetic and copies ran while one was open for 5% -> 1% of each run, Pallas kernels for 6% -> 1%
where the time goes in v2:
time: 227 us; the launch traced here: 225 us
  waiting for transfers between devices  91.9 us (40%)
  starting transfers between devices  64.3 us (28%)
  Pallas kernels  52.3 us (23%)
  blocking collectives  12.2 us (5%)
  other arithmetic  2.78 us (1%)
    ppermute x7, waiting for transfers between devices, add_from(): arrived = lax.ppermute(taps, axis, partner)  42.4 us
    all_to_all x4, starting transfers between devices, spread(): return lax.all_to_all(array, axis, split_axis=0, concat_axis=0, tiled=True)  29.6 us
    pallas_call x1, Pallas kernels, middle(): pl.pallas_call(middle_kernel, out_shape=(in_hbm((8, 256, 128), BF16), in_...  25.2 us
    all_to_all x4, waiting for transfers between devices, spread(): return lax.all_to_all(array, axis, split_axis=0, concat_axis=0, tiled=True)  21.5 us
    ppermute x7, waiting for transfers between devices, per_device(): lax.ppermute(part, 'seq', [(i, i ^ k + 1) for i in range(8)])  17.6 us
    ppermute x7, starting transfers between devices, add_from(): arrived = lax.ppermute(taps, axis, partner)  15.2 us
    all_to_all x1, blocking collectives, spread(): return lax.all_to_all(array, axis, split_axis=0, concat_axis=0, tiled=True)  12.2 us
    ppermute x7, starting transfers between devices, per_device(): lax.ppermute(part, 'seq', [(i, i ^ k + 1) for i in range(8)])  12.2 us
  transfers between devices with their start and end apart: 21, of which 13 were waited for; matrix products, arithmetic and copies ran while one was open for 1% of the time, Pallas kernels for 1%

profile of v2, /device:TPU:24, one launch (start us, length us, event | category | flops | bytes accessed | tf_op | source)
XLA Modules:
  0.0 225.0 jit_solution(18022528491960644449)
XLA Ops:
  0.7 2.2 pack.1
  2.8 7.3 %all-to-all-start = ((bf16[8,3,128,128]{3,2,1,0:T(8,128)(2,1)}), bf16[8,3,128,128]{3,2,1,0:T(8,128)(2,1)S(1)}, u32[]{:S(2)}, u32[]{:S(2)}) async-start(bf16[8,3,128,128]{3,2,1,0:T(8,128)(2,1)} %pack.1), calls=%async_computation | async-start | bytes 1572864 | tf_op jit(solution)/shard_map/all_to_all | solution.py:508
  10.9 11.0 %all-to-all-done.qkv_ref = bf16[8,3,128,128]{3,2,1,0:T(8,128)(2,1)S(1)} async-done(((bf16[8,3,128,128]{3,2,1,0:T(8,128)(2,1)}), bf16[8,3,128,128]{3,2,1,0:T(8,128)(2,1)S(1)}, u32[]{:S(2)}, u32[]{:S(2)}) %all-to-all-start) | async-done | bytes 786464 | tf_op jit(solution)/shard_map/all_to_all | solution.py:508
  21.9 9.2 %attend.1 = (bf16[8,192,128]{2,1,0:T(8,128)(2,1)}, bf16[2,1024,1024]{2,1,0:T(8,128)(2,1)}) custom-call(bf16[8,3,128,128]{3,2,1,0:T(8,128)(2,1)S(1)} %all-to-all-done.qkv_ref, f32[1,1024]{1,0:T(1,128)S(1)} %dynamic-slice_convert_fusion.ids_ref), custom_call_target="tpu_custom_call" | custom-call | tf_op jit(solution)/shard_map/attend/pallas_call | solution.py:102
  31.1 5.4 %all-to-all-start.1 = ((bf16[8,192,128]{2,1,0:T(8,128)(2,1)}), bf16[8,192,128]{2,1,0:T(8,128)(2,1)S(1)}, u32[]{:S(2)}, u32[]{:S(2)}) async-start(bf16[8,192,128]{2,1,0:T(8,128)(2,1)} %get-tuple-element.27), calls=%async_computation.1 | async-start | bytes 786432 | tf_op jit(solution)/shard_map/all_to_all | solution.py:508
  36.4 4.9 %collective-permute-start = (bf16[64,1024]{1,0:T(8,128)(2,1)S(1)}, bf16[64,1024]{1,0:T(8,128)(2,1)S(1)}, u32[]{:S(2)}, u32[]{:S(2)}) collective-permute-start(bf16[64,1024]{1,0:T(8,128)(2,1)S(1)} %pad_maximum_fusion), channel_id=1, source_target_pairs={{0,1},{1,2},{2,3},{3,4},{4,5},{5,6},{6,7},{8,9},{9,10},{10,11},{11... | collective-permute-start | bytes 393224 | tf_op jit(solution)/shard_map/ppermute | solution.py:540
  41.3 1.9 collective-permute-start.1
  43.3 1.9 collective-permute-done.before_ref
  45.3 6.5 %collective-permute-done.1.after_ref = bf16[64,1024]{1,0:T(8,128)(2,1)S(1)} collective-permute-done((bf16[64,1024]{1,0:T(8,128)(2,1)S(1)}, bf16[64,1024]{1,0:T(8,128)(2,1)S(1)}, u32[]{:S(2)}, u32[]{:S(2)}) %collective-permute-start.1) | collective-permute-done | bytes 131104 | tf_op jit(solution)/shard_map/ppermute | solution.py:545
  51.8 25.2 %middle.1 = (bf16[8,256,128]{2,1,0:T(8,128)(2,1)}, bf16[288,1024]{1,0:T(8,128)(2,1)}, bf16[288,1024]{1,0:T(8,128)(2,1)}) custom-call(s32[1]{0:T(128)} %bitcast.3.parity_ref, bf16[8,192,128]{2,1,0:T(8,128)(2,1)S(1)} %all-to-all-done.1.mixed_ref, bf16[128,1024]{1,0:T(8,128)(2,1)S(1)} %bitcast.26, bf16[128,1024]{1,0:T(8,128)(2,1)S(1)} %bitcast.27, ...), custom_call_target="tpu_custom_call" | custom-call | tf_op jit(solution)/shard_map/middle/pallas_call | solution.py:312
  77.1 12.2 %all_to_all.25.got_ref = bf16[8,256,128]{2,1,0:T(8,128)(2,1)S(1)} all-to-all(bf16[8,256,128]{2,1,0:T(8,128)(2,1)} %get-tuple-element.28), channel_id=1, replica_groups=mesh['dp'=32,'seq'=8] {'seq'}, dimensions={0} | all-to-all | bytes 1048576 | tf_op jit(solution)/shard_map/all_to_all | solution.py:508
  89.3 9.8 %attend_back.1 = bf16[32,8,16,128]{3,2,1,0:T(8,128)(2,1)} custom-call(bf16[8,3,128,128]{3,2,1,0:T(8,128)(2,1)S(1)} %all-to-all-done.qkv_ref, bf16[8,256,128]{2,1,0:T(8,128)(2,1)S(1)} %all_to_all.25.got_ref, bf16[2,1024,1024]{2,1,0:T(8,128)(2,1)} %get-tuple-element.29.weights_ref), custom_call_target="tpu_custom_call" | custom-call | tf_op jit(solution)/shard_map/attend_back/pallas_call | solution.py:434
  99.1 12.5 %all-to-all-start.3 = ((bf16[256,16,128]{2,1,0:T(8,128)(2,1)}), bf16[256,16,128]{2,1,0:T(8,128)(2,1)S(1)}, u32[]{:S(2)}, u32[]{:S(2)}) async-start(bf16[256,16,128]{2,1,0:T(8,128)(2,1)} %bitcast.32), calls=%async_computation.3 | async-start | bytes 2097152 | tf_op jit(solution)/shard_map/all_to_all | solution.py:508
  112.0 1.9 collective-permute-done.2.received_ref
  113.9 2.9 %product.1 = (f32[128,1024]{1,0:T(8,128)S(1)}, bf16[128,1024]{1,0:T(8,128)(2,1)}, bf16[128,1024]{1,0:T(8,128)(2,1)}, bf16[128,1024]{1,0:T(8,128)(2,1)}, bf16[128...) custom-call(s32[1]{0:T(128)} %bitcast.16.place_ref, ...), custom_call_target="tpu_custom_call" | custom-call | tf_op jit(solution)/shard_map/product/pallas_call | solution.py:373
  116.8 1.7 collective-permute-start.10
  120.3 17.6 %collective-permute-done.10 = f32[32,1024]{1,0:T(8,128)S(1)} collective-permute-done((f32[32,1024]{1,0:T(8,128)}, f32[32,1024]{1,0:T(8,128)S(1)}, u32[]{:S(2)}, u32[]{:S(2)}) %collective-permute-start.10) | collective-permute-done | bytes 131104 | tf_op jit(solution)/shard_map/ppermute | solution.py:512
  138.9 2.9 %collective-permute-start.11 = (f32[32,1024]{1,0:T(8,128)S(1)}, f32[32,1024]{1,0:T(8,128)S(1)}, u32[]{:S(2)}, u32[]{:S(2)}) collective-permute-start(f32[32,1024]{1,0:T(8,128)S(1)} %add.62), channel_id=1, source_target_pairs={{0,32},{8,40},{16,48},{24,56},{32,0},{40,8},{48,16},{56,24},{64,96... | collective-permute-start | bytes 393224 | tf_op jit(solution)/shard_map/ppermute | solution.py:512
  141.8 5.9 %collective-permute-done.11 = f32[32,1024]{1,0:T(8,128)S(1)} collective-permute-done((f32[32,1024]{1,0:T(8,128)S(1)}, f32[32,1024]{1,0:T(8,128)S(1)}, u32[]{:S(2)}, u32[]{:S(2)}) %collective-permute-start.11) | collective-permute-done | bytes 131104 | tf_op jit(solution)/shard_map/ppermute | solution.py:512
  147.7 5.6 %collective-permute-start.12 = (f32[32,1024]{1,0:T(8,128)S(1)}, f32[32,1024]{1,0:T(8,128)S(1)}, u32[]{:S(2)}, u32[]{:S(2)}) collective-permute-start(f32[32,1024]{1,0:T(8,128)S(1)} %add.63), channel_id=1, source_target_pairs={{0,64},{8,72},{16,80},{24,88},{32,96},{40,104},{48,112},{56,120},{... | collective-permute-start | bytes 393224 | tf_op jit(solution)/shard_map/ppermute | solution.py:512
  153.7 3.1 %collective-permute-start.6 = (bf16[128,1024]{1,0:T(8,128)(2,1)}, bf16[128,1024]{1,0:T(8,128)(2,1)S(1)}, u32[]{:S(2)}, u32[]{:S(2)}) collective-permute-start(bf16[128,1024]{1,0:T(8,128)(2,1)} %get-tuple-element.36), channel_id=1, source_target_pairs={{0,4},{1,5},{2,6},{3,7},{4,0},{5,1},{6,2},{7,3},{8,12},{9,13},{10,... | collective-permute-start | bytes 786440 | tf_op jit(solution)/shard_map/ppermute | solution.py:574
  157.6 5.9 %collective-permute-start.8 = (bf16[128,1024]{1,0:T(8,128)(2,1)}, bf16[128,1024]{1,0:T(8,128)(2,1)S(1)}, u32[]{:S(2)}, u32[]{:S(2)}) collective-permute-start(bf16[128,1024]{1,0:T(8,128)(2,1)} %get-tuple-element.38), channel_id=1, source_target_pairs={{0,6},{1,7},{2,4},{3,5},{4,2},{5,3},{6,0},{7,1},{8,14},{9,15},{10,... | collective-permute-start | bytes 786440 | tf_op jit(solution)/shard_map/ppermute | solution.py:574
  165.3 5.1 %collective-permute-done.7 = bf16[128,1024]{1,0:T(8,128)(2,1)S(1)} collective-permute-done((bf16[128,1024]{1,0:T(8,128)(2,1)}, bf16[128,1024]{1,0:T(8,128)(2,1)S(1)}, u32[]{:S(2)}, u32[]{:S(2)}) %collective-permute-start.7) | collective-permute-done | bytes 262176 | tf_op jit(solution)/shard_map/ppermute | solution.py:574
  170.4 6.9 %collective-permute-done.8 = bf16[128,1024]{1,0:T(8,128)(2,1)S(1)} collective-permute-done((bf16[128,1024]{1,0:T(8,128)(2,1)}, bf16[128,1024]{1,0:T(8,128)(2,1)S(1)}, u32[]{:S(2)}, u32[]{:S(2)}) %collective-permute-start.8) | collective-permute-done | bytes 262176 | tf_op jit(solution)/shard_map/ppermute | solution.py:574
  177.3 5.7 %collective-permute-done.9 = bf16[128,1024]{1,0:T(8,128)(2,1)S(1)} collective-permute-done((bf16[128,1024]{1,0:T(8,128)(2,1)}, bf16[128,1024]{1,0:T(8,128)(2,1)S(1)}, u32[]{:S(2)}, u32[]{:S(2)}) %collective-permute-start.9) | collective-permute-done | bytes 262176 | tf_op jit(solution)/shard_map/ppermute | solution.py:574
  183.9 1.9 swap.1
  185.8 4.5 %all-to-all-start.4 = ((bf16[32,160,128]{2,1,0:T(8,128)(2,1)}), bf16[32,160,128]{2,1,0:T(8,128)(2,1)S(1)}, u32[]{:S(2)}, u32[]{:S(2)}) async-start(bf16[32,160,128]{2,1,0:T(8,128)(2,1)} %swap.1), calls=%async_computation.4 | async-start | bytes 2621440 | tf_op jit(solution)/shard_map/all_to_all | solution.py:508
  190.2 2.9 %collective-permute-start.14 = (f32[32,1024]{1,0:T(8,128)S(1)}, f32[32,1024]{1,0:T(8,128)S(1)}, u32[]{:S(2)}, u32[]{:S(2)}) collective-permute-start(f32[32,1024]{1,0:T(8,128)S(1)} %add.65), channel_id=1, source_target_pairs={{0,4},{1,5},{2,6},{3,7},{4,0},{5,1},{6,2},{7,3},{8,12},{9,13},{10,... | collective-permute-start | bytes 393224 | tf_op jit(solution)/shard_map/ppermute | solution.py:512
  193.1 7.8 %collective-permute-done.14 = f32[32,1024]{1,0:T(8,128)S(1)} collective-permute-done((f32[32,1024]{1,0:T(8,128)S(1)}, f32[32,1024]{1,0:T(8,128)S(1)}, u32[]{:S(2)}, u32[]{:S(2)}) %collective-permute-start.14) | collective-permute-done | bytes 131104 | tf_op jit(solution)/shard_map/ppermute | solution.py:512
  201.0 5.0 %collective-permute-done.15 = f32[32,1024]{1,0:T(8,128)S(1)} collective-permute-done((f32[32,1024]{1,0:T(8,128)S(1)}, f32[32,1024]{1,0:T(8,128)S(1)}, u32[]{:S(2)}, u32[]{:S(2)}) %collective-permute-start.15) | collective-permute-done | bytes 131104 | tf_op jit(solution)/shard_map/ppermute | solution.py:512
  206.5 6.1 %collective-permute-done.16 = f32[32,1024]{1,0:T(8,128)S(1)} collective-permute-done((f32[32,1024]{1,0:T(8,128)S(1)}, f32[32,1024]{1,0:T(8,128)S(1)}, u32[]{:S(2)}, u32[]{:S(2)}) %collective-permute-start.16) | collective-permute-done | bytes 131104 | tf_op jit(solution)/shard_map/ppermute | solution.py:512
  213.3 10.6 %all-to-all-done.4.got_ref = bf16[32,160,128]{2,1,0:T(8,128)(2,1)S(1)} async-done(((bf16[32,160,128]{2,1,0:T(8,128)(2,1)}), bf16[32,160,128]{2,1,0:T(8,128)(2,1)S(1)}, u32[]{:S(2)}, u32[]{:S(2)}) %all-to-all-start.4) | async-done | bytes 1310752 | tf_op jit(solution)/shard_map/all_to_all | solution.py:508
  (49 shorter events, 10.4 us)
Async XLA Ops:
  0.6 10.3 %copy-start.1 = (bf16[1,128,1024]{2,1,0:T(8,128)(2,1)S(1)}, bf16[1,128,1024]{2,1,0:T(8,128)(2,1)}, u32[]{:S(2)}) copy-start(bf16[1,128,1024]{2,1,0:T(8,128)(2,1)} %param.17) | copy-start | bytes 786436
  0.6 10.3 %copy-start = (bf16[1,128,1024]{2,1,0:T(8,128)(2,1)S(1)}, bf16[1,128,1024]{2,1,0:T(8,128)(2,1)}, u32[]{:S(2)}) copy-start(bf16[1,128,1024]{2,1,0:T(8,128)(2,1)} %param.16) | copy-start | bytes 786436
  2.8 49.0 %copy-start.3 = (bf16[31,1024]{1,0:T(8,128)(2,1)S(1)}, bf16[31,1024]{1,0:T(8,128)(2,1)}, u32[]{:S(2)}) copy-start(bf16[31,1024]{1,0:T(8,128)(2,1)} %taps_ref.1) | copy-start | bytes 190468
  2.8 49.0 %copy-start.4 = (f32[1024]{0:T(1024)S(1)}, f32[1024]{0:T(1024)}, u32[]{:S(2)}) copy-start(f32[1024]{0:T(1024)} %param.22) | copy-start | bytes 12292
  2.8 49.0 %copy-start.5 = (f32[1024]{0:T(1024)S(1)}, f32[1024]{0:T(1024)}, u32[]{:S(2)}) copy-start(f32[1024]{0:T(1024)} %param.23) | copy-start | bytes 12292
  2.8 19.1 %all-to-all-start = ((bf16[8,3,128,128]{3,2,1,0:T(8,128)(2,1)}), bf16[8,3,128,128]{3,2,1,0:T(8,128)(2,1)S(1)}, u32[]{:S(2)}, u32[]{:S(2)}) async-start(bf16[8,3,128,128]{3,2,1,0:T(8,128)(2,1)} %pack.1), calls=%async_computation | async-start | bytes 1572864 | tf_op jit(solution)/shard_map/all_to_all | solution.py:508
  31.1 20.8 %all-to-all-start.1 = ((bf16[8,192,128]{2,1,0:T(8,128)(2,1)}), bf16[8,192,128]{2,1,0:T(8,128)(2,1)S(1)}, u32[]{:S(2)}, u32[]{:S(2)}) async-start(bf16[8,192,128]{2,1,0:T(8,128)(2,1)} %get-tuple-element.27), calls=%async_computation.1 | async-start | bytes 786432 | tf_op jit(solution)/shard_map/all_to_all | solution.py:508
  36.4 8.9 %collective-permute-start = (bf16[64,1024]{1,0:T(8,128)(2,1)S(1)}, bf16[64,1024]{1,0:T(8,128)(2,1)S(1)}, u32[]{:S(2)}, u32[]{:S(2)}) collective-permute-start(bf16[64,1024]{1,0:T(8,128)(2,1)S(1)} %pad_maximum_fusion), channel_id=1, source_target_pairs={{0,1},{1,2},{2,3},{3,4},{4,5},{5,6},{6,7},{8,9},{9,10},{10,11},{11... | collective-permute-start | bytes 393224 | tf_op jit(solution)/shard_map/ppermute | solution.py:540
  41.3 10.5 %collective-permute-start.1 = (bf16[64,1024]{1,0:T(8,128)(2,1)S(1)}, bf16[64,1024]{1,0:T(8,128)(2,1)S(1)}, u32[]{:S(2)}, u32[]{:S(2)}) collective-permute-start(bf16[64,1024]{1,0:T(8,128)(2,1)S(1)} %pad_maximum_fusion.1), channel_id=1, source_target_pairs={{1,0},{2,1},{3,2},{4,3},{5,4},{6,5},{7,6},{9,8},{10,9},{11,10},{12... | collective-permute-start | bytes 393224 | tf_op jit(solution)/shard_map/ppermute | solution.py:545
  99.1 12.5 %copy-start.7 = (bf16[288,1024]{1,0:T(8,128)(2,1)S(1)}, bf16[288,1024]{1,0:T(8,128)(2,1)}, u32[]{:S(2)}) copy-start(bf16[288,1024]{1,0:T(8,128)(2,1)} %get-tuple-element.31) | copy-start | bytes 1769476
  99.1 14.8 %copy-start.2 = (bf16[288,1024]{1,0:T(8,128)(2,1)S(1)}, bf16[288,1024]{1,0:T(8,128)(2,1)}, u32[]{:S(2)}) copy-start(bf16[288,1024]{1,0:T(8,128)(2,1)} %get-tuple-element.30.keep_ref) | copy-start | bytes 1769476
  99.1 84.4 %all-to-all-start.3 = ((bf16[256,16,128]{2,1,0:T(8,128)(2,1)}), bf16[256,16,128]{2,1,0:T(8,128)(2,1)S(1)}, u32[]{:S(2)}, u32[]{:S(2)}) async-start(bf16[256,16,128]{2,1,0:T(8,128)(2,1)} %bitcast.32), calls=%async_computation.3 | async-start | bytes 2097152 | tf_op jit(solution)/shard_map/all_to_all | solution.py:508
  111.6 2.3 %collective-permute-start.2 = (bf16[288,1024]{1,0:T(8,128)(2,1)S(1)}, bf16[288,1024]{1,0:T(8,128)(2,1)S(1)}, u32[]{:S(2)}, u32[]{:S(2)}) collective-permute-start(bf16[288,1024]{1,0:T(8,128)(2,1)S(1)} %copy-done.7), channel_id=1, source_target_pairs={{0,8},{8,0},{16,24},{24,16},{32,40},{40,32},{48,56},{56,48},{64,72... | collective-permute-start | bytes 1769480 | tf_op jit(solution)/shard_map/ppermute | solution.py:569
  116.8 21.2 %collective-permute-start.10 = (f32[32,1024]{1,0:T(8,128)}, f32[32,1024]{1,0:T(8,128)S(1)}, u32[]{:S(2)}, u32[]{:S(2)}) collective-permute-start(f32[32,1024]{1,0:T(8,128)} %get-tuple-element.40), channel_id=1, source_target_pairs={{0,16},{8,24},{16,0},{24,8},{32,48},{40,56},{48,32},{56,40},{64,80... | collective-permute-start | bytes 393224 | tf_op jit(solution)/shard_map/ppermute | solution.py:512
  118.5 38.2 %collective-permute-start.3 = (bf16[128,1024]{1,0:T(8,128)(2,1)}, bf16[128,1024]{1,0:T(8,128)(2,1)S(1)}, u32[]{:S(2)}, u32[]{:S(2)}) collective-permute-start(bf16[128,1024]{1,0:T(8,128)(2,1)} %get-tuple-element.33), channel_id=1, source_target_pairs={{0,1},{1,0},{2,3},{3,2},{4,5},{5,4},{6,7},{7,6},{8,9},{9,8},{10,11... | collective-permute-start | bytes 786440 | tf_op jit(solution)/shard_map/ppermute | solution.py:574
  119.3 38.3 %collective-permute-start.4 = (bf16[128,1024]{1,0:T(8,128)(2,1)}, bf16[128,1024]{1,0:T(8,128)(2,1)S(1)}, u32[]{:S(2)}, u32[]{:S(2)}) collective-permute-start(bf16[128,1024]{1,0:T(8,128)(2,1)} %get-tuple-element.34), channel_id=1, source_target_pairs={{0,2},{1,3},{2,0},{3,1},{4,6},{5,7},{6,4},{7,5},{8,10},{9,11},{10,... | collective-permute-start | bytes 786440 | tf_op jit(solution)/shard_map/ppermute | solution.py:574
  138.9 8.8 %collective-permute-start.11 = (f32[32,1024]{1,0:T(8,128)S(1)}, f32[32,1024]{1,0:T(8,128)S(1)}, u32[]{:S(2)}, u32[]{:S(2)}) collective-permute-start(f32[32,1024]{1,0:T(8,128)S(1)} %add.62), channel_id=1, source_target_pairs={{0,32},{8,40},{16,48},{24,56},{32,0},{40,8},{48,16},{56,24},{64,96... | collective-permute-start | bytes 393224 | tf_op jit(solution)/shard_map/ppermute | solution.py:512
  147.7 15.8 %collective-permute-start.12 = (f32[32,1024]{1,0:T(8,128)S(1)}, f32[32,1024]{1,0:T(8,128)S(1)}, u32[]{:S(2)}, u32[]{:S(2)}) collective-permute-start(f32[32,1024]{1,0:T(8,128)S(1)} %add.63), channel_id=1, source_target_pairs={{0,64},{8,72},{16,80},{24,88},{32,96},{40,104},{48,112},{56,120},{... | collective-permute-start | bytes 393224 | tf_op jit(solution)/shard_map/ppermute | solution.py:512
  153.3 10.4 %collective-permute-start.5 = (bf16[128,1024]{1,0:T(8,128)(2,1)}, bf16[128,1024]{1,0:T(8,128)(2,1)S(1)}, u32[]{:S(2)}, u32[]{:S(2)}) collective-permute-start(bf16[128,1024]{1,0:T(8,128)(2,1)} %get-tuple-element.35), channel_id=1, source_target_pairs={{0,3},{1,2},{2,1},{3,0},{4,7},{5,6},{6,5},{7,4},{8,11},{9,10},{10,... | collective-permute-start | bytes 786440 | tf_op jit(solution)/shard_map/ppermute | solution.py:574
  153.7 11.7 %collective-permute-start.6 = (bf16[128,1024]{1,0:T(8,128)(2,1)}, bf16[128,1024]{1,0:T(8,128)(2,1)S(1)}, u32[]{:S(2)}, u32[]{:S(2)}) collective-permute-start(bf16[128,1024]{1,0:T(8,128)(2,1)} %get-tuple-element.36), channel_id=1, source_target_pairs={{0,4},{1,5},{2,6},{3,7},{4,0},{5,1},{6,2},{7,3},{8,12},{9,13},{10,... | collective-permute-start | bytes 786440 | tf_op jit(solution)/shard_map/ppermute | solution.py:574
  156.7 13.7 %collective-permute-start.7 = (bf16[128,1024]{1,0:T(8,128)(2,1)}, bf16[128,1024]{1,0:T(8,128)(2,1)S(1)}, u32[]{:S(2)}, u32[]{:S(2)}) collective-permute-start(bf16[128,1024]{1,0:T(8,128)(2,1)} %get-tuple-element.37), channel_id=1, source_target_pairs={{0,5},{1,4},{2,7},{3,6},{4,1},{5,0},{6,3},{7,2},{8,13},{9,12},{10,... | collective-permute-start | bytes 786440 | tf_op jit(solution)/shard_map/ppermute | solution.py:574
  157.6 19.7 %collective-permute-start.8 = (bf16[128,1024]{1,0:T(8,128)(2,1)}, bf16[128,1024]{1,0:T(8,128)(2,1)S(1)}, u32[]{:S(2)}, u32[]{:S(2)}) collective-permute-start(bf16[128,1024]{1,0:T(8,128)(2,1)} %get-tuple-element.38), channel_id=1, source_target_pairs={{0,6},{1,7},{2,4},{3,5},{4,2},{5,3},{6,0},{7,1},{8,14},{9,15},{10,... | collective-permute-start | bytes 786440 | tf_op jit(solution)/shard_map/ppermute | solution.py:574
  163.5 19.4 %collective-permute-start.9 = (bf16[128,1024]{1,0:T(8,128)(2,1)}, bf16[128,1024]{1,0:T(8,128)(2,1)S(1)}, u32[]{:S(2)}, u32[]{:S(2)}) collective-permute-start(bf16[128,1024]{1,0:T(8,128)(2,1)} %get-tuple-element.39), channel_id=1, source_target_pairs={{0,7},{1,6},{2,5},{3,4},{4,3},{5,2},{6,1},{7,0},{8,15},{9,14},{10,... | collective-permute-start | bytes 786440 | tf_op jit(solution)/shard_map/ppermute | solution.py:574
  163.8 19.7 %collective-permute-start.13 = (f32[32,1024]{1,0:T(8,128)S(1)}, f32[32,1024]{1,0:T(8,128)S(1)}, u32[]{:S(2)}, u32[]{:S(2)}) collective-permute-start(f32[32,1024]{1,0:T(8,128)S(1)} %add.64), channel_id=1, source_target_pairs={{0,128},{8,136},{16,144},{24,152},{32,160},{40,168},{48,176},{56,1... | collective-permute-start | bytes 393224 | tf_op jit(solution)/shard_map/ppermute | solution.py:512
  183.2 0.7 copy-start.6
  185.8 38.1 %all-to-all-start.4 = ((bf16[32,160,128]{2,1,0:T(8,128)(2,1)}), bf16[32,160,128]{2,1,0:T(8,128)(2,1)S(1)}, u32[]{:S(2)}, u32[]{:S(2)}) async-start(bf16[32,160,128]{2,1,0:T(8,128)(2,1)} %swap.1), calls=%async_computation.4 | async-start | bytes 2621440 | tf_op jit(solution)/shard_map/all_to_all | solution.py:508
  190.2 10.7 %collective-permute-start.14 = (f32[32,1024]{1,0:T(8,128)S(1)}, f32[32,1024]{1,0:T(8,128)S(1)}, u32[]{:S(2)}, u32[]{:S(2)}) collective-permute-start(f32[32,1024]{1,0:T(8,128)S(1)} %add.65), channel_id=1, source_target_pairs={{0,4},{1,5},{2,6},{3,7},{4,0},{5,1},{6,2},{7,3},{8,12},{9,13},{10,... | collective-permute-start | bytes 393224 | tf_op jit(solution)/shard_map/ppermute | solution.py:512
  200.9 5.1 %collective-permute-start.15 = (f32[32,1024]{1,0:T(8,128)S(1)}, f32[32,1024]{1,0:T(8,128)S(1)}, u32[]{:S(2)}, u32[]{:S(2)}) collective-permute-start(f32[32,1024]{1,0:T(8,128)S(1)} %add.66), channel_id=1, source_target_pairs={{0,1},{1,0},{2,3},{3,2},{4,5},{5,4},{6,7},{7,6},{8,9},{9,8},{10,11... | collective-permute-start | bytes 393224 | tf_op jit(solution)/shard_map/ppermute | solution.py:512
  206.1 6.6 %collective-permute-start.16 = (f32[32,1024]{1,0:T(8,128)S(1)}, f32[32,1024]{1,0:T(8,128)S(1)}, u32[]{:S(2)}, u32[]{:S(2)}) collective-permute-start(f32[32,1024]{1,0:T(8,128)S(1)} %add.67), channel_id=1, source_target_pairs={{0,2},{1,3},{2,0},{3,1},{4,6},{5,7},{6,4},{7,5},{8,10},{9,11},{10,... | collective-permute-start | bytes 393224 | tf_op jit(solution)/shard_map/ppermute | solution.py:512

commit v3 on v2

--- a/solution.py
+++ b/solution.py
@@ -63,7 +63,9 @@
     )(from_hbm(queries), from_hbm(keys), from_hbm(values))
 
 
-def attend_kernel(qkv_ref, ids_ref, out_ref, weights_ref, id_scratch, mixed_scratch):
+def attend_kernel(
+    qkv_ref, ids_ref, out_ref, weights_ref, id_scratch, mixed_scratch, turned_scratch, score_scratch
+):
     step = pl.program_id(0)
 
     @pl.when(step == 0)
@@ -71,23 +73,37 @@
         id_scratch[...] = jnp.broadcast_to(ids_ref[...], (128, 1024)).T
         mixed_scratch[0:HALO, :] = jnp.zeros((HALO, 128), BF16)
         mixed_scratch[1024 + HALO :, :] = jnp.zeros((HALO, 128), BF16)
-
-    keys = qkv_ref[:, 1].reshape(1024, 128)
-    values = qkv_ref[:, 2].reshape(1024, 128)
+        turned_scratch[...] = qkv_ref[:, 2].reshape(1024, 128).T
+
     queries = qkv_ref[pl.ds(2 * step, 2), 0].reshape(256, 128) * jnp.asarray(HEAD_DIM**-0.5, BF16)
     row_ids = ids_ref[:, pl.ds(pl.multiple_of(256 * step, 256), 256)]
-    key_ids = id_scratch[...]
-    same = jnp.concatenate([key_ids, key_ids], 1) == row_ids
+    peaks = []
+    for head in range(2):
+        own_queries = half_of(queries, head)
+        peak = jnp.full((8, 256), MASKED, F32)
+        for i in range(8):
+            rows = slice(128 * i, 128 * i + 128)
+            key_ids = id_scratch[rows, :]
+            same = jnp.concatenate([key_ids, key_ids], 1) == row_ids
+            scores = jnp.where(same, across(qkv_ref[i, 1], own_queries, NT), MASKED)
+            score_scratch[head, rows, :] = scores
+            peak = jnp.maximum(peak, jnp.max(scores.reshape(16, 8, 256), 0))
+        peaks.append(jnp.max(peak, 0, keepdims=True))
+    scales = []
+    for head in range(2):
+        total = jnp.zeros((8, 256), F32)
+        for i in range(8):
+            rows = slice(128 * i, 128 * i + 128)
+            raised = jnp.exp(score_scratch[head, rows, :] - peaks[head])
+            score_scratch[head, rows, :] = raised
+            total = total + jnp.sum(raised.reshape(16, 8, 256), 0)
+        scales.append(1.0 / jnp.sum(total, 0, keepdims=True))
     parts = []
     for head in range(2):
-        scores = across(keys, half_of(queries, head), NT)
-        scores = jnp.where(same, scores, MASKED)
-        highest = jnp.max(scores, 0, keepdims=True)
-        raised = jnp.exp(scores - highest)
-        total = jnp.sum(raised, 0, keepdims=True)
-        weights = (raised * (1.0 / total)).astype(BF16)
-        weights_ref[head] = weights
-        mixed = across(values, weights, TN)
+        for i in range(8):
+            rows = slice(128 * i, 128 * i + 128)
+            weights_ref[head, rows, :] = (score_scratch[head, rows, :] * scales[head]).astype(BF16)
+        mixed = across(turned_scratch[...], weights_ref[head], NN)
         parts.append(mixed[64 * head : 64 * head + 64])
     mixed = jnp.concatenate(parts, 0).T.astype(BF16)
     mixed_scratch[pl.ds(pl.multiple_of(HALO + 256 * step, 32), 256), :] = mixed
@@ -114,7 +130,12 @@
             pl.BlockSpec((8, WINDOW, 128), lambda j: (0, 0, 0)),
             pl.BlockSpec((2, 1024, 256), lambda j: (0, 0, j)),
         ),
-        scratch_shapes=[pltpu.VMEM((1024, 128), F32), pltpu.VMEM((1024 + 2 * HALO, 128), BF16)],
+        scratch_shapes=[
+            pltpu.VMEM((1024, 128), F32),
+            pltpu.VMEM((1024 + 2 * HALO, 128), BF16),
+            pltpu.VMEM((128, 1024), BF16),
+            pltpu.VMEM((2, 1024, 256), F32),
+        ],
         compiler_params=pltpu.CompilerParams(
             dimension_semantics=("arbitrary",), vmem_limit_bytes=20 << 20
         ),
@@ -159,6 +180,7 @@
     act_grad_ref,
     activated_ref,
     in_grad_ref,
+    tap_sums_ref,
 ):
     own = slice(HALO, HALO + ROWS)
     attn_out_copy = pltpu.make_async_copy(attn_out_hbm, attn_out_ref, arrivals.at[0])
@@ -209,20 +231,24 @@
 
     conv_gain = conv_gain_ref[...]
 
-    @pl.loop(0, 20)
-    def _(group):
-        base = pl.multiple_of(16 + 8 * group, 8)
+    def tapped(source_ref, base, weight_of):
         own_ids = ids_moved_ref[0, pl.ds(base, 8), :]
         sums = [jnp.zeros((8, 128), F32) for _ in range(8)]
         for tap in range(TAPS):
             m, a = tap_place(tap)
             rows = pl.ds(pl.multiple_of(base + 8 * a, 8), 8)
             same = ids_moved_ref[m, rows, :] == own_ids
+            at = weight_of(tap)
             for block in range(8):
                 cols = slice(128 * block, 128 * block + 128)
-                term = jnp.where(same, moved_ref[m, rows, cols], 0.0)
-                sums[block] = sums[block] + term * taps_f32_ref[tap : tap + 1, cols]
-        conv_out = jnp.concatenate(sums, 1)
+                term = jnp.where(same, source_ref[m, rows, cols], 0.0)
+                sums[block] = sums[block] + term * taps_f32_ref[at : at + 1, cols]
+        return jnp.concatenate(sums, 1)
+
+    @pl.loop(0, 20)
+    def _(group):
+        base = pl.multiple_of(16 + 8 * group, 8)
+        conv_out = tapped(moved_ref, base, lambda tap: tap)
         shifted = conv_out - jnp.mean(conv_out, -1, keepdims=True)
         inverse = lax.rsqrt(jnp.mean(shifted * shifted, -1, keepdims=True) + EPSILON)
         hat = shifted * inverse
@@ -243,30 +269,48 @@
         for m in range(8):
             grad_moved_ref[m, 0:184, cols] = grad_ref[m : m + 184, cols]
 
-        def row_group(group, tap_sums):
+    @pl.loop(0, 16)
+    def _(group):
+        base = pl.multiple_of(HALO + 8 * group, 8)
+        in_grad_ref[pl.ds(pl.multiple_of(8 * group, 8), 8), :] = tapped(
+            grad_moved_ref, base, lambda tap: 30 - tap
+        )
+
+    tap_sums_ref[31:32, :] = jnp.zeros((1, 1024), F32)
+    for first in range(0, TAPS, 4):
+        here = list(range(first, min(first + 4, TAPS)))
+
+        def row_group(group, sums, here=here):
             base = pl.multiple_of(HALO + 8 * group, 8)
             own_ids = ids_moved_ref[0, pl.ds(base, 8), :]
-            own_grad = grad_moved_ref[0, pl.ds(base, 8), cols]
-            total = jnp.zeros((8, 128), F32)
-            sums = []
-            for tap in range(TAPS):
+            places = []
+            for tap in here:
                 m, a = tap_place(tap)
                 rows = pl.ds(pl.multiple_of(base + 8 * a, 8), 8)
-                same = ids_moved_ref[m, rows, :] == own_ids
-                sums.append(tap_sums[tap] + own_grad * jnp.where(same, moved_ref[m, rows, cols], 0.0))
-                back = jnp.where(same, grad_moved_ref[m, rows, cols], 0.0)
-                total = total + back * taps_f32_ref[30 - tap : 31 - tap, cols]
-            in_grad_ref[pl.ds(pl.multiple_of(8 * group, 8), 8), cols] = total
-            return tuple(sums)
-
-        tap_sums = lax.fori_loop(
-            0, 16, row_group, tuple(jnp.zeros((8, 128), F32) for _ in range(TAPS))
+                places.append((m, rows, ids_moved_ref[m, rows, :] == own_ids))
+            grown = []
+            for block in range(8):
+                cols = slice(128 * block, 128 * block + 128)
+                own_grad = grad_ref[pl.ds(base, 8), cols]
+                for at, (m, rows, same) in enumerate(places):
+                    term = jnp.where(same, moved_ref[m, rows, cols], 0.0)
+                    grown.append(sums[len(here) * block + at] + own_grad * term)
+            return tuple(grown)
+
+        sums = lax.fori_loop(
+            0,
+            16,
+            row_group,
+            tuple(jnp.zeros((8, 128), F32) for _ in range(8 * len(here))),
+            unroll=4,
         )
-        rows = [jnp.sum(part, 0, keepdims=True) for part in tap_sums]
-        rows.append(jnp.zeros((1, 128), F32))
-        tap_part = jnp.concatenate(rows, 0).astype(BF16)
-        keep_ref[256:288, cols] = tap_part
-        send_ref[256:288, cols] = tap_part
+        for at, tap in enumerate(here):
+            tap_sums_ref[tap : tap + 1, :] = jnp.concatenate(
+                [jnp.sum(sums[len(here) * block + at], 0, keepdims=True) for block in range(8)], 1
+            )
+    tap_part = tap_sums_ref[...].astype(BF16)
+    keep_ref[256:288, :] = tap_part
+    send_ref[256:288, :] = tap_part
 
     back = jnp.zeros((ROWS, 1024), F32)
     for c in range(4):
@@ -337,14 +381,14 @@
             pltpu.VMEM((WINDOW, 1024), F32),
             pltpu.VMEM((WINDOW, 1024), F32),
             pltpu.VMEM((ROWS, 1024), F32),
+            pltpu.VMEM((32, 1024), F32),
         ],
         compiler_params=pltpu.CompilerParams(vmem_limit_bytes=40 << 20),
         name="middle",
     )(parity, *arrays)
 
 
-def product_kernel(place_ref, keep_ref, received_ref, own_ref, *out_refs):
-    taps_ref = out_refs[7]
+def product_kernel(place_ref, keep_ref, received_ref, own_ref, sent_ref):
     left = jnp.concatenate([keep_ref[0:128], received_ref[0:128]], 0)
     right = jnp.concatenate([keep_ref[128:256], received_ref[128:256]], 0)
     row = lax.broadcasted_iota(jnp.int32, (1024, 128), 0)
@@ -361,49 +405,58 @@
         )
         ordered = across(left, order, NN).astype(BF16)
         result = across(ordered, right, TN)
-        if c == 0:
-            own_ref[...] = result[0:128]
+        if c < 2:
+            own_ref[256 * c : 256 * c + 256] = result
         else:
-            out_refs[2 * c - 1][...] = result[0:128].astype(BF16)
-        out_refs[2 * c][...] = result[128:256].astype(BF16)
-    taps_ref[...] = keep_ref[256:288].astype(F32) + received_ref[256:288].astype(F32)
+            sent_ref[256 * c - 512 : 256 * c - 256] = result.astype(BF16)
 
 
 def product(place, keep, received):
     return pl.pallas_call(
         product_kernel,
-        out_shape=(
-            jax.ShapeDtypeStruct((ROWS, 1024), F32),
-            *(in_hbm((ROWS, 1024), BF16) for _ in range(7)),
-            in_hbm((32, 1024), F32),
-        ),
+        out_shape=(in_hbm((512, 1024), F32), in_hbm((512, 1024), BF16)),
         in_specs=[whole(pltpu.SMEM), whole(), whole()],
-        out_specs=(whole(),) * 9,
+        out_specs=(whole(),) * 2,
         compiler_params=pltpu.CompilerParams(vmem_limit_bytes=14 << 20),
         name="product",
     )(place, keep, received)
 
 
-def attend_back_kernel(qkv_ref, got_ref, weights_ref, out_ref, dq_ref, dk_ref, dv_ref):
+def attend_back_kernel(
+    qkv_ref, got_ref, weights_ref, out_ref, dq_ref, dk_ref, dv_ref, turned_scratch, slope_scratch, change_scratch
+):
     step = pl.program_id(0)
-    keys = qkv_ref[:, 1].reshape(1024, 128)
-    values = qkv_ref[:, 2].reshape(1024, 128)
+
+    @pl.when(step == 0)
+    def _():
+        turned_scratch[...] = qkv_ref[:, 1].reshape(1024, 128).T
+
     queries = qkv_ref[pl.ds(2 * step, 2), 0].reshape(256, 128) * jnp.asarray(HEAD_DIM**-0.5, BF16)
     upstream = got_ref[pl.ds(2 * step, 2), 0:128].reshape(256, 128)
+    own_queries = [half_of(queries, head) for head in range(2)]
+    own_up = [half_of(upstream, head) for head in range(2)]
+    deltas = []
+    for head in range(2):
+        delta = jnp.zeros((8, 256), F32)
+        for i in range(8):
+            rows = slice(128 * i, 128 * i + 128)
+            slope = across(qkv_ref[i, 2], own_up[head], NT)
+            slope_scratch[head, rows, :] = slope
+            product = weights_ref[head, rows, :].astype(F32) * slope
+            delta = delta + jnp.sum(product.reshape(16, 8, 256), 0)
+        deltas.append(jnp.sum(delta, 0, keepdims=True))
     dq_parts = []
-    dk_add = jnp.zeros((1024, 128), F32)
-    dv_add = jnp.zeros((1024, 128), F32)
     for head in range(2):
-        own_up = half_of(upstream, head)
-        slope = across(values, own_up, NT)
-        weights = weights_ref[head]
-        wide = weights.astype(F32)
-        delta = jnp.sum(wide * slope, 0, keepdims=True)
-        score_grad = (wide * (slope - delta)).astype(BF16)
-        dv_add += across(weights, own_up, NN)
-        dk_add += across(score_grad, half_of(queries, head), NN)
-        dq = across(keys, score_grad, TN)
+        for i in range(8):
+            rows = slice(128 * i, 128 * i + 128)
+            wide = weights_ref[head, rows, :].astype(F32)
+            change = wide * (slope_scratch[head, rows, :] - deltas[head])
+            change_scratch[rows, 256 * head : 256 * head + 256] = change.astype(BF16)
+        dq = across(turned_scratch[...], change_scratch[:, 256 * head : 256 * head + 256], NN)
         dq_parts.append(dq[64 * head : 64 * head + 64])
+    both_weights = jnp.concatenate([weights_ref[0], weights_ref[1]], 1)
+    dv_add = across(both_weights, jnp.concatenate(own_up, 0), NN)
+    dk_add = across(change_scratch[...], jnp.concatenate(own_queries, 0), NN)
     dq = jnp.concatenate(dq_parts, 0).T * HEAD_DIM**-0.5
     dq_ref[pl.ds(pl.multiple_of(256 * step, 256), 256), :] = dq.astype(BF16)
 
@@ -445,6 +498,9 @@
             pltpu.VMEM((1024, 128), BF16),
             pltpu.VMEM((1024, 128), F32),
             pltpu.VMEM((1024, 128), F32),
+            pltpu.VMEM((128, 1024), BF16),
+            pltpu.VMEM((2, 1024, 256), F32),
+            pltpu.VMEM((1024, 512), BF16),
         ],
         compiler_params=pltpu.CompilerParams(
             dimension_semantics=("arbitrary",), vmem_limit_bytes=20 << 20
@@ -454,14 +510,16 @@
 
 
 def swap_kernel(plan_ref, got_ref, tail_ref, out_ref):
-    @pl.loop(0, 32)
-    def _(slot):
-        source = plan_ref[slot]
-        for h in range(8):
-            out_ref[slot, 16 * h : 16 * h + 16, :] = got_ref[source, h]
-        rows = tail_ref[slot]
-        pieces = [rows[0:4, 128 * c : 128 * c + 128] for c in range(8)]
-        out_ref[slot, 128:160, :] = jnp.concatenate(pieces, 0).astype(BF16)
+    @pl.loop(0, 16)
+    def _(pair):
+        rows = tail_ref[pl.ds(pl.multiple_of(8 * pair, 8), 8), :]
+        for e in range(2):
+            slot = 2 * pair + e
+            source = plan_ref[slot]
+            for h in range(8):
+                out_ref[slot, 16 * h : 16 * h + 16, :] = got_ref[source, h]
+            pieces = [rows[4 * e : 4 * e + 4, 128 * c : 128 * c + 128] for c in range(8)]
+            out_ref[slot, 128:160, :] = jnp.concatenate(pieces, 0).astype(BF16)
 
 
 def swap(plan, got, tail):
@@ -506,6 +564,10 @@
 
 def spread(array, axis):
     return lax.all_to_all(array, axis, split_axis=0, concat_axis=0, tiled=True)
+
+
+def along_z(device, partners):
+    return (device & 17) | (partners[(device >> 1) & 7] << 1)
 
 
 def add_from(taps, axis, partner):
@@ -567,21 +629,25 @@
     )
     got = spread(outgoing, "seq")
     received = lax.ppermute(send, "dp", [(i, i ^ 1) for i in range(32)])
-    own, *parts, taps = product(place[None].astype(jnp.int32), keep, received)
+    taps = keep[256:288].astype(F32) + received[256:288].astype(F32)
     taps = add_from(taps, "dp", [(i, i ^ 2) for i in range(32)])
-    taps = add_from(taps, "dp", [(i, i ^ 4) for i in range(32)])
-    arrived = [
-        lax.ppermute(part, "seq", [(i, i ^ (k + 1)) for i in range(8)])
-        for k, part in enumerate(parts)
-    ]
-    taps = add_from(taps, "dp", [(i, i ^ 8) for i in range(32)])
+    own, sent = product(place[None].astype(jnp.int32), keep, received)
+    crossed = lax.ppermute(sent, "seq", [(i, i ^ 4) for i in range(8)])
+    taps = add_from(taps, "dp", [(i, along_z(i, (7, 2, 1, 4, 3, 6, 5, 0))) for i in range(32)])
+    taps = add_from(taps, "dp", [(i, i ^ 16) for i in range(32)])
     first = attend_back(qkv, got, weights)
     first = spread(first.reshape(256, 16, 128), ("dp", "seq"))
     first = first.reshape(32, 8, 16, 128)
+    own = own + crossed.astype(F32)
+    quarters = [own[128 * k : 128 * k + 128] for k in range(4)]
+    quarters = [quarters[0]] + [part.astype(BF16) for part in quarters[1:]]
+    arrived = [
+        lax.ppermute(quarters[k], "seq", [(i, i ^ k) for i in range(8)]) for k in (1, 2, 3)
+    ]
+    tail = quarters[0]
     for part in arrived:
-        own = own + part.astype(F32)
-    tail = jnp.pad(own.reshape(32, 4, 1024), ((0, 0), (0, 4), (0, 0)))
-    taps = add_from(taps, "dp", [(i, i ^ 16) for i in range(32)])
+        tail = tail + part.astype(F32)
+    taps = add_from(taps, "dp", [(i, along_z(i, (3, 6, 5, 0, 7, 2, 1, 4))) for i in range(32)])
 
     second, taps = lax.optimization_barrier((swap(plan, first, tail), taps))
     for bit in (4, 1, 2):

time: 227 us -> 206 us (0.907)
  blocking collectives: 12.2 us -> 0 us
  Pallas kernels: 52.3 us -> 46.3 us
  waiting for transfers between devices: 91.9 us -> 86.3 us
  other arithmetic: 2.78 us -> 5.41 us
    ppermute x7 -> x4, waiting for transfers between devices: 17.6 us -> 3.22 us  [the longest x3 3.22 us: per_device(): lax.ppermute(quarters[k], 'seq', [(i, i ^ k) for i in range(8)])]
    all_to_all x1 -> x0, blocking collectives: 12.2 us -> none  [spread(): return lax.all_to_all(array, axis, split_axis=0, concat_axis=0, tiled=True)]
    ppermute x7, waiting for transfers between devices: 42.4 us -> 49.9 us  [add_from(): arrived = lax.ppermute(taps, axis, partner)]
    all_to_all x4 -> x5, starting transfers between devices: 29.6 us -> 35.2 us  [spread(): return lax.all_to_all(array, axis, split_axis=0, concat_axis=0, tiled=True)]
    ppermute x7 -> x4, starting transfers between devices: 12.2 us -> 7.15 us  [the longest x3 4.18 us: per_device(): lax.ppermute(quarters[k], 'seq', [(i, i ^ k) for i in range(8)])]
    all_to_all x4 -> x5, waiting for transfers between devices: 21.5 us -> 24.8 us  [spread(): return lax.all_to_all(array, axis, split_axis=0, concat_axis=0, tiled=True)]
    pallas_call x1, Pallas kernels: 25.2 us -> 22.7 us  [middle(): pl.pallas_call(middle_kernel, out_shape=(in_hbm((8, 256, 128), BF16), in_...]
  transfers between devices with their start and end apart: 21 -> 19, of which waited for: 13 -> 12; matrix products, arithmetic and copies ran while one was open for 1% -> 3% of each run, Pallas kernels for 1% -> 6%
where the time goes in v3:
time: 206 us; the launch traced here: 203 us
  waiting for transfers between devices  86.3 us (42%)
  starting transfers between devices  63.2 us (31%)
  Pallas kernels  46.3 us (22%)
  other arithmetic  5.41 us (3%)
    ppermute x7, waiting for transfers between devices, add_from(): arrived = lax.ppermute(taps, axis, partner)  49.9 us
    all_to_all x5, starting transfers between devices, spread(): return lax.all_to_all(array, axis, split_axis=0, concat_axis=0, tiled=True)  35.2 us
    all_to_all x5, waiting for transfers between devices, spread(): return lax.all_to_all(array, axis, split_axis=0, concat_axis=0, tiled=True)  24.8 us
    pallas_call x1, Pallas kernels, middle(): pl.pallas_call(middle_kernel, out_shape=(in_hbm((8, 256, 128), BF16), in_...  22.7 us
    ppermute x7, starting transfers between devices, add_from(): arrived = lax.ppermute(taps, axis, partner)  14 us
    pallas_call x1, Pallas kernels, attend_back(): pl.pallas_call(attend_back_kernel, grid=(4,), out_shape=in_hbm((32, 8, 16...  8.61 us
    pallas_call x1, Pallas kernels, attend(): pl.pallas_call(attend_kernel, grid=(4,), out_shape=(in_hbm((8, WINDOW, 12...  7.04 us
    ppermute x1, waiting for transfers between devices, per_device(): lax.ppermute(jnp.concatenate([stream[:HALO], cotangent[:HALO]], 0), 'seq'...  6.52 us
  transfers between devices with their start and end apart: 19, of which 12 were waited for; matrix products, arithmetic and copies ran while one was open for 3% of the time, Pallas kernels for 6%

profile of v3, /device:TPU:24, one launch (start us, length us, event | category | flops | bytes accessed | tf_op | source)
XLA Modules:
  0.0 203.4 jit_solution(14615243255061361768)
XLA Ops:
  0.7 2.2 %pack.1 = bf16[8,3,128,128]{3,2,1,0:T(8,128)(2,1)} custom-call(bf16[128,1024]{1,0:T(8,128)(2,1)} %bitcast.33, bf16[128,1024]{1,0:T(8,128)(2,1)} %bitcast.34, bf16[128,1024]{1,0:T(8,128)(2,1)} %bitcast.35), custom_call_target="tpu_custom_call" | custom-call | tf_op jit(solution)/shard_map/pack/pallas_call | solution.py:56
  2.8 7.3 %all-to-all-start = ((bf16[8,3,128,128]{3,2,1,0:T(8,128)(2,1)}), bf16[8,3,128,128]{3,2,1,0:T(8,128)(2,1)S(1)}, u32[]{:S(2)}, u32[]{:S(2)}) async-start(bf16[8,3,128,128]{3,2,1,0:T(8,128)(2,1)} %pack.1), calls=%async_computation | async-start | bytes 1572864 | tf_op jit(solution)/shard_map/all_to_all | solution.py:566
  10.9 11.0 %all-to-all-done.qkv_ref = bf16[8,3,128,128]{3,2,1,0:T(8,128)(2,1)S(1)} async-done(((bf16[8,3,128,128]{3,2,1,0:T(8,128)(2,1)}), bf16[8,3,128,128]{3,2,1,0:T(8,128)(2,1)S(1)}, u32[]{:S(2)}, u32[]{:S(2)}) %all-to-all-start) | async-done | bytes 786464 | tf_op jit(solution)/shard_map/all_to_all | solution.py:566
  21.9 7.0 %attend.1 = (bf16[8,192,128]{2,1,0:T(8,128)(2,1)}, bf16[2,1024,1024]{2,1,0:T(8,128)(2,1)}) custom-call(bf16[8,3,128,128]{3,2,1,0:T(8,128)(2,1)S(1)} %all-to-all-done.qkv_ref, f32[1,1024]{1,0:T(1,128)S(1)} %dynamic-slice_convert_fusion.ids_ref), custom_call_target="tpu_custom_call" | custom-call | tf_op jit(solution)/shard_map/attend/pallas_call | solution.py:118
  28.9 5.4 %all-to-all-start.1 = ((bf16[8,192,128]{2,1,0:T(8,128)(2,1)}), bf16[8,192,128]{2,1,0:T(8,128)(2,1)S(1)}, u32[]{:S(2)}, u32[]{:S(2)}) async-start(bf16[8,192,128]{2,1,0:T(8,128)(2,1)} %get-tuple-element.20), calls=%async_computation.1 | async-start | bytes 786432 | tf_op jit(solution)/shard_map/all_to_all | solution.py:566
  34.3 4.9 %collective-permute-start = (bf16[64,1024]{1,0:T(8,128)(2,1)S(1)}, bf16[64,1024]{1,0:T(8,128)(2,1)S(1)}, u32[]{:S(2)}, u32[]{:S(2)}) collective-permute-start(bf16[64,1024]{1,0:T(8,128)(2,1)S(1)} %pad_maximum_fusion), channel_id=1, source_target_pairs={{0,1},{1,2},{2,3},{3,4},{4,5},{5,6},{6,7},{8,9},{9,10},{10,11},{11... | collective-permute-start | bytes 393224 | tf_op jit(solution)/shard_map/ppermute | solution.py:602
  39.2 1.9 collective-permute-start.1
  41.2 1.9 collective-permute-done.before_ref
  43.2 6.5 %collective-permute-done.1.after_ref = bf16[64,1024]{1,0:T(8,128)(2,1)S(1)} collective-permute-done((bf16[64,1024]{1,0:T(8,128)(2,1)S(1)}, bf16[64,1024]{1,0:T(8,128)(2,1)S(1)}, u32[]{:S(2)}, u32[]{:S(2)}) %collective-permute-start.1) | collective-permute-done | bytes 131104 | tf_op jit(solution)/shard_map/ppermute | solution.py:607
  49.7 22.7 %middle.1 = (bf16[8,256,128]{2,1,0:T(8,128)(2,1)}, bf16[288,1024]{1,0:T(8,128)(2,1)}, bf16[288,1024]{1,0:T(8,128)(2,1)}) custom-call(s32[1]{0:T(128)} %bitcast.3.parity_ref, bf16[8,192,128]{2,1,0:T(8,128)(2,1)S(1)} %all-to-all-done.1.mixed_ref, bf16[128,1024]{1,0:T(8,128)(2,1)S(1)} %bitcast.26, bf16[128,1024]{1,0:T(8,128)(2,1)S(1)} %bitcast.27, ...), custom_call_target="tpu_custom_call" | custom-call | tf_op jit(solution)/shard_map/middle/pallas_call | solution.py:356
  72.6 4.5 %all-to-all-start.2 = ((bf16[8,256,128]{2,1,0:T(8,128)(2,1)}), bf16[8,256,128]{2,1,0:T(8,128)(2,1)S(1)}, u32[]{:S(2)}, u32[]{:S(2)}) async-start(bf16[8,256,128]{2,1,0:T(8,128)(2,1)} %get-tuple-element.21), calls=%async_computation.2 | async-start | bytes 1048576 | tf_op jit(solution)/shard_map/all_to_all | solution.py:566
  78.2 2.8 %product.1 = (f32[512,1024]{1,0:T(8,128)}, bf16[512,1024]{1,0:T(8,128)(2,1)}) custom-call(s32[1]{0:T(128)} %bitcast.16.place_ref, bf16[288,1024]{1,0:T(8,128)(2,1)S(1)} %copy-done, bf16[288,1024]{1,0:T(8,128)(2,1)S(1)} %collective-permute-done.2.received_ref), custom_call_target="tpu_custom_call" | custom-call | tf_op jit(solution)/shard_map/product/pallas_call | solution.py:415
  81.0 3.0 %collective-permute-start.3 = (bf16[512,1024]{1,0:T(8,128)(2,1)}, bf16[512,1024]{1,0:T(8,128)(2,1)S(1)}, u32[]{:S(2)}, u32[]{:S(2)}) collective-permute-start(bf16[512,1024]{1,0:T(8,128)(2,1)} %get-tuple-element.26), channel_id=1, source_target_pairs={{0,4},{1,5},{2,6},{3,7},{4,0},{5,1},{6,2},{7,3},{8,12},{9,13},{10,... | collective-permute-start | bytes 3145736 | tf_op jit(solution)/shard_map/ppermute | solution.py:635
  83.9 3.5 %all-to-all-done.2.got_ref = bf16[8,256,128]{2,1,0:T(8,128)(2,1)S(1)} async-done(((bf16[8,256,128]{2,1,0:T(8,128)(2,1)}), bf16[8,256,128]{2,1,0:T(8,128)(2,1)S(1)}, u32[]{:S(2)}, u32[]{:S(2)}) %all-to-all-start.2) | async-done | bytes 524320 | tf_op jit(solution)/shard_map/all_to_all | solution.py:566
  87.4 8.6 %attend_back.1 = bf16[32,8,16,128]{3,2,1,0:T(8,128)(2,1)} custom-call(bf16[8,3,128,128]{3,2,1,0:T(8,128)(2,1)S(1)} %all-to-all-done.qkv_ref, bf16[8,256,128]{2,1,0:T(8,128)(2,1)S(1)} %all-to-all-done.2.got_ref, bf16[2,1024,1024]{2,1,0:T(8,128)(2,1)} %get-tuple-element.22.weights_ref), custom_call_target="tpu_custom_call" | custom-call | tf_op jit(solution)/shard_map/attend_back/pallas_call | solution.py:487
  96.0 12.1 %all-to-all-start.3 = ((bf16[256,16,128]{2,1,0:T(8,128)(2,1)}), bf16[256,16,128]{2,1,0:T(8,128)(2,1)S(1)}, u32[]{:S(2)}, u32[]{:S(2)}) async-start(bf16[256,16,128]{2,1,0:T(8,128)(2,1)} %bitcast.32), calls=%async_computation.3 | async-start | bytes 2097152 | tf_op jit(solution)/shard_map/all_to_all | solution.py:566
  109.0 1.8 collective-permute-start.7
  110.8 23.6 %collective-permute-done.7 = f32[32,1024]{1,0:T(8,128)S(1)} collective-permute-done((f32[32,1024]{1,0:T(8,128)S(1)}, f32[32,1024]{1,0:T(8,128)S(1)}, u32[]{:S(2)}, u32[]{:S(2)}) %collective-permute-start.7) | collective-permute-done | bytes 131104 | tf_op jit(solution)/shard_map/ppermute | solution.py:574
  135.3 4.1 %collective-permute-start.8 = (f32[32,1024]{1,0:T(8,128)S(1)}, f32[32,1024]{1,0:T(8,128)S(1)}, u32[]{:S(2)}, u32[]{:S(2)}) collective-permute-start(f32[32,1024]{1,0:T(8,128)S(1)} %fusion.2), channel_id=1, source_target_pairs={{0,112},{8,120},{16,32},{24,40},{32,16},{40,24},{48,64},{56,72},{6... | collective-permute-start | bytes 393224 | tf_op jit(solution)/shard_map/ppermute | solution.py:574
  139.4 3.2 %collective-permute-done.8 = f32[32,1024]{1,0:T(8,128)S(1)} collective-permute-done((f32[32,1024]{1,0:T(8,128)S(1)}, f32[32,1024]{1,0:T(8,128)S(1)}, u32[]{:S(2)}, u32[]{:S(2)}) %collective-permute-start.8) | collective-permute-done | bytes 131104 | tf_op jit(solution)/shard_map/ppermute | solution.py:574
  144.2 2.0 fusion.3
  148.3 2.2 %collective-permute-start.5 = (bf16[128,1024]{1,0:T(8,128)(2,1)S(1)}, bf16[128,1024]{1,0:T(8,128)(2,1)S(1)}, u32[]{:S(2)}, u32[]{:S(2)}) collective-permute-start(bf16[128,1024]{1,0:T(8,128)(2,1)S(1)} %get-tuple-element.38), channel_id=1, source_target_pairs={{0,2},{1,3},{2,0},{3,1},{4,6},{5,7},{6,4},{7,5},{8,10},{9,11},{10,... | collective-permute-start | bytes 786440 | tf_op jit(solution)/shard_map/ppermute | solution.py:645
  150.5 2.2 %collective-permute-start.10 = (f32[32,1024]{1,0:T(8,128)S(1)}, f32[32,1024]{1,0:T(8,128)S(1)}, u32[]{:S(2)}, u32[]{:S(2)}) collective-permute-start(f32[32,1024]{1,0:T(8,128)S(1)} %add.54), channel_id=1, source_target_pairs={{0,48},{8,56},{16,96},{24,104},{32,80},{40,88},{48,0},{56,8},{64,1... | collective-permute-start | bytes 393224 | tf_op jit(solution)/shard_map/ppermute | solution.py:574
  152.7 4.7 %collective-permute-done.10 = f32[32,1024]{1,0:T(8,128)S(1)} collective-permute-done((f32[32,1024]{1,0:T(8,128)S(1)}, f32[32,1024]{1,0:T(8,128)S(1)}, u32[]{:S(2)}, u32[]{:S(2)}) %collective-permute-start.10) | collective-permute-done | bytes 131104 | tf_op jit(solution)/shard_map/ppermute | solution.py:574
  157.4 3.2 %collective-permute-done.6 = bf16[128,1024]{1,0:T(8,128)(2,1)S(1)} collective-permute-done((bf16[128,1024]{1,0:T(8,128)(2,1)S(1)}, bf16[128,1024]{1,0:T(8,128)(2,1)S(1)}, u32[]{:S(2)}, u32[]{:S(2)}) %collective-permute-start.6) | collective-permute-done | bytes 262176 | tf_op jit(solution)/shard_map/ppermute | solution.py:645
  160.8 1.8 swap.1
  162.6 6.0 %all-to-all-start.4 = ((bf16[32,160,128]{2,1,0:T(8,128)(2,1)}), bf16[32,160,128]{2,1,0:T(8,128)(2,1)S(1)}, u32[]{:S(2)}, u32[]{:S(2)}) async-start(bf16[32,160,128]{2,1,0:T(8,128)(2,1)} %swap.1), calls=%async_computation.4 | async-start | bytes 2621440 | tf_op jit(solution)/shard_map/all_to_all | solution.py:566
  168.6 3.2 %collective-permute-start.11 = (f32[32,1024]{1,0:T(8,128)S(1)}, f32[32,1024]{1,0:T(8,128)S(1)}, u32[]{:S(2)}, u32[]{:S(2)}) collective-permute-start(f32[32,1024]{1,0:T(8,128)S(1)} %add.55), channel_id=1, source_target_pairs={{0,4},{1,5},{2,6},{3,7},{4,0},{5,1},{6,2},{7,3},{8,12},{9,13},{10,... | collective-permute-start | bytes 393224 | tf_op jit(solution)/shard_map/ppermute | solution.py:574
  171.7 7.8 %collective-permute-done.11 = f32[32,1024]{1,0:T(8,128)S(1)} collective-permute-done((f32[32,1024]{1,0:T(8,128)S(1)}, f32[32,1024]{1,0:T(8,128)S(1)}, u32[]{:S(2)}, u32[]{:S(2)}) %collective-permute-start.11) | collective-permute-done | bytes 131104 | tf_op jit(solution)/shard_map/ppermute | solution.py:574
  179.7 5.0 %collective-permute-done.12 = f32[32,1024]{1,0:T(8,128)S(1)} collective-permute-done((f32[32,1024]{1,0:T(8,128)S(1)}, f32[32,1024]{1,0:T(8,128)S(1)}, u32[]{:S(2)}, u32[]{:S(2)}) %collective-permute-start.12) | collective-permute-done | bytes 131104 | tf_op jit(solution)/shard_map/ppermute | solution.py:574
  185.6 5.7 %collective-permute-done.13 = f32[32,1024]{1,0:T(8,128)S(1)} collective-permute-done((f32[32,1024]{1,0:T(8,128)S(1)}, f32[32,1024]{1,0:T(8,128)S(1)}, u32[]{:S(2)}, u32[]{:S(2)}) %collective-permute-start.13) | collective-permute-done | bytes 131104 | tf_op jit(solution)/shard_map/ppermute | solution.py:574
  191.9 10.3 %all-to-all-done.4.got_ref = bf16[32,160,128]{2,1,0:T(8,128)(2,1)S(1)} async-done(((bf16[32,160,128]{2,1,0:T(8,128)(2,1)}), bf16[32,160,128]{2,1,0:T(8,128)(2,1)S(1)}, u32[]{:S(2)}, u32[]{:S(2)}) %all-to-all-start.4) | async-done | bytes 1310752 | tf_op jit(solution)/shard_map/all_to_all | solution.py:566
  (43 shorter events, 10.5 us)
Async XLA Ops:
  0.6 10.3 %copy-start.2 = (bf16[1,128,1024]{2,1,0:T(8,128)(2,1)S(1)}, bf16[1,128,1024]{2,1,0:T(8,128)(2,1)}, u32[]{:S(2)}) copy-start(bf16[1,128,1024]{2,1,0:T(8,128)(2,1)} %param.17) | copy-start | bytes 786436
  0.6 10.3 %copy-start.1 = (bf16[1,128,1024]{2,1,0:T(8,128)(2,1)S(1)}, bf16[1,128,1024]{2,1,0:T(8,128)(2,1)}, u32[]{:S(2)}) copy-start(bf16[1,128,1024]{2,1,0:T(8,128)(2,1)} %param.16) | copy-start | bytes 786436
  2.8 46.9 %copy-start.3 = (bf16[31,1024]{1,0:T(8,128)(2,1)S(1)}, bf16[31,1024]{1,0:T(8,128)(2,1)}, u32[]{:S(2)}) copy-start(bf16[31,1024]{1,0:T(8,128)(2,1)} %taps_ref.1) | copy-start | bytes 190468
  2.8 46.9 %copy-start.4 = (f32[1024]{0:T(1024)S(1)}, f32[1024]{0:T(1024)}, u32[]{:S(2)}) copy-start(f32[1024]{0:T(1024)} %param.22) | copy-start | bytes 12292
  2.8 46.9 %copy-start.5 = (f32[1024]{0:T(1024)S(1)}, f32[1024]{0:T(1024)}, u32[]{:S(2)}) copy-start(f32[1024]{0:T(1024)} %param.23) | copy-start | bytes 12292
  2.8 19.1 %all-to-all-start = ((bf16[8,3,128,128]{3,2,1,0:T(8,128)(2,1)}), bf16[8,3,128,128]{3,2,1,0:T(8,128)(2,1)S(1)}, u32[]{:S(2)}, u32[]{:S(2)}) async-start(bf16[8,3,128,128]{3,2,1,0:T(8,128)(2,1)} %pack.1), calls=%async_computation | async-start | bytes 1572864 | tf_op jit(solution)/shard_map/all_to_all | solution.py:566
  28.9 20.8 %all-to-all-start.1 = ((bf16[8,192,128]{2,1,0:T(8,128)(2,1)}), bf16[8,192,128]{2,1,0:T(8,128)(2,1)S(1)}, u32[]{:S(2)}, u32[]{:S(2)}) async-start(bf16[8,192,128]{2,1,0:T(8,128)(2,1)} %get-tuple-element.20), calls=%async_computation.1 | async-start | bytes 786432 | tf_op jit(solution)/shard_map/all_to_all | solution.py:566
  34.3 8.9 %collective-permute-start = (bf16[64,1024]{1,0:T(8,128)(2,1)S(1)}, bf16[64,1024]{1,0:T(8,128)(2,1)S(1)}, u32[]{:S(2)}, u32[]{:S(2)}) collective-permute-start(bf16[64,1024]{1,0:T(8,128)(2,1)S(1)} %pad_maximum_fusion), channel_id=1, source_target_pairs={{0,1},{1,2},{2,3},{3,4},{4,5},{5,6},{6,7},{8,9},{9,10},{10,11},{11... | collective-permute-start | bytes 393224 | tf_op jit(solution)/shard_map/ppermute | solution.py:602
  39.2 10.5 %collective-permute-start.1 = (bf16[64,1024]{1,0:T(8,128)(2,1)S(1)}, bf16[64,1024]{1,0:T(8,128)(2,1)S(1)}, u32[]{:S(2)}, u32[]{:S(2)}) collective-permute-start(bf16[64,1024]{1,0:T(8,128)(2,1)S(1)} %pad_maximum_fusion.1), channel_id=1, source_target_pairs={{1,0},{2,1},{3,2},{4,3},{5,4},{6,5},{7,6},{9,8},{10,9},{11,10},{12... | collective-permute-start | bytes 393224 | tf_op jit(solution)/shard_map/ppermute | solution.py:607
  72.5 4.6 %collective-permute-start.2 = (bf16[288,1024]{1,0:T(8,128)(2,1)}, bf16[288,1024]{1,0:T(8,128)(2,1)S(1)}, u32[]{:S(2)}, u32[]{:S(2)}) collective-permute-start(bf16[288,1024]{1,0:T(8,128)(2,1)} %get-tuple-element.24), channel_id=1, source_target_pairs={{0,8},{8,0},{16,24},{24,16},{32,40},{40,32},{48,56},{56,48},{64,72... | collective-permute-start | bytes 1769480 | tf_op jit(solution)/shard_map/ppermute | solution.py:631
  72.6 14.9 %all-to-all-start.2 = ((bf16[8,256,128]{2,1,0:T(8,128)(2,1)}), bf16[8,256,128]{2,1,0:T(8,128)(2,1)S(1)}, u32[]{:S(2)}, u32[]{:S(2)}) async-start(bf16[8,256,128]{2,1,0:T(8,128)(2,1)} %get-tuple-element.21), calls=%async_computation.2 | async-start | bytes 1048576 | tf_op jit(solution)/shard_map/all_to_all | solution.py:566
  77.1 1.1 copy-start
  81.0 63.3 %collective-permute-start.3 = (bf16[512,1024]{1,0:T(8,128)(2,1)}, bf16[512,1024]{1,0:T(8,128)(2,1)S(1)}, u32[]{:S(2)}, u32[]{:S(2)}) collective-permute-start(bf16[512,1024]{1,0:T(8,128)(2,1)} %get-tuple-element.26), channel_id=1, source_target_pairs={{0,4},{1,5},{2,6},{3,7},{4,0},{5,1},{6,2},{7,3},{8,12},{9,13},{10,... | collective-permute-start | bytes 3145736 | tf_op jit(solution)/shard_map/ppermute | solution.py:635
  96.0 64.8 %all-to-all-start.3 = ((bf16[256,16,128]{2,1,0:T(8,128)(2,1)}), bf16[256,16,128]{2,1,0:T(8,128)(2,1)S(1)}, u32[]{:S(2)}, u32[]{:S(2)}) async-start(bf16[256,16,128]{2,1,0:T(8,128)(2,1)} %bitcast.32), calls=%async_computation.3 | async-start | bytes 2097152 | tf_op jit(solution)/shard_map/all_to_all | solution.py:566
  109.0 25.5 %collective-permute-start.7 = (f32[32,1024]{1,0:T(8,128)S(1)}, f32[32,1024]{1,0:T(8,128)S(1)}, u32[]{:S(2)}, u32[]{:S(2)}) collective-permute-start(f32[32,1024]{1,0:T(8,128)S(1)} %convert_add_fusion.1), channel_id=1, source_target_pairs={{0,16},{8,24},{16,0},{24,8},{32,48},{40,56},{48,32},{56,40},{64,80... | collective-permute-start | bytes 393224 | tf_op jit(solution)/shard_map/ppermute | solution.py:574
  135.3 7.3 %collective-permute-start.8 = (f32[32,1024]{1,0:T(8,128)S(1)}, f32[32,1024]{1,0:T(8,128)S(1)}, u32[]{:S(2)}, u32[]{:S(2)}) collective-permute-start(f32[32,1024]{1,0:T(8,128)S(1)} %fusion.2), channel_id=1, source_target_pairs={{0,112},{8,120},{16,32},{24,40},{32,16},{40,24},{48,64},{56,72},{6... | collective-permute-start | bytes 393224 | tf_op jit(solution)/shard_map/ppermute | solution.py:574
  142.7 7.8 %collective-permute-start.9 = (f32[32,1024]{1,0:T(8,128)S(1)}, f32[32,1024]{1,0:T(8,128)S(1)}, u32[]{:S(2)}, u32[]{:S(2)}) collective-permute-start(f32[32,1024]{1,0:T(8,128)S(1)} %add.53), channel_id=1, source_target_pairs={{0,128},{8,136},{16,144},{24,152},{32,160},{40,168},{48,176},{56,1... | collective-permute-start | bytes 393224 | tf_op jit(solution)/shard_map/ppermute | solution.py:574
  146.2 14.6 %copy-start.6 = (s32[32]{0:T(128)S(1)}, s32[32]{0:T(128)}, u32[]{:S(2)}) copy-start(s32[32]{0:T(128)} %plan_ref.1) | copy-start | bytes 388
  146.3 11.1 %collective-permute-start.4 = (bf16[128,1024]{1,0:T(8,128)(2,1)S(1)}, bf16[128,1024]{1,0:T(8,128)(2,1)S(1)}, u32[]{:S(2)}, u32[]{:S(2)}) collective-permute-start(bf16[128,1024]{1,0:T(8,128)(2,1)S(1)} %get-tuple-element.36), channel_id=1, source_target_pairs={{0,1},{1,0},{2,3},{3,2},{4,5},{5,4},{6,7},{7,6},{8,9},{9,8},{10,11... | collective-permute-start | bytes 786440 | tf_op jit(solution)/shard_map/ppermute | solution.py:645
  147.2 13.4 %collective-permute-start.6 = (bf16[128,1024]{1,0:T(8,128)(2,1)S(1)}, bf16[128,1024]{1,0:T(8,128)(2,1)S(1)}, u32[]{:S(2)}, u32[]{:S(2)}) collective-permute-start(bf16[128,1024]{1,0:T(8,128)(2,1)S(1)} %get-tuple-element.37), channel_id=1, source_target_pairs={{0,3},{1,2},{2,1},{3,0},{4,7},{5,6},{6,5},{7,4},{8,11},{9,10},{10,... | collective-permute-start | bytes 786440 | tf_op jit(solution)/shard_map/ppermute | solution.py:645
  148.3 12.3 %collective-permute-start.5 = (bf16[128,1024]{1,0:T(8,128)(2,1)S(1)}, bf16[128,1024]{1,0:T(8,128)(2,1)S(1)}, u32[]{:S(2)}, u32[]{:S(2)}) collective-permute-start(bf16[128,1024]{1,0:T(8,128)(2,1)S(1)} %get-tuple-element.38), channel_id=1, source_target_pairs={{0,2},{1,3},{2,0},{3,1},{4,6},{5,7},{6,4},{7,5},{8,10},{9,11},{10,... | collective-permute-start | bytes 786440 | tf_op jit(solution)/shard_map/ppermute | solution.py:645
  150.5 6.9 %collective-permute-start.10 = (f32[32,1024]{1,0:T(8,128)S(1)}, f32[32,1024]{1,0:T(8,128)S(1)}, u32[]{:S(2)}, u32[]{:S(2)}) collective-permute-start(f32[32,1024]{1,0:T(8,128)S(1)} %add.54), channel_id=1, source_target_pairs={{0,48},{8,56},{16,96},{24,104},{32,80},{40,88},{48,0},{56,8},{64,1... | collective-permute-start | bytes 393224 | tf_op jit(solution)/shard_map/ppermute | solution.py:574
  162.6 39.6 %all-to-all-start.4 = ((bf16[32,160,128]{2,1,0:T(8,128)(2,1)}), bf16[32,160,128]{2,1,0:T(8,128)(2,1)S(1)}, u32[]{:S(2)}, u32[]{:S(2)}) async-start(bf16[32,160,128]{2,1,0:T(8,128)(2,1)} %swap.1), calls=%async_computation.4 | async-start | bytes 2621440 | tf_op jit(solution)/shard_map/all_to_all | solution.py:566
  168.6 10.9 %collective-permute-start.11 = (f32[32,1024]{1,0:T(8,128)S(1)}, f32[32,1024]{1,0:T(8,128)S(1)}, u32[]{:S(2)}, u32[]{:S(2)}) collective-permute-start(f32[32,1024]{1,0:T(8,128)S(1)} %add.55), channel_id=1, source_target_pairs={{0,4},{1,5},{2,6},{3,7},{4,0},{5,1},{6,2},{7,3},{8,12},{9,13},{10,... | collective-permute-start | bytes 393224 | tf_op jit(solution)/shard_map/ppermute | solution.py:574
  179.5 5.1 %collective-permute-start.12 = (f32[32,1024]{1,0:T(8,128)S(1)}, f32[32,1024]{1,0:T(8,128)S(1)}, u32[]{:S(2)}, u32[]{:S(2)}) collective-permute-start(f32[32,1024]{1,0:T(8,128)S(1)} %add.56), channel_id=1, source_target_pairs={{0,1},{1,0},{2,3},{3,2},{4,5},{5,4},{6,7},{7,6},{8,9},{9,8},{10,11... | collective-permute-start | bytes 393224 | tf_op jit(solution)/shard_map/ppermute | solution.py:574
  184.7 6.6 %collective-permute-start.13 = (f32[32,1024]{1,0:T(8,128)S(1)}, f32[32,1024]{1,0:T(8,128)S(1)}, u32[]{:S(2)}, u32[]{:S(2)}) collective-permute-start(f32[32,1024]{1,0:T(8,128)S(1)} %add.57), channel_id=1, source_target_pairs={{0,2},{1,3},{2,0},{3,1},{4,6},{5,7},{6,4},{7,5},{8,10},{9,11},{10,... | collective-permute-start | bytes 393224 | tf_op jit(solution)/shard_map/ppermute | solution.py:574

commit v4 on v3

--- a/solution.py
+++ b/solution.py
@@ -147,6 +147,42 @@
     return (tap + 1) % 8, (tap + 1) // 8 - 2
 
 
+def prepare_kernel(
+    cotangent_ref,
+    before_ref,
+    after_ref,
+    ids_ref,
+    point_out_ref,
+    taps_ref,
+    act_grad_ref,
+    ids_moved_ref,
+    taps_f32_ref,
+):
+    taps_f32_ref[...] = taps_ref[...].astype(F32)
+    ids = jnp.broadcast_to(ids_ref[...], (128, 256)).T
+    for m in range(8):
+        ids_moved_ref[m] = ids[m : m + WINDOW]
+    cotangent = jnp.concatenate(
+        [before_ref[HALO : 2 * HALO], cotangent_ref[...], after_ref[HALO : 2 * HALO]], 0
+    )
+    act_grad_ref[...] = across(cotangent, point_out_ref[...], NT)
+
+
+def prepare(*arrays):
+    return pl.pallas_call(
+        prepare_kernel,
+        out_shape=(
+            jax.ShapeDtypeStruct((WINDOW, 1024), F32),
+            jax.ShapeDtypeStruct((8, WINDOW, 128), F32),
+            in_hbm((TAPS, 1024), F32),
+        ),
+        in_specs=[whole()] * 6,
+        out_specs=(whole(),) * 3,
+        compiler_params=pltpu.CompilerParams(vmem_limit_bytes=12 << 20),
+        name="prepare",
+    )(*arrays)
+
+
 def middle_kernel(
     parity_ref,
     mixed_ref,
@@ -154,11 +190,11 @@
     cotangent_ref,
     before_ref,
     after_ref,
-    ids_ref,
+    act_grad_ref,
+    ids_moved_ref,
     attn_out_hbm,
     point_in_hbm,
-    taps_ref,
-    point_out_hbm,
+    taps_f32_ref,
     norm_gain_ref,
     conv_gain_ref,
     out_ref,
@@ -166,18 +202,14 @@
     send_ref,
     attn_out_ref,
     point_in_ref,
-    point_out_ref,
     arrivals,
     conv_in_ref,
     moved_ref,
     grad_ref,
     grad_moved_ref,
-    ids_moved_ref,
-    taps_f32_ref,
     hat_ref,
     linear_ref,
     logistic_ref,
-    act_grad_ref,
     activated_ref,
     in_grad_ref,
     tap_sums_ref,
@@ -185,16 +217,10 @@
     own = slice(HALO, HALO + ROWS)
     attn_out_copy = pltpu.make_async_copy(attn_out_hbm, attn_out_ref, arrivals.at[0])
     point_in_copy = pltpu.make_async_copy(point_in_hbm, point_in_ref, arrivals.at[1])
-    point_out_copy = pltpu.make_async_copy(point_out_hbm, point_out_ref, arrivals.at[2])
     attn_out_copy.start()
     point_in_copy.start()
-    point_out_copy.start()
-    ids = jnp.broadcast_to(ids_ref[...], (128, 256)).T
     grad_ref[...] = jnp.zeros_like(grad_ref)
-    taps_f32_ref[...] = taps_ref[...].astype(F32)
     conv_in_ref[0:8, 0:128] = jnp.zeros((8, 128), F32)
-    for m in range(8):
-        ids_moved_ref[m] = ids[m : m + WINDOW]
 
     mixed = jnp.concatenate([mixed_ref[h] for h in range(8)], 1)
     attn_out_copy.wait()
@@ -217,12 +243,6 @@
         linear_ref[:, cols] = linear[own]
         logistic_ref[:, cols] = logistic[own]
 
-    cotangent = jnp.concatenate(
-        [before_ref[HALO : 2 * HALO], cotangent_ref[...], after_ref[HALO : 2 * HALO]], 0
-    )
-    point_out_copy.wait()
-    act_grad_ref[...] = across(cotangent, point_out_ref[...], NT)
-
     @pl.loop(0, 8)
     def _(block):
         cols = pl.ds(pl.multiple_of(128 * block, 128), 128)
@@ -302,7 +322,7 @@
             16,
             row_group,
             tuple(jnp.zeros((8, 128), F32) for _ in range(8 * len(here))),
-            unroll=4,
+            unroll=2,
         )
         for at, tap in enumerate(here):
             tap_sums_ref[tap : tap + 1, :] = jnp.concatenate(
@@ -361,24 +381,20 @@
             in_hbm((288, 1024), BF16),
         ),
         in_specs=[whole(pltpu.SMEM)]
-        + [whole()] * 6
-        + [whole(pl.ANY), whole(pl.ANY), whole(), whole(pl.ANY), whole(), whole()],
+        + [whole()] * 7
+        + [whole(pl.ANY), whole(pl.ANY), whole(), whole(), whole()],
         out_specs=(whole(), whole(), whole()),
         scratch_shapes=[
             pltpu.VMEM((1024, 1024), BF16),
             pltpu.VMEM((1024, 2048), BF16),
-            pltpu.VMEM((1024, 1024), BF16),
-            pltpu.SemaphoreType.DMA((3,)),
+            pltpu.SemaphoreType.DMA((2,)),
             pltpu.VMEM((WINDOW, 1024), F32),
             pltpu.VMEM((8, WINDOW, 1024), F32),
             pltpu.VMEM((WINDOW, 1024), F32),
             pltpu.VMEM((8, WINDOW, 1024), F32),
-            pltpu.VMEM((8, WINDOW, 128), F32),
-            pltpu.VMEM((TAPS, 1024), F32),
             pltpu.VMEM((ROWS, 1024), F32),
             pltpu.VMEM((ROWS, 1024), F32),
             pltpu.VMEM((ROWS, 1024), F32),
-            pltpu.VMEM((WINDOW, 1024), F32),
             pltpu.VMEM((WINDOW, 1024), F32),
             pltpu.VMEM((ROWS, 1024), F32),
             pltpu.VMEM((32, 1024), F32),
@@ -570,9 +586,10 @@
     return (device & 17) | (partners[(device >> 1) & 7] << 1)
 
 
-def add_from(taps, axis, partner):
-    arrived = lax.ppermute(taps, axis, partner)
-    return taps + arrived
+def add_from(taps, axis, partner, narrow=False):
+    sent = taps.astype(BF16) if narrow else taps
+    arrived = lax.ppermute(sent, axis, partner)
+    return sent.astype(F32) + arrived.astype(F32)
 
 
 def per_device(
@@ -612,6 +629,9 @@
     qkv = spread(pack(queries, keys, values), "seq")
     mixed_heads, weights = attend(qkv, ids[None])
     mixed = spread(mixed_heads, "seq")
+    act_grad, ids_moved, taps_wide = prepare(
+        cotangent, before, after, ids_window[None], from_hbm(point_out), from_hbm(kernel)
+    )
     outgoing, keep, send = middle(
         lax.rem(slot, 2)[None].astype(jnp.int32),
         mixed,
@@ -619,11 +639,11 @@
         cotangent,
         before,
         after,
-        ids_window[None],
+        act_grad,
+        ids_moved,
         from_hbm(attn_out),
         from_hbm(point_in),
-        kernel,
-        from_hbm(point_out),
+        from_hbm(taps_wide),
         norm_gain[None],
         conv_gain[None],
     )
@@ -647,7 +667,7 @@
     tail = quarters[0]
     for part in arrived:
         tail = tail + part.astype(F32)
-    taps = add_from(taps, "dp", [(i, along_z(i, (3, 6, 5, 0, 7, 2, 1, 4))) for i in range(32)])
+    taps = add_from(taps, "dp", [(i, along_z(i, (3, 6, 5, 0, 7, 2, 1, 4))) for i in range(32)], True)
 
     second, taps = lax.optimization_barrier((swap(plan, first, tail), taps))
     for bit in (4, 1, 2):

time: 206 us -> 217 us (1.053)
  blocking collectives: 0 us -> 14.3 us
  starting transfers between devices: 63.2 us -> 58.2 us
  Pallas kernels: 46.3 us -> 49.6 us
    all_to_all x0 -> x1, blocking collectives: none -> 14.3 us  [spread(): return lax.all_to_all(array, axis, split_axis=0, concat_axis=0, tiled=True)]
    ppermute x3, waiting for transfers between devices: 3.22 us -> 11 us  [per_device(): lax.ppermute(quarters[k], 'seq', [(i, i ^ k) for i in range(8)])]
    all_to_all x5 -> x4, starting transfers between devices: 35.2 us -> 30 us  [spread(): return lax.all_to_all(array, axis, split_axis=0, concat_axis=0, tiled=True)]
    ppermute x7, waiting for transfers between devices: 49.9 us -> 45.7 us  [add_from(): arrived = lax.ppermute(sent, axis, partner)]
    pallas_call x0 -> x1, Pallas kernels: none -> 3.01 us  [prepare(): pl.pallas_call(prepare_kernel, out_shape=(jax.ShapeDtypeStruct((WINDOW, 1...]
    all_to_all x5 -> x4, waiting for transfers between devices: 24.8 us -> 22.6 us  [spread(): return lax.all_to_all(array, axis, split_axis=0, concat_axis=0, tiled=True)]
  transfers between devices with their start and end apart: 19 -> 18, of which waited for: 12 -> 12; matrix products, arithmetic and copies ran while one was open for 3% -> 2% of each run, Pallas kernels for 6% -> 7%
where the time goes in v4:
time: 217 us; the launch traced here: 215 us
  waiting for transfers between devices  87.8 us (40%)
  starting transfers between devices  58.2 us (27%)
  Pallas kernels  49.6 us (23%)
  blocking collectives  14.3 us (7%)
  other arithmetic  3.76 us (2%)
    ppermute x7, waiting for transfers between devices, add_from(): arrived = lax.ppermute(sent, axis, partner)  45.7 us
    all_to_all x4, starting transfers between devices, spread(): return lax.all_to_all(array, axis, split_axis=0, concat_axis=0, tiled=True)  30 us
    pallas_call x1, Pallas kernels, middle(): pl.pallas_call(middle_kernel, out_shape=(in_hbm((8, 256, 128), BF16), in_...  23.1 us
    all_to_all x4, waiting for transfers between devices, spread(): return lax.all_to_all(array, axis, split_axis=0, concat_axis=0, tiled=True)  22.6 us
    all_to_all x1, blocking collectives, spread(): return lax.all_to_all(array, axis, split_axis=0, concat_axis=0, tiled=True)  14.3 us
    ppermute x7, starting transfers between devices, add_from(): arrived = lax.ppermute(sent, axis, partner)  14.1 us
    ppermute x3, waiting for transfers between devices, per_device(): lax.ppermute(quarters[k], 'seq', [(i, i ^ k) for i in range(8)])  11 us
    pallas_call x1, Pallas kernels, attend_back(): pl.pallas_call(attend_back_kernel, grid=(4,), out_shape=in_hbm((32, 8, 16...  8.56 us
  transfers between devices with their start and end apart: 18, of which 12 were waited for; matrix products, arithmetic and copies ran while one was open for 2% of the time, Pallas kernels for 7%

profile of v4, /device:TPU:24, one launch (start us, length us, event | category | flops | bytes accessed | tf_op | source)
XLA Modules:
  0.0 214.6 jit_solution(8622949293394539627)
XLA Ops:
  0.7 2.2 %pack.1 = bf16[8,3,128,128]{3,2,1,0:T(8,128)(2,1)} custom-call(bf16[128,1024]{1,0:T(8,128)(2,1)} %bitcast.34, bf16[128,1024]{1,0:T(8,128)(2,1)} %bitcast.35, bf16[128,1024]{1,0:T(8,128)(2,1)} %bitcast.36), custom_call_target="tpu_custom_call" | custom-call | tf_op jit(solution)/shard_map/pack/pallas_call | solution.py:56
  2.9 7.1 %all-to-all-start = ((bf16[8,3,128,128]{3,2,1,0:T(8,128)(2,1)}), bf16[8,3,128,128]{3,2,1,0:T(8,128)(2,1)S(1)}, u32[]{:S(2)}, u32[]{:S(2)}) async-start(bf16[8,3,128,128]{3,2,1,0:T(8,128)(2,1)} %pack.1), calls=%async_computation | async-start | bytes 1572864 | tf_op jit(solution)/shard_map/all_to_all | solution.py:582
  10.8 11.0 %all-to-all-done.qkv_ref = bf16[8,3,128,128]{3,2,1,0:T(8,128)(2,1)S(1)} async-done(((bf16[8,3,128,128]{3,2,1,0:T(8,128)(2,1)}), bf16[8,3,128,128]{3,2,1,0:T(8,128)(2,1)S(1)}, u32[]{:S(2)}, u32[]{:S(2)}) %all-to-all-start) | async-done | bytes 786464 | tf_op jit(solution)/shard_map/all_to_all | solution.py:582
  21.8 7.0 %attend.1 = (bf16[8,192,128]{2,1,0:T(8,128)(2,1)}, bf16[2,1024,1024]{2,1,0:T(8,128)(2,1)}) custom-call(bf16[8,3,128,128]{3,2,1,0:T(8,128)(2,1)S(1)} %all-to-all-done.qkv_ref, f32[1,1024]{1,0:T(1,128)S(1)} %dynamic-slice_convert_fusion.ids_ref), custom_call_target="tpu_custom_call" | custom-call | tf_op jit(solution)/shard_map/attend/pallas_call | solution.py:118
  28.8 5.5 %all-to-all-start.1 = ((bf16[8,192,128]{2,1,0:T(8,128)(2,1)}), bf16[8,192,128]{2,1,0:T(8,128)(2,1)S(1)}, u32[]{:S(2)}, u32[]{:S(2)}) async-start(bf16[8,192,128]{2,1,0:T(8,128)(2,1)} %get-tuple-element.23), calls=%async_computation.1 | async-start | bytes 786432 | tf_op jit(solution)/shard_map/all_to_all | solution.py:582
  34.3 4.9 %collective-permute-start = (bf16[64,1024]{1,0:T(8,128)(2,1)S(1)}, bf16[64,1024]{1,0:T(8,128)(2,1)S(1)}, u32[]{:S(2)}, u32[]{:S(2)}) collective-permute-start(bf16[64,1024]{1,0:T(8,128)(2,1)S(1)} %pad_maximum_fusion), channel_id=1, source_target_pairs={{0,1},{1,2},{2,3},{3,4},{4,5},{5,6},{6,7},{8,9},{9,10},{10,11},{11... | collective-permute-start | bytes 393224 | tf_op jit(solution)/shard_map/ppermute | solution.py:619
  39.2 1.9 collective-permute-start.1
  41.2 1.9 collective-permute-done.before_ref
  43.2 6.5 %collective-permute-done.1.after_ref = bf16[64,1024]{1,0:T(8,128)(2,1)S(1)} collective-permute-done((bf16[64,1024]{1,0:T(8,128)(2,1)S(1)}, bf16[64,1024]{1,0:T(8,128)(2,1)S(1)}, u32[]{:S(2)}, u32[]{:S(2)}) %collective-permute-start.1) | collective-permute-done | bytes 131104 | tf_op jit(solution)/shard_map/ppermute | solution.py:624
  49.7 3.0 %prepare.1 = (f32[192,1024]{1,0:T(8,128)S(1)}, f32[8,192,128]{2,1,0:T(8,128)S(1)}, f32[31,1024]{1,0:T(8,128)}) custom-call(bf16[128,1024]{1,0:T(8,128)(2,1)S(1)} %bitcast.26, bf16[64,1024]{1,0:T(8,128)(2,1)S(1)} %collective-permute-done.before_ref, bf16[64,1024]{1,0:T(8,128)(2,1)S(1)} %collective-permute-done.1.after_ref, f32[1,256]{1,0:T(1,128)S(1)} %bitcast.30, ...), custom_call_target="tpu_custom_call" | custom-call | tf_op jit(solution)/shard_map/prepare/pallas_call | solution.py:172
  52.7 23.1 %middle.1 = (bf16[8,256,128]{2,1,0:T(8,128)(2,1)}, bf16[288,1024]{1,0:T(8,128)(2,1)}, bf16[288,1024]{1,0:T(8,128)(2,1)}) custom-call(s32[1]{0:T(128)} %bitcast.3.parity_ref, bf16[8,192,128]{2,1,0:T(8,128)(2,1)S(1)} %all-to-all-done.1.mixed_ref, bf16[128,1024]{1,0:T(8,128)(2,1)S(1)} %bitcast.28, bf16[128,1024]{1,0:T(8,128)(2,1)S(1)} %bitcast.27, ...), custom_call_target="tpu_custom_call" | custom-call | tf_op jit(solution)/shard_map/middle/pallas_call | solution.py:376
  75.9 14.3 %all_to_all.25.got_ref = bf16[8,256,128]{2,1,0:T(8,128)(2,1)S(1)} all-to-all(bf16[8,256,128]{2,1,0:T(8,128)(2,1)} %get-tuple-element.27), channel_id=1, replica_groups=mesh['dp'=32,'seq'=8] {'seq'}, dimensions={0} | all-to-all | bytes 1048576 | tf_op jit(solution)/shard_map/all_to_all | solution.py:582
  90.2 8.6 %attend_back.1 = bf16[32,8,16,128]{3,2,1,0:T(8,128)(2,1)} custom-call(bf16[8,3,128,128]{3,2,1,0:T(8,128)(2,1)S(1)} %all-to-all-done.qkv_ref, bf16[8,256,128]{2,1,0:T(8,128)(2,1)S(1)} %all_to_all.25.got_ref, bf16[2,1024,1024]{2,1,0:T(8,128)(2,1)} %get-tuple-element.28.weights_ref), custom_call_target="tpu_custom_call" | custom-call | tf_op jit(solution)/shard_map/attend_back/pallas_call | solution.py:503
  98.7 12.5 %all-to-all-start.3 = ((bf16[256,16,128]{2,1,0:T(8,128)(2,1)}), bf16[256,16,128]{2,1,0:T(8,128)(2,1)S(1)}, u32[]{:S(2)}, u32[]{:S(2)}) async-start(bf16[256,16,128]{2,1,0:T(8,128)(2,1)} %bitcast.33), calls=%async_computation.3 | async-start | bytes 2097152 | tf_op jit(solution)/shard_map/all_to_all | solution.py:582
  111.3 2.8 %product.1 = (f32[512,1024]{1,0:T(8,128)}, bf16[512,1024]{1,0:T(8,128)(2,1)}) custom-call(s32[1]{0:T(128)} %bitcast.16.place_ref, bf16[288,1024]{1,0:T(8,128)(2,1)S(1)} %copy-done.1, bf16[288,1024]{1,0:T(8,128)(2,1)S(1)} %collective-permute-done.2.received_ref), custom_call_target="tpu_custom_call" | custom-call | tf_op jit(solution)/shard_map/product/pallas_call | solution.py:431
  114.1 3.0 %collective-permute-start.3 = (bf16[512,1024]{1,0:T(8,128)(2,1)}, bf16[512,1024]{1,0:T(8,128)(2,1)S(1)}, u32[]{:S(2)}, u32[]{:S(2)}) collective-permute-start(bf16[512,1024]{1,0:T(8,128)(2,1)} %get-tuple-element.32), channel_id=1, source_target_pairs={{0,4},{1,5},{2,6},{3,7},{4,0},{5,1},{6,2},{7,3},{8,12},{9,13},{10,... | collective-permute-start | bytes 3145736 | tf_op jit(solution)/shard_map/ppermute | solution.py:655
  117.1 1.8 collective-permute-start.7
  118.9 18.7 %collective-permute-done.7 = f32[32,1024]{1,0:T(8,128)S(1)} collective-permute-done((f32[32,1024]{1,0:T(8,128)S(1)}, f32[32,1024]{1,0:T(8,128)S(1)}, u32[]{:S(2)}, u32[]{:S(2)}) %collective-permute-start.7) | collective-permute-done | bytes 131104 | tf_op jit(solution)/shard_map/ppermute | solution.py:591
  137.6 4.1 %collective-permute-start.8 = (f32[32,1024]{1,0:T(8,128)S(1)}, f32[32,1024]{1,0:T(8,128)S(1)}, u32[]{:S(2)}, u32[]{:S(2)}) collective-permute-start(f32[32,1024]{1,0:T(8,128)S(1)} %fusion.2), channel_id=1, source_target_pairs={{0,112},{8,120},{16,32},{24,40},{32,16},{40,24},{48,64},{56,72},{6... | collective-permute-start | bytes 393224 | tf_op jit(solution)/shard_map/ppermute | solution.py:591
  141.7 3.2 %collective-permute-done.8 = f32[32,1024]{1,0:T(8,128)S(1)} collective-permute-done((f32[32,1024]{1,0:T(8,128)S(1)}, f32[32,1024]{1,0:T(8,128)S(1)}, u32[]{:S(2)}, u32[]{:S(2)}) %collective-permute-start.8) | collective-permute-done | bytes 131104 | tf_op jit(solution)/shard_map/ppermute | solution.py:591
  146.5 5.7 %collective-permute-done.9 = f32[32,1024]{1,0:T(8,128)S(1)} collective-permute-done((f32[32,1024]{1,0:T(8,128)S(1)}, f32[32,1024]{1,0:T(8,128)S(1)}, u32[]{:S(2)}, u32[]{:S(2)}) %collective-permute-start.9) | collective-permute-done | bytes 131104 | tf_op jit(solution)/shard_map/ppermute | solution.py:591
  152.1 3.6 %collective-permute-start.10 = (bf16[32,1024]{1,0:T(8,128)(2,1)S(1)}, bf16[32,1024]{1,0:T(8,128)(2,1)S(1)}, u32[]{:S(2)}, u32[]{:S(2)}) collective-permute-start(bf16[32,1024]{1,0:T(8,128)(2,1)S(1)} %add_convert_fusion), channel_id=1, source_target_pairs={{0,48},{8,56},{16,96},{24,104},{32,80},{40,88},{48,0},{56,8},{64,1... | collective-permute-start | bytes 196616 | tf_op jit(solution)/shard_map/ppermute | solution.py:591
  155.7 2.0 fusion.3
  160.0 2.0 collective-permute-start.5
  162.0 5.1 %collective-permute-done.4 = bf16[128,1024]{1,0:T(8,128)(2,1)S(1)} collective-permute-done((bf16[128,1024]{1,0:T(8,128)(2,1)S(1)}, bf16[128,1024]{1,0:T(8,128)(2,1)S(1)}, u32[]{:S(2)}, u32[]{:S(2)}) %collective-permute-start.4) | collective-permute-done | bytes 262176 | tf_op jit(solution)/shard_map/ppermute | solution.py:665
  167.1 5.9 %collective-permute-done.6 = bf16[128,1024]{1,0:T(8,128)(2,1)S(1)} collective-permute-done((bf16[128,1024]{1,0:T(8,128)(2,1)S(1)}, bf16[128,1024]{1,0:T(8,128)(2,1)S(1)}, u32[]{:S(2)}, u32[]{:S(2)}) %collective-permute-start.6) | collective-permute-done | bytes 262176 | tf_op jit(solution)/shard_map/ppermute | solution.py:665
  175.0 4.8 %all-to-all-start.4 = ((bf16[32,160,128]{2,1,0:T(8,128)(2,1)}), bf16[32,160,128]{2,1,0:T(8,128)(2,1)S(1)}, u32[]{:S(2)}, u32[]{:S(2)}) async-start(bf16[32,160,128]{2,1,0:T(8,128)(2,1)} %swap.1), calls=%async_computation.4 | async-start | bytes 2621440 | tf_op jit(solution)/shard_map/all_to_all | solution.py:582
  179.8 1.8 collective-permute-start.11
  181.7 7.8 %collective-permute-done.11 = f32[32,1024]{1,0:T(8,128)S(1)} collective-permute-done((f32[32,1024]{1,0:T(8,128)S(1)}, f32[32,1024]{1,0:T(8,128)S(1)}, u32[]{:S(2)}, u32[]{:S(2)}) %collective-permute-start.11) | collective-permute-done | bytes 131104 | tf_op jit(solution)/shard_map/ppermute | solution.py:591
  189.7 4.9 %collective-permute-done.12 = f32[32,1024]{1,0:T(8,128)S(1)} collective-permute-done((f32[32,1024]{1,0:T(8,128)S(1)}, f32[32,1024]{1,0:T(8,128)S(1)}, u32[]{:S(2)}, u32[]{:S(2)}) %collective-permute-start.12) | collective-permute-done | bytes 131104 | tf_op jit(solution)/shard_map/ppermute | solution.py:591
  195.6 5.6 %collective-permute-done.13 = f32[32,1024]{1,0:T(8,128)S(1)} collective-permute-done((f32[32,1024]{1,0:T(8,128)S(1)}, f32[32,1024]{1,0:T(8,128)S(1)}, u32[]{:S(2)}, u32[]{:S(2)}) %collective-permute-start.13) | collective-permute-done | bytes 131104 | tf_op jit(solution)/shard_map/ppermute | solution.py:591
  201.8 11.7 %all-to-all-done.4.got_ref = bf16[32,160,128]{2,1,0:T(8,128)(2,1)S(1)} async-done(((bf16[32,160,128]{2,1,0:T(8,128)(2,1)}), bf16[32,160,128]{2,1,0:T(8,128)(2,1)S(1)}, u32[]{:S(2)}, u32[]{:S(2)}) %all-to-all-start.4) | async-done | bytes 1310752 | tf_op jit(solution)/shard_map/all_to_all | solution.py:582
  (41 shorter events, 9.9 us)
Async XLA Ops:
  0.6 10.1 %copy-start = (bf16[1,128,1024]{2,1,0:T(8,128)(2,1)S(1)}, bf16[1,128,1024]{2,1,0:T(8,128)(2,1)}, u32[]{:S(2)}) copy-start(bf16[1,128,1024]{2,1,0:T(8,128)(2,1)} %param.17) | copy-start | bytes 786436
  0.6 10.1 %copy-start.2 = (bf16[1,128,1024]{2,1,0:T(8,128)(2,1)S(1)}, bf16[1,128,1024]{2,1,0:T(8,128)(2,1)}, u32[]{:S(2)}) copy-start(bf16[1,128,1024]{2,1,0:T(8,128)(2,1)} %param.16) | copy-start | bytes 786436
  2.9 18.9 %all-to-all-start = ((bf16[8,3,128,128]{3,2,1,0:T(8,128)(2,1)}), bf16[8,3,128,128]{3,2,1,0:T(8,128)(2,1)S(1)}, u32[]{:S(2)}, u32[]{:S(2)}) async-start(bf16[8,3,128,128]{3,2,1,0:T(8,128)(2,1)} %pack.1), calls=%async_computation | async-start | bytes 1572864 | tf_op jit(solution)/shard_map/all_to_all | solution.py:582
  28.8 23.9 %copy-start.3 = (f32[1024]{0:T(1024)S(1)}, f32[1024]{0:T(1024)}, u32[]{:S(2)}) copy-start(f32[1024]{0:T(1024)} %param.22) | copy-start | bytes 12292
  28.8 23.9 %copy-start.4 = (f32[1024]{0:T(1024)S(1)}, f32[1024]{0:T(1024)}, u32[]{:S(2)}) copy-start(f32[1024]{0:T(1024)} %param.23) | copy-start | bytes 12292
  28.8 23.9 %all-to-all-start.1 = ((bf16[8,192,128]{2,1,0:T(8,128)(2,1)}), bf16[8,192,128]{2,1,0:T(8,128)(2,1)S(1)}, u32[]{:S(2)}, u32[]{:S(2)}) async-start(bf16[8,192,128]{2,1,0:T(8,128)(2,1)} %get-tuple-element.23), calls=%async_computation.1 | async-start | bytes 786432 | tf_op jit(solution)/shard_map/all_to_all | solution.py:582
  34.3 8.9 %collective-permute-start = (bf16[64,1024]{1,0:T(8,128)(2,1)S(1)}, bf16[64,1024]{1,0:T(8,128)(2,1)S(1)}, u32[]{:S(2)}, u32[]{:S(2)}) collective-permute-start(bf16[64,1024]{1,0:T(8,128)(2,1)S(1)} %pad_maximum_fusion), channel_id=1, source_target_pairs={{0,1},{1,2},{2,3},{3,4},{4,5},{5,6},{6,7},{8,9},{9,10},{10,11},{11... | collective-permute-start | bytes 393224 | tf_op jit(solution)/shard_map/ppermute | solution.py:619
  39.2 10.5 %collective-permute-start.1 = (bf16[64,1024]{1,0:T(8,128)(2,1)S(1)}, bf16[64,1024]{1,0:T(8,128)(2,1)S(1)}, u32[]{:S(2)}, u32[]{:S(2)}) collective-permute-start(bf16[64,1024]{1,0:T(8,128)(2,1)S(1)} %pad_maximum_fusion.1), channel_id=1, source_target_pairs={{1,0},{2,1},{3,2},{4,3},{5,4},{6,5},{7,6},{9,8},{10,9},{11,10},{12... | collective-permute-start | bytes 393224 | tf_op jit(solution)/shard_map/ppermute | solution.py:624
  75.8 35.5 %collective-permute-start.2 = (bf16[288,1024]{1,0:T(8,128)(2,1)}, bf16[288,1024]{1,0:T(8,128)(2,1)S(1)}, u32[]{:S(2)}, u32[]{:S(2)}) collective-permute-start(bf16[288,1024]{1,0:T(8,128)(2,1)} %get-tuple-element.30), channel_id=1, source_target_pairs={{0,8},{8,0},{16,24},{24,16},{32,40},{40,32},{48,56},{56,48},{64,72... | collective-permute-start | bytes 1769480 | tf_op jit(solution)/shard_map/ppermute | solution.py:651
  98.7 12.5 %copy-start.1 = (bf16[288,1024]{1,0:T(8,128)(2,1)S(1)}, bf16[288,1024]{1,0:T(8,128)(2,1)}, u32[]{:S(2)}) copy-start(bf16[288,1024]{1,0:T(8,128)(2,1)} %get-tuple-element.29.keep_ref) | copy-start | bytes 1769476
  98.7 74.4 %all-to-all-start.3 = ((bf16[256,16,128]{2,1,0:T(8,128)(2,1)}), bf16[256,16,128]{2,1,0:T(8,128)(2,1)S(1)}, u32[]{:S(2)}, u32[]{:S(2)}) async-start(bf16[256,16,128]{2,1,0:T(8,128)(2,1)} %bitcast.33), calls=%async_computation.3 | async-start | bytes 2097152 | tf_op jit(solution)/shard_map/all_to_all | solution.py:582
  114.1 41.6 %collective-permute-start.3 = (bf16[512,1024]{1,0:T(8,128)(2,1)}, bf16[512,1024]{1,0:T(8,128)(2,1)S(1)}, u32[]{:S(2)}, u32[]{:S(2)}) collective-permute-start(bf16[512,1024]{1,0:T(8,128)(2,1)} %get-tuple-element.32), channel_id=1, source_target_pairs={{0,4},{1,5},{2,6},{3,7},{4,0},{5,1},{6,2},{7,3},{8,12},{9,13},{10,... | collective-permute-start | bytes 3145736 | tf_op jit(solution)/shard_map/ppermute | solution.py:655
  117.1 20.5 %collective-permute-start.7 = (f32[32,1024]{1,0:T(8,128)S(1)}, f32[32,1024]{1,0:T(8,128)S(1)}, u32[]{:S(2)}, u32[]{:S(2)}) collective-permute-start(f32[32,1024]{1,0:T(8,128)S(1)} %convert_add_fusion.2), channel_id=1, source_target_pairs={{0,16},{8,24},{16,0},{24,8},{32,48},{40,56},{48,32},{56,40},{64,80... | collective-permute-start | bytes 393224 | tf_op jit(solution)/shard_map/ppermute | solution.py:591
  137.6 7.3 %collective-permute-start.8 = (f32[32,1024]{1,0:T(8,128)S(1)}, f32[32,1024]{1,0:T(8,128)S(1)}, u32[]{:S(2)}, u32[]{:S(2)}) collective-permute-start(f32[32,1024]{1,0:T(8,128)S(1)} %fusion.2), channel_id=1, source_target_pairs={{0,112},{8,120},{16,32},{24,40},{32,16},{40,24},{48,64},{56,72},{6... | collective-permute-start | bytes 393224 | tf_op jit(solution)/shard_map/ppermute | solution.py:591
  144.9 7.2 %collective-permute-start.9 = (f32[32,1024]{1,0:T(8,128)S(1)}, f32[32,1024]{1,0:T(8,128)S(1)}, u32[]{:S(2)}, u32[]{:S(2)}) collective-permute-start(f32[32,1024]{1,0:T(8,128)S(1)} %add.53), channel_id=1, source_target_pairs={{0,128},{8,136},{16,144},{24,152},{32,160},{40,168},{48,176},{56,1... | collective-permute-start | bytes 393224 | tf_op jit(solution)/shard_map/ppermute | solution.py:591
  152.1 9.9 %collective-permute-start.10 = (bf16[32,1024]{1,0:T(8,128)(2,1)S(1)}, bf16[32,1024]{1,0:T(8,128)(2,1)S(1)}, u32[]{:S(2)}, u32[]{:S(2)}) collective-permute-start(bf16[32,1024]{1,0:T(8,128)(2,1)S(1)} %add_convert_fusion), channel_id=1, source_target_pairs={{0,48},{8,56},{16,96},{24,104},{32,80},{40,88},{48,0},{56,8},{64,1... | collective-permute-start | bytes 196616 | tf_op jit(solution)/shard_map/ppermute | solution.py:591
  157.8 15.4 %copy-start.5 = (s32[32]{0:T(128)S(1)}, s32[32]{0:T(128)}, u32[]{:S(2)}) copy-start(s32[32]{0:T(128)} %plan_ref.1) | copy-start | bytes 388
  157.8 9.3 %collective-permute-start.4 = (bf16[128,1024]{1,0:T(8,128)(2,1)S(1)}, bf16[128,1024]{1,0:T(8,128)(2,1)S(1)}, u32[]{:S(2)}, u32[]{:S(2)}) collective-permute-start(bf16[128,1024]{1,0:T(8,128)(2,1)S(1)} %get-tuple-element.42), channel_id=1, source_target_pairs={{0,1},{1,0},{2,3},{3,2},{4,5},{5,4},{6,7},{7,6},{8,9},{9,8},{10,11... | collective-permute-start | bytes 786440 | tf_op jit(solution)/shard_map/ppermute | solution.py:665
  158.8 14.2 %collective-permute-start.6 = (bf16[128,1024]{1,0:T(8,128)(2,1)S(1)}, bf16[128,1024]{1,0:T(8,128)(2,1)S(1)}, u32[]{:S(2)}, u32[]{:S(2)}) collective-permute-start(bf16[128,1024]{1,0:T(8,128)(2,1)S(1)} %get-tuple-element.43), channel_id=1, source_target_pairs={{0,3},{1,2},{2,1},{3,0},{4,7},{5,6},{6,5},{7,4},{8,11},{9,10},{10,... | collective-permute-start | bytes 786440 | tf_op jit(solution)/shard_map/ppermute | solution.py:665
  160.0 13.1 %collective-permute-start.5 = (bf16[128,1024]{1,0:T(8,128)(2,1)S(1)}, bf16[128,1024]{1,0:T(8,128)(2,1)S(1)}, u32[]{:S(2)}, u32[]{:S(2)}) collective-permute-start(bf16[128,1024]{1,0:T(8,128)(2,1)S(1)} %get-tuple-element.44), channel_id=1, source_target_pairs={{0,2},{1,3},{2,0},{3,1},{4,6},{5,7},{6,4},{7,5},{8,10},{9,11},{10,... | collective-permute-start | bytes 786440 | tf_op jit(solution)/shard_map/ppermute | solution.py:665
  175.0 38.5 %all-to-all-start.4 = ((bf16[32,160,128]{2,1,0:T(8,128)(2,1)}), bf16[32,160,128]{2,1,0:T(8,128)(2,1)S(1)}, u32[]{:S(2)}, u32[]{:S(2)}) async-start(bf16[32,160,128]{2,1,0:T(8,128)(2,1)} %swap.1), calls=%async_computation.4 | async-start | bytes 2621440 | tf_op jit(solution)/shard_map/all_to_all | solution.py:582
  179.8 9.6 %collective-permute-start.11 = (f32[32,1024]{1,0:T(8,128)S(1)}, f32[32,1024]{1,0:T(8,128)S(1)}, u32[]{:S(2)}, u32[]{:S(2)}) collective-permute-start(f32[32,1024]{1,0:T(8,128)S(1)} %convert_add_fusion.1), channel_id=1, source_target_pairs={{0,4},{1,5},{2,6},{3,7},{4,0},{5,1},{6,2},{7,3},{8,12},{9,13},{10,... | collective-permute-start | bytes 393224 | tf_op jit(solution)/shard_map/ppermute | solution.py:591
  189.4 5.1 %collective-permute-start.12 = (f32[32,1024]{1,0:T(8,128)S(1)}, f32[32,1024]{1,0:T(8,128)S(1)}, u32[]{:S(2)}, u32[]{:S(2)}) collective-permute-start(f32[32,1024]{1,0:T(8,128)S(1)} %add.56), channel_id=1, source_target_pairs={{0,1},{1,0},{2,3},{3,2},{4,5},{5,4},{6,7},{7,6},{8,9},{9,8},{10,11... | collective-permute-start | bytes 393224 | tf_op jit(solution)/shard_map/ppermute | solution.py:591
  194.6 6.6 %collective-permute-start.13 = (f32[32,1024]{1,0:T(8,128)S(1)}, f32[32,1024]{1,0:T(8,128)S(1)}, u32[]{:S(2)}, u32[]{:S(2)}) collective-permute-start(f32[32,1024]{1,0:T(8,128)S(1)} %add.57), channel_id=1, source_target_pairs={{0,2},{1,3},{2,0},{3,1},{4,6},{5,7},{6,4},{7,5},{8,10},{9,11},{10,... | collective-permute-start | bytes 393224 | tf_op jit(solution)/shard_map/ppermute | solution.py:591
